TPU v7x, 128 devices: a whole 4x4x4 slice. The times are simulated.
128 devices in a mesh: seq: 16 (over x, z), nbr: 4 (over y), batch: 2 (over core).
Axes of the slice: x: 4, y: 4, z: 4, core: 2. Of those that a mesh axis runs over, the one named last changes fastest.
Arguments:
- hidden: bfloat16 [4096, 4096], P(('batch', 'seq'), 'nbr'), parts along dimension 0, may hold values from -6 to 6
- d_out: bfloat16 [4096, 4096], P(('batch', 'seq'), 'nbr'), parts along dimension 0, may hold values from -6 to 6
- nbr_emb: bfloat16 [768, 128, 896], P(('batch', 'seq', 'nbr')), parts along dimension 0, may hold values from -6 to 6
- slot_span: int32 [768], P(('batch', 'seq')), parts along dimension 0, may hold values from -1 to 1, as said below
- dec_gain: bfloat16 [4096], P('nbr'), may hold values from 0.5 to 1.5
- enc_gain: bfloat16 [896], replicated, may hold values from 0.5 to 1.5
- w_cond: bfloat16 [4096, 896], P('nbr'), may hold values from -0.75 to 0.75
- w_enc: bfloat16 [896, 896], replicated, may hold values from -0.1875 to 0.1875
- w_q: bfloat16 [4096, 2048], P('seq', 'nbr'), may hold values from -0.09375 to 0.09375
- w_k: bfloat16 [896, 2048], P('seq', 'nbr'), may hold values from -8 to 8
- w_v: bfloat16 [896, 2048], P('seq', 'nbr'), may hold values from -0.1875 to 0.1875
- w_o: bfloat16 [2048, 4096], P('nbr', 'seq'), may hold values from -0.125 to 0.125
Outputs:
- out: bfloat16 [4096, 4096], P(('batch', 'seq'), 'nbr'), parts along dimension 0
- d_hidden: bfloat16 [4096, 4096], P(('batch', 'seq'), 'nbr'), parts along dimension 0
- d_enc: bfloat16 [768, 128, 896], P(('batch', 'seq', 'nbr')), parts along dimension 0
- d_wo: float32 [4096, 4096], P(('batch', 'nbr'), 'seq'), parts along dimension 0
- d_wk: float32 [1792, 2048], P(('batch', 'seq'), 'nbr'), parts along dimension 0
- d_wv: float32 [1792, 2048], P(('batch', 'seq'), 'nbr'), parts along dimension 0
There are 2 independent parts, one for each index of `batch`. A program takes and returns all parts, laid end to end along the dimension named above; an argument that names none is the same for every part. Nothing has to cross between parts.
Inputs may be any that keep to these rules, and one draw needn't show every extreme that they name: `slot_span`: A slot on seq index s serves a span of seq index s, counted from 0 within its 2 spans; -1 marks an empty slot. Every span is served by 1 to 8 slots, and one span of each seq index by exactly 8. Within each seq index one nbr index has all 6 slots live.
All inputs are finite; a program needn't handle non-finite values.
Results may differ from a plain program's by a relative error of at most 0.018.
The roundings to bfloat16 on the way count: a program that leaves them out, or rounds other values in their place, can miss the bound.
Values may be sent and summed in bfloat16 or wider, within the bound.
No kernel may reach another device: no remote copies, remote signals or barrier semaphores. Data moves between devices by JAX's collectives and lax.ppermute only.
A program may use at most 128 MiB of HBM per device.

v0:
```python
import jax
import jax.numpy as jnp
from jax import lax
from jax.experimental import pallas as pl
from jax.experimental.pallas import tpu as pltpu
from jax.sharding import PartitionSpec as P

HD = 128
CLEN = 64
NLEN = 128
KMAX = 8
F32 = jnp.float32
BF16 = jnp.bfloat16
VMEM = pl.BlockSpec(memory_space=pltpu.VMEM)
SMEM = pl.BlockSpec(memory_space=pltpu.SMEM)


def dot(a, b, dims=((1,), (0,))):
    return lax.dot_general(a, b, (dims, ((), ())), preferred_element_type=F32)


NT = ((1,), (1,))
TN = ((0,), (0,))


def shift(x, by):
    n = lax.axis_size("nbr")
    return lax.ppermute(x, "nbr", [(i, (i + by) % n) for i in range(n)])


def ring_gather(x):
    half = x.shape[0] // 2
    right = shift(x, -1)
    left = shift(x, 1)
    far_a = shift(right[:half], -1)
    far_b = shift(left[half:], 1)
    return right, far_a, far_b, left


def scattered(parts):
    return [parts[0]] + [shift(parts[r], r) for r in (2, 1, 3)]


def total(shares):
    return sum(x.astype(F32) for x in shares)


def sum_small(x):
    return x + shift(x, 1) + shift(x, 2) + shift(x, 3)


def exchange(parts):
    return lax.all_to_all(parts, "seq", split_axis=0, concat_axis=0, tiled=True)


def rms_scale(values):
    return lax.rsqrt(jnp.mean(values * values, axis=-1, keepdims=True) + 1e-06)


def cost(products, moved):
    return pl.CostEstimate(flops=2 * products, transcendentals=0, bytes_accessed=moved)


def project_kernel(n_ref, x_ref, w, o_ref, acc):
    step = pl.program_id(0)
    x = x_ref[0]
    part = jnp.zeros(acc.shape, F32)
    for s in range(4):
        block = w[2 * s : 2 * s + 2].reshape(256, 512)
        part += dot(x[:, 256 * s : 256 * s + 256], block)

    @pl.when(step == 0)
    def _():
        acc[...] = part

    @pl.when((step > 0) & (step < 3))
    def _():
        acc[...] += part

    @pl.when(step == 3)
    def _():
        o_ref[...] = (acc[...] + part).astype(BF16)


def project(n, x, weights, row):
    tokens = x.shape[1]
    return pl.pallas_call(
        project_kernel,
        grid_spec=pltpu.PrefetchScalarGridSpec(
            num_scalar_prefetch=1,
            grid=(4,),
            in_specs=[
                pl.BlockSpec((1, tokens, 1024), lambda r, n: (r, 0, 0)),
                pl.BlockSpec((8, 128, 512), lambda r, n: ((n[0] + r) % 4, row, 0)),
            ],
            out_specs=pl.BlockSpec((tokens, 512), lambda r, n: (0, 0)),
            scratch_shapes=[pltpu.VMEM((tokens, 512), F32)],
        ),
        out_shape=jax.ShapeDtypeStruct((tokens, 512), BF16),
        cost_estimate=cost(tokens * 4096 * 512, 6 << 20),
        compiler_params=pltpu.CompilerParams(vmem_limit_bytes=24 << 20),
        name="project",
    )(n, x, weights)


def forward_kernel(tab, e0, e1, e2, e3, wk, wv, q, enc, ctx, probs, kb, vb):
    tables = ((e0, 0), (e1, 6), (e2, 12), (e3, 18))

    def pick(j, carry):
        src = tab[j]

        @pl.when(src < 0)
        def _():
            enc[j] = jnp.zeros(enc.shape[1:], BF16)

        for ref, first in tables:

            @pl.when((src >= first) & (src < first + ref.shape[0]))
            def _(ref=ref, first=first):
                enc[j] = ref[src - first]

        return carry

    lax.fori_loop(0, 2 * KMAX, pick, 0)

    def kv(c, carry):
        x = enc[pl.ds(4 * c, 4)].reshape(4 * NLEN, enc.shape[2])
        rows = pl.ds(pl.multiple_of(c * 512, 512), 512)
        kb[rows, :] = dot(x, wk[...]).astype(BF16)
        vb[rows, :] = dot(x, wv[...]).astype(BF16)
        return carry

    lax.fori_loop(0, 4, kv, 0)
    factor = HD ** (-0.5)
    heads = q.shape[1] // HD
    keys = KMAX * NLEN
    for c in range(2):
        limit = tab[2 * KMAX + c] * NLEN
        allowed = lax.broadcasted_iota(jnp.int32, (CLEN, keys), 1) < limit
        toks = slice(c * CLEN, (c + 1) * CLEN)
        rows = slice(c * keys, (c + 1) * keys)
        for h in range(heads):
            cols = slice(h * HD, (h + 1) * HD)
            s = jnp.where(allowed, dot(q[toks, cols], kb[rows, cols], NT) * factor, -1e30)
            w = jnp.exp(s - jnp.max(s, axis=-1, keepdims=True))
            p = w / jnp.sum(w, axis=-1, keepdims=True)
            probs[c * heads + h] = p
            ctx[toks, cols] = dot(p.astype(BF16), vb[rows, cols]).astype(BF16)


def forward(tab, blocks, wk, wv, q):
    rows = 2 * KMAX * NLEN
    flat = jax.ShapeDtypeStruct((rows, q.shape[1]), BF16)
    probs = jax.ShapeDtypeStruct((2 * q.shape[1] // HD, CLEN, KMAX * NLEN), F32)
    return pl.pallas_call(
        forward_kernel,
        in_specs=[SMEM] + [VMEM] * 7,
        out_specs=[VMEM] * 5,
        out_shape=[
            pltpu.HBM((2 * KMAX, NLEN, wk.shape[0]), BF16),
            jax.ShapeDtypeStruct(q.shape, BF16),
            probs,
            flat,
            flat,
        ],
        cost_estimate=cost(2048 * 896 * 1024, 36 << 20),
        compiler_params=pltpu.CompilerParams(vmem_limit_bytes=32 << 20),
        name="forward",
    )(tab, *blocks, wk, wv, q)


def backward_kernel(inv, probs, kb, vb, q, dc, wk, wv, dq, dk, dv, out, de):
    factor = HD ** (-0.5)
    heads = q.shape[1] // HD
    keys = KMAX * NLEN
    for c in range(2):
        toks = slice(c * CLEN, (c + 1) * CLEN)
        rows = slice(c * keys, (c + 1) * keys)
        for h in range(heads):
            cols = slice(h * HD, (h + 1) * HD)
            dh = dc[toks, cols]
            p = probs[c * heads + h]
            dp = dot(dh, vb[rows, cols], NT)
            rd = jnp.sum(p * dp, axis=-1, keepdims=True)
            ds = (p * (dp - rd) * factor).astype(BF16)
            dq[toks, cols] = dot(ds, kb[rows, cols]).astype(BF16)
            dk[rows, cols] = dot(ds, q[toks, cols], TN).astype(BF16)
            dv[rows, cols] = dot(p.astype(BF16), dh, TN).astype(BF16)

    def grad(c, carry):
        rows = pl.ds(pl.multiple_of(c * 512, 512), 512)
        part = dot(dk[rows, :], wk[...], NT) + dot(dv[rows, :], wv[...], NT)
        de[pl.ds(4 * c, 4)] = part.astype(BF16).reshape(4, NLEN, wk.shape[0])
        return carry

    lax.fori_loop(0, 4, grad, 0)

    def place(i, carry):
        src = inv[i]

        @pl.when(src < 0)
        def _():
            out[i] = jnp.zeros(out.shape[1:], BF16)

        @pl.when(src >= 0)
        def _():
            out[i] = de[src]

        return carry

    lax.fori_loop(0, out.shape[0], place, 0)


def backward(inv, probs, kb, vb, q, dc, wk, wv):
    width = wk.shape[0]
    return pl.pallas_call(
        backward_kernel,
        in_specs=[SMEM] + [VMEM] * 7,
        out_specs=[VMEM] * 4,
        out_shape=[
            jax.ShapeDtypeStruct(q.shape, BF16),
            pltpu.HBM(kb.shape, BF16),
            pltpu.HBM(kb.shape, BF16),
            pltpu.HBM((inv.shape[0], NLEN, width), BF16),
        ],
        scratch_shapes=[pltpu.VMEM((2 * KMAX, NLEN, width), BF16)],
        cost_estimate=cost(2048 * 896 * 1024, 40 << 20),
        compiler_params=pltpu.CompilerParams(vmem_limit_bytes=34 << 20),
        name="backward",
    )(inv, probs, kb, vb, q, dc, wk, wv)


def unproject_kernel(n_ref, ctx, dq, more, w, o):
    tokens = ctx.shape[0]
    for s in range(4):
        cols = slice(256 * s, 256 * s + 256)
        wq = w[2 * s : 2 * s + 2, :128].reshape(256, 512)
        wo = w[2 * s : 2 * s + 2, 128:].reshape(256, 512)
        o[0, :tokens, cols] = dot(ctx[...], wo, NT).astype(BF16)
        o[0, tokens : 2 * tokens, cols] = dot(dq[...], wq, NT).astype(BF16)
    o[0, 2 * tokens :, :] = more[...]


def unproject(n, ctx, dq, more, weights):
    tokens = ctx.shape[0]
    rows = 2 * tokens + more.shape[0]
    return pl.pallas_call(
        unproject_kernel,
        grid_spec=pltpu.PrefetchScalarGridSpec(
            num_scalar_prefetch=1,
            grid=(4,),
            in_specs=[
                pl.BlockSpec((tokens, 512), lambda r, n: (0, 0)),
                pl.BlockSpec((tokens, 512), lambda r, n: (0, 0)),
                pl.BlockSpec(more.shape, lambda r, n: (0, 0)),
                pl.BlockSpec((8, 256, 512), lambda r, n: ((n[0] + r) % 4, 0, 0)),
            ],
            out_specs=pl.BlockSpec((1, rows, 1024), lambda r, n: (r, 0, 0)),
        ),
        out_shape=jax.ShapeDtypeStruct((4, rows, 1024), BF16),
        cost_estimate=cost(2 * tokens * 4096 * 512, 12 << 20),
        compiler_params=pltpu.CompilerParams(vmem_limit_bytes=24 << 20),
        name="unproject",
    )(n, ctx, dq, more, weights)


def outer_kernel(at, d, ctx, a0, a1, a2, a3, b0, b1, b2, b3):
    n, x, z = at[0], at[1], at[2]
    upper, lower = (a0, a1, a2, a3), (b0, b1, b2, b3)
    half = a0.shape[1]
    for i in range(4):
        block = lax.rem(x + i + 4 - n, 4)
        for j in range(4):
            first = pl.multiple_of(lax.rem(z + j, 4) * 2 * half, 2 * half)
            part = dot(d[block, :, pl.ds(first, 2 * half)], ctx[...], TN).astype(BF16)
            upper[i][j] = part[:half]
            lower[j][i] = part[half:]


def outer(at, dout, ctx):
    share = jax.ShapeDtypeStruct((4, 128, ctx.shape[1]), BF16)
    return pl.pallas_call(
        outer_kernel,
        in_specs=[SMEM, VMEM, VMEM],
        out_specs=[VMEM] * 8,
        out_shape=[share] * 8,
        cost_estimate=cost(ctx.shape[0] * 4096 * 512, 6 << 20),
        compiler_params=pltpu.CompilerParams(vmem_limit_bytes=24 << 20),
        name="outer",
    )(at, dout, ctx)


def along_x(share, by):
    return lax.ppermute(share, "seq", [(i, (i // 4 + by) % 4 * 4 + i % 4) for i in range(16)])


def along_z(share, by):
    return lax.ppermute(share, "seq", [(i, i // 4 * 4 + (i + by) % 4) for i in range(16)])


def slot_tables(slot_span, n):
    slots = slot_span.shape[0]
    ids = jnp.arange(slots, dtype=jnp.int32)
    before = ids[None, :] < ids[:, None]
    same = slot_span[None, :] == slot_span[:, None]
    rank = jnp.sum(same & before, axis=1, dtype=jnp.int32)
    where = jnp.where(slot_span >= 0, slot_span * KMAX + rank, -1).astype(jnp.int32)
    spot = jnp.arange(2 * KMAX, dtype=jnp.int32)
    hit = where[None, :] == spot[:, None]
    relative = (ids + slots - 6 * n) % slots
    source = jnp.sum(jnp.where(hit, relative[None, :] + 1, 0), axis=1, dtype=jnp.int32) - 1
    counts = jnp.sum(slot_span[None, :] == jnp.arange(2)[:, None], axis=1, dtype=jnp.int32)
    return jnp.concatenate([source, counts]), where


def body(hidden, d_out, nbr_emb, slot_span, dec_gain, enc_gain, w_cond, w_enc, w_q, w_k, w_v, w_o):
    n = lax.axis_index("nbr")
    b = lax.axis_index("batch")
    n1 = n.astype(jnp.int32).reshape(1)
    tokens, feats = hidden.shape
    spans = tokens // CLEN

    q_half = lax.dynamic_slice_in_dim(w_q, b * 128, 128, axis=0)
    o_half = lax.dynamic_slice_in_dim(w_o, b * 128, 128, axis=1).T
    kv_half = jnp.where(b == 0, w_k, w_v)
    weights = lax.all_gather(
        jnp.concatenate([q_half, o_half, kv_half], axis=0), ("seq", "batch"), axis=0
    )

    gain_rows = jnp.broadcast_to(dec_gain[None], (8, feats))
    half = tokens // 2
    state = jnp.concatenate([hidden[:half], gain_rows, hidden[half:], gain_rows], axis=0)
    h1, h2a, h2b, h3 = ring_gather(state)

    pooled = jnp.mean(hidden.astype(F32).reshape(spans, CLEN, feats), axis=1).astype(BF16)
    length = lax.axis_size("seq")
    carried = lax.ppermute(
        pooled[spans - 1 :], "seq", [(i, i + 1) for i in range(length - 1)]
    )
    previous = jnp.concatenate([carried, pooled[: spans - 1]], axis=0)
    condition = sum_small(jnp.dot(previous, w_cond, preferred_element_type=F32))

    nbr_emb = lax.optimization_barrier((nbr_emb, condition))[0]
    e1, e2a, e2b, e3 = ring_gather(nbr_emb)
    later = lax.optimization_barrier((d_out, e2a, e2b, weights))
    weights = later[3]
    d2, d1, d3 = (shift(later[0], r) for r in (2, -1, 1))

    tab, inv = slot_tables(slot_span, n)
    rel_span = jnp.roll(slot_span.reshape(4, 6), -n, axis=0).reshape(-1)

    def encode(block, first):
        own = lax.slice_in_dim(rel_span, first, first + block.shape[0])
        own = own[:, None, None]
        cond = jnp.where(own == 0, condition[0], jnp.where(own == 1, condition[1], 0.0))
        x = block.astype(F32) + cond
        enc_normed = (x * rms_scale(x) * enc_gain.astype(F32)).astype(BF16)
        width = x.shape[2]
        mixed = jnp.dot(
            enc_normed.reshape(-1, width), w_enc, preferred_element_type=F32
        ).reshape(x.shape)
        return (x + jax.nn.silu(mixed)).astype(BF16)


    def states(rows):
        return jnp.concatenate([rows[:half], rows[half + 8 : tokens + 8]], axis=0)

    hid_rel = jnp.stack(
        [hidden, states(h1), jnp.concatenate([h2a[:half], h2b[:half]], axis=0), states(h3)]
    )
    gain_rel = jnp.stack([dec_gain, h1[half], h2a[half], h3[half]])
    hf = hid_rel.astype(F32)
    rstd = lax.rsqrt(jnp.mean(hf * hf, axis=(0, 2)) + 1e-06)[:, None]
    normed = (hf * rstd[None] * gain_rel.astype(F32)[:, None, :]).astype(BF16)
    dout_rel = jnp.stack([d_out, d1, d2, d3])

    pairs = weights.reshape(16, 2, 312, 512)
    weights = pltpu.with_memory_space_constraint(weights, pltpu.HBM)
    wk = pairs[:, 0, 256:].reshape(-1, 512)
    wv = pairs[:, 1, 256:].reshape(-1, 512)

    query = project(n1, normed, weights, 0)
    e2, query, wk, wv = lax.optimization_barrier(
        (jnp.concatenate([e2a, e2b], axis=0), query, wk, wv)
    )
    encoded = [encode(nbr_emb, 0), encode(e1, 6), encode(e2, 12), encode(e3, 18)]
    enc, ctx, probs, keys, values = forward(tab, encoded, wk, wv, query)
    d_ctx = project(n1, dout_rel, weights, 1)
    d_query, d_key, d_value, parts = backward(
        inv, probs, keys, values, query, d_ctx, wk, wv
    )
    d_enc = lax.psum_scatter(parts, "nbr", scatter_dimension=0, tiled=True)
    ctx = lax.optimization_barrier((ctx, d_query))[0]

    place = lax.axis_index("seq").astype(jnp.int32)
    at = jnp.stack([n.astype(jnp.int32), place // 4, place % 4])
    d_wo_parts = outer(at, dout_rel, ctx)
    upper = [along_x(d_wo_parts[i], i) for i in (2, 1, 3)]
    lower = [along_z(d_wo_parts[4 + i], i) for i in (2, 1, 3)]
    upper = total([d_wo_parts[0]] + upper).astype(BF16)
    lower = total([d_wo_parts[4]] + lower).astype(BF16)
    upper = total([upper[0]] + [along_z(upper[i], i) for i in (2, 1, 3)])
    lower = total([lower[0]] + [along_x(lower[i], i) for i in (2, 1, 3)])
    d_wo = jnp.concatenate([upper, lower], axis=0).T

    inner = jnp.sum(d_query.astype(F32) * query.astype(F32), axis=-1).astype(BF16)
    more = jnp.broadcast_to(jnp.pad(inner, (0, feats - tokens))[None], (16, feats))
    sums = total(scattered(unproject(n1, ctx, d_query, more, weights)))
    out_sum, own_grad = sums[:tokens], sums[tokens : 2 * tokens]
    stat = sums[2 * tokens, :tokens][:, None] / (rstd * (4 * feats))

    rows = enc.reshape(-1, enc.shape[2])
    d_wk_part = dot(rows, d_key, TN).astype(BF16).reshape(16, -1, 512)
    d_wv_part = dot(rows, d_value, TN).astype(BF16).reshape(16, -1, 512)
    d_wkv_parts = jnp.concatenate([d_wk_part, d_wv_part], axis=1)
    d_wkv = jnp.sum(exchange(d_wkv_parts).astype(F32), axis=0)
    d_wk, d_wv = d_wkv[:56], d_wkv[56:]

    own = hidden.astype(F32)
    out = (own + out_sum).astype(BF16)
    scaled = dec_gain.astype(F32) * own_grad
    d_hidden = d_out.astype(F32) + rstd * scaled - own * rstd**3 * stat
    return (out, d_hidden.astype(BF16), d_enc, d_wo, d_wk, d_wv)


def solution(mesh):
    placed = (
        P(("batch", "seq"), "nbr"),
        P(("batch", "seq"), "nbr"),
        P(("batch", "seq", "nbr"), None, None),
        P(("batch", "seq")),
        P("nbr"),
        P(),
        P("nbr", None),
        P(),
        P("seq", "nbr"),
        P("seq", "nbr"),
        P("seq", "nbr"),
        P("nbr", "seq"),
    )
    return jax.shard_map(
        body,
        mesh=mesh,
        in_specs=placed,
        out_specs=(
            P(("batch", "seq"), "nbr"),
            P(("batch", "seq"), "nbr"),
            P(("batch", "seq", "nbr"), None, None),
            P(("batch", "nbr"), "seq"),
            P(("batch", "seq"), "nbr"),
            P(("batch", "seq"), "nbr"),
        ),
        check_vma=False,
    )
```

profile of v0, /device:TPU:0, one launch (start us, length us, event | category | flops | bytes accessed | tf_op | source)
XLA Modules:
  0.0 228.4 jit_solution(4427491528475311563)
XLA Ops:
  7.3 1.7 constant_dynamic-slice_fusion
  9.0 1.7 copy.27
  12.4 1.6 pad_maximum_fusion.4
  16.6 3.1 %collective-permute-start.8 = (bf16[144,1024]{1,0:T(8,128)(2,1)}, bf16[144,1024]{1,0:T(8,128)(2,1)}, u32[]{:S(2)}, u32[]{:S(2)}) collective-permute-start(bf16[144,1024]{1,0:T(8,128)(2,1)} %pad_maximum_fusion.5), channel_id=1, source_target_pairs={{0,6},{2,0},{4,2},{6,4},{1,7},{3,1},{5,3},{7,5},{8,14},{10,8},{12,... | collective-permute-start | bytes 884744 | tf_op jit(solution)/shard_map/ppermute | solution.py:28
  19.8 3.8 %collective-permute-start = (bf16[1,1024]{1,0:T(2,128)(2,1)S(1)}, bf16[1,1024]{1,0:T(2,128)(2,1)S(1)}, u32[]{:S(2)}, u32[]{:S(2)}) collective-permute-start(bf16[1,1024]{1,0:T(2,128)(2,1)S(1)} %get-tuple-element.101), channel_id=1, source_target_pairs={{0,8},{8,16},{16,24},{24,32},{32,40},{40,48},{48,56},{56,64},{64,7... | collective-permute-start | bytes 6152 | tf_op jit(solution)/shard_map/ppermute | solution.py:337
  25.9 4.1 %collective-permute-start.2 = (f32[2,896]{1,0:T(2,128)S(1)}, f32[2,896]{1,0:T(2,128)S(1)}, u32[]{:S(2)}, u32[]{:S(2)}) collective-permute-start(f32[2,896]{1,0:T(2,128)S(1)} %fusion.43), channel_id=1, source_target_pairs={{0,4},{2,6},{4,0},{6,2},{1,5},{3,7},{5,1},{7,3},{8,12},{10,14},{12... | collective-permute-start | bytes 21512 | tf_op jit(solution)/shard_map/ppermute | solution.py:28
  30.2 1.4 collective-permute-done.2
  31.7 2.0 collective-permute-done.3
  33.7 1.3 collective-permute-start.4
  36.4 3.1 %add_convert_fusion.3.e0 = bf16[6,128,896]{2,1,0:T(8,128)(2,1)} fusion(bf16[6,128,896]{2,1,0:T(8,128)(2,1)S(1)} %copy-done.9, bf16[896,896]{1,0:T(8,128)(2,1)S(1)} %copy-done.15, f32[896]{0:T(1024)S(1)} %convert_element_type.180, f32[6,128]{1,0:T(8,128)S(1)} %add_rsqrt_fusion.3, f32[6,896]{1,0:T(8,128)S(1)} %get-tuple-element.100), kind=kOutput, calls=%fused_computation.13 | convolution fusion | flops 1242071040 | bytes 4386304 | tf_op jit(solution)/shard_map/dot_general | solution.py:359
  40.4 2.6 %collective-permute-start.9 = (bf16[72,1024]{1,0:T(8,128)(2,1)S(1)}, bf16[72,1024]{1,0:T(8,128)(2,1)S(1)}, u32[]{:S(2)}, u32[]{:S(2)}) collective-permute-start(bf16[72,1024]{1,0:T(8,128)(2,1)S(1)} %slice.186), channel_id=1, source_target_pairs={{0,6},{2,0},{4,2},{6,4},{1,7},{3,1},{5,3},{7,5},{8,14},{10,8},{12,... | collective-permute-start | bytes 442376 | tf_op jit(solution)/shard_map/ppermute | solution.py:28
  47.5 18.7 %collective-permute-done.9 = bf16[72,1024]{1,0:T(8,128)(2,1)S(1)} collective-permute-done((bf16[72,1024]{1,0:T(8,128)(2,1)S(1)}, bf16[72,1024]{1,0:T(8,128)(2,1)S(1)}, u32[]{:S(2)}, u32[]{:S(2)}) %collective-permute-start.9) | collective-permute-done | bytes 147488 | tf_op jit(solution)/shard_map/ppermute | solution.py:28
  66.2 1.9 collective-permute-done.11
  69.4 2.0 collective-permute-start.7
  72.2 3.2 %add_convert_fusion.e3 = bf16[6,128,896]{2,1,0:T(8,128)(2,1)} fusion(bf16[6,128,896]{2,1,0:T(8,128)(2,1)S(1)} %collective-permute-done.6, bf16[896,896]{1,0:T(8,128)(2,1)S(1)} %copy-done.15, f32[6,128]{1,0:T(8,128)S(1)} %add_rsqrt_fusion, f32[6,896]{1,0:T(8,128)S(1)} %get-tuple-element.97, f32[896]{0:T(1024)S(1)} %convert_element_type.180), kind=kOutput, calls=%fused_computation.1 | convolution fusion | flops 1242071040 | bytes 4386304 | tf_op jit(solution)/shard_map/dot_general | solution.py:359
  75.4 3.1 %add_convert_fusion.2.e1 = bf16[6,128,896]{2,1,0:T(8,128)(2,1)} fusion(bf16[6,128,896]{2,1,0:T(8,128)(2,1)S(1)} %collective-permute-done.4, bf16[896,896]{1,0:T(8,128)(2,1)S(1)} %copy-done.15, f32[6,128]{1,0:T(8,128)S(1)} %add_rsqrt_fusion.2, f32[6,896]{1,0:T(8,128)S(1)} %get-tuple-element.98, f32[896]{0:T(1024)S(1)} %convert_element_type.180), kind=kOutput, calls=%fused_computation.9 | convolution fusion | flops 1242071040 | bytes 4386304 | tf_op jit(solution)/shard_map/dot_general | solution.py:359
  78.6 3.9 %collective-permute-done.5 = bf16[3,128,896]{2,1,0:T(8,128)(2,1)S(1)} collective-permute-done((bf16[3,128,896]{2,1,0:T(8,128)(2,1)S(1)}, bf16[3,128,896]{2,1,0:T(8,128)(2,1)S(1)}, u32[]{:S(2)}, u32[]{:S(2)}) %collective-permute-start.5) | collective-permute-done | bytes 688160 | tf_op jit(solution)/shard_map/ppermute | solution.py:28
  82.5 4.8 %collective-permute-done.7 = bf16[3,128,896]{2,1,0:T(8,128)(2,1)S(1)} collective-permute-done((bf16[3,128,896]{2,1,0:T(8,128)(2,1)S(1)}, bf16[3,128,896]{2,1,0:T(8,128)(2,1)S(1)}, u32[]{:S(2)}, u32[]{:S(2)}) %collective-permute-start.7) | collective-permute-done | bytes 688160 | tf_op jit(solution)/shard_map/ppermute | solution.py:28
  87.7 1.9 collective-permute-start.14
  89.6 1.6 fusion.51
  91.2 3.7 %project.2.q = bf16[128,512]{1,0:T(8,128)(2,1)S(1)} custom-call(s32[1]{0:T(128)} %bitcast.n_ref, bf16[4,128,1024]{2,1,0:T(8,128)(2,1)S(1)} %fusion.2.x_ref, bf16[32,312,512]{2,1,0:T(8,128)(2,1)} %bitcast.106), custom_call_target="tpu_custom_call" | custom-call | flops 536870912 | bytes 6291456 | tf_op jit(solution)/shard_map/project/pallas_call | solution.py:87
  95.4 2.1 add_convert_fusion.1.e2
  97.6 11.6 %forward.1 = (bf16[16,128,896]{2,1,0:T(8,128)(2,1)}, bf16[128,512]{1,0:T(8,128)(2,1)S(1)}, f32[8,64,1024]{2,1,0:T(8,128)S(1)}, bf16[2048,512]{1,0:T(8,128)(2,1)S(1)}, bf16[2048,512]{1,0:T(8,128)(2,1)S(1)}) custom-call(s32[18]{0:T(128)S(1)} %pad_add_fusion.1.tab, bf16[6,128,896]{2,1,0:T(8,128)(2,1)S(1)} %copy-done.4, bf16[6,128,896]{2,1,0:T(8,128)(2,1)S(1)} %copy-done.6, ...), custom_call_target="tpu_custom_call" | custom-call | flops 3758096384 | bytes 37748736 | tf_op jit(solution)/shard_map/forward/pallas_call | solution.py:155
  109.4 3.6 %project.3.dc = bf16[128,512]{1,0:T(8,128)(2,1)S(1)} custom-call(s32[1]{0:T(128)} %bitcast.n_ref, bf16[4,128,1024]{2,1,0:T(8,128)(2,1)S(1)} %pad_maximum_fusion.3.x_ref.d, bf16[32,312,512]{2,1,0:T(8,128)(2,1)} %bitcast.107), custom_call_target="tpu_custom_call" | custom-call | flops 536870912 | bytes 6291456 | tf_op jit(solution)/shard_map/project/pallas_call | solution.py:87
  113.0 14.1 %backward.1 = (bf16[128,512]{1,0:T(8,128)(2,1)S(1)}, bf16[2048,512]{1,0:T(8,128)(2,1)}, bf16[2048,512]{1,0:T(8,128)(2,1)}, bf16[24,128,896]{2,1,0:T(8,128)(2,1)}) custom-call(s32[24]{0:T(128)S(1)} %get-tuple-element.113.inv, f32[8,64,1024]{2,1,0:T(8,128)S(1)} %get-tuple-element.38.probs, bf16[2048,512]{1,0:T(8,128)(2,1)S(1)} %get-tuple-element.39.kb, ...), custom_call_target="tpu_custom_call" | custom-call | flops 3758096384 | bytes 41943040 | tf_op jit(solution)/shard_map/backward/pallas_call | solution.py:216
  127.3 2.6 %outer.1 = (bf16[4,128,512]{2,1,0:T(8,128)(2,1)S(1)}, bf16[4,128,512]{2,1,0:T(8,128)(2,1)}, bf16[4,128,512]{2,1,0:T(8,128)(2,1)}, bf16[4,128,512]{2,1,0:T(8,128)...) custom-call(s32[3]{0:T(128)S(1)} %pad_add_fusion.2.at, ...), custom_call_target="tpu_custom_call" | custom-call | flops 536870912 | bytes 6291456 | tf_op jit(solution)/shard_map/outer/pallas_call | solution.py:282
  129.9 5.8 %collective-permute-start.18 = (bf16[4,128,512]{2,1,0:T(8,128)(2,1)}, bf16[4,128,512]{2,1,0:T(8,128)(2,1)}, u32[]{:S(2)}, u32[]{:S(2)}) collective-permute-start(bf16[4,128,512]{2,1,0:T(8,128)(2,1)} %get-tuple-element.46), channel_id=1, source_target_pairs={{0,64},{8,72},{16,80},{24,88},{32,96},{40,104},{48,112},{56,120},{... | collective-permute-start | bytes 1572872 | tf_op jit(solution)/shard_map/ppermute | solution.py:294
  136.5 2.3 %collective-permute-start.20 = (bf16[4,128,512]{2,1,0:T(8,128)(2,1)}, bf16[4,128,512]{2,1,0:T(8,128)(2,1)}, u32[]{:S(2)}, u32[]{:S(2)}) collective-permute-start(bf16[4,128,512]{2,1,0:T(8,128)(2,1)} %get-tuple-element.48), channel_id=1, source_target_pairs={{0,96},{8,104},{16,112},{24,120},{32,0},{40,8},{48,16},{56,24},{64... | collective-permute-start | bytes 1572872 | tf_op jit(solution)/shard_map/ppermute | solution.py:294
  138.9 5.8 %convolution_convert_fusion.1 = bf16[896,512]{1,0:T(8,128)(2,1)S(1)} fusion(bf16[2048,896]{1,0:T(8,128)(2,1)} %bitcast.118, bf16[2048,512]{1,0:T(8,128)(2,1)} %get-tuple-element.54), kind=kOutput, calls=%fused_computation.32 | convolution fusion | flops 1879506944 | bytes 6684672 | tf_op jit(solution)/shard_map/dot_general | solution.py:19
  144.8 2.1 convolution_convert_fusion
  146.8 1.4 pad_maximum_fusion
  148.3 4.5 %all-to-all-start = ((bf16[16,112,512]{2,1,0:T(8,128)(2,1)}), bf16[16,112,512]{2,1,0:T(8,128)(2,1)}, u32[]{:S(2)}, u32[]{:S(2)}) async-start(bf16[16,112,512]{2,1,0:T(8,128)(2,1)} %pad_maximum_fusion), calls=%async_computation.1 | async-start | bytes 3670016 | tf_op jit(solution)/shard_map/all_to_all | solution.py:53
  152.8 3.3 %collective-permute-start.24 = (bf16[4,128,512]{2,1,0:T(8,128)(2,1)S(1)}, bf16[4,128,512]{2,1,0:T(8,128)(2,1)S(1)}, u32[]{:S(2)}, u32[]{:S(2)}) collective-permute-start(bf16[4,128,512]{2,1,0:T(8,128)(2,1)S(1)} %copy-done.3), channel_id=1, source_target_pairs={{0,16},{8,24},{16,0},{24,8},{32,48},{40,56},{48,32},{56,40},{64,80... | collective-permute-start | bytes 1572872 | tf_op jit(solution)/shard_map/ppermute | solution.py:298
  156.9 5.9 %unproject.1 = bf16[4,272,1024]{2,1,0:T(8,128)(2,1)S(1)} custom-call(s32[1]{0:T(128)} %bitcast.n_ref, bf16[128,512]{1,0:T(8,128)(2,1)S(1)} %get-tuple-element.43.ctx, bf16[128,512]{1,0:T(8,128)(2,1)S(1)} %get-tuple-element.42.dq, bf16[16,1024]{1,0:T(8,128)(2,1)S(1)} %broadcast_in_dim.140.more, bf16[32,312,512]{2,1,0:T(8,128)(2,1)} %bitcast.108), custom_call_target="tpu_custom_call" | custom-call | flops 1073741824 | bytes 12582912 | tf_op jit(solution)/shard_map/unproject/pallas_call | solution.py:247
  162.9 2.8 %collective-permute-start.26 = (bf16[4,128,512]{2,1,0:T(8,128)(2,1)S(1)}, bf16[4,128,512]{2,1,0:T(8,128)(2,1)S(1)}, u32[]{:S(2)}, u32[]{:S(2)}) collective-permute-start(bf16[4,128,512]{2,1,0:T(8,128)(2,1)S(1)} %get-tuple-element.52), channel_id=1, source_target_pairs={{0,24},{8,0},{16,8},{24,16},{32,56},{40,32},{48,40},{56,48},{64,88... | collective-permute-start | bytes 1572872 | tf_op jit(solution)/shard_map/ppermute | solution.py:298
  165.7 3.6 %collective-permute-start.15 = (bf16[272,1024]{1,0:T(8,128)(2,1)S(1)}, bf16[272,1024]{1,0:T(8,128)(2,1)S(1)}, u32[]{:S(2)}, u32[]{:S(2)}) collective-permute-start(bf16[272,1024]{1,0:T(8,128)(2,1)S(1)} %get-tuple-element.78), channel_id=1, source_target_pairs={{0,4},{2,6},{4,0},{6,2},{1,5},{3,7},{5,1},{7,3},{8,12},{10,14},{12... | collective-permute-start | bytes 1671176 | tf_op jit(solution)/shard_map/ppermute | solution.py:28
  169.3 1.6 add_convert_fusion.5
  170.9 14.5 %collective-permute-done.24 = bf16[4,128,512]{2,1,0:T(8,128)(2,1)S(1)} collective-permute-done((bf16[4,128,512]{2,1,0:T(8,128)(2,1)S(1)}, bf16[4,128,512]{2,1,0:T(8,128)(2,1)S(1)}, u32[]{:S(2)}, u32[]{:S(2)}) %collective-permute-start.24) | collective-permute-done | bytes 524320 | tf_op jit(solution)/shard_map/ppermute | solution.py:298
  185.4 2.9 %collective-permute-start.17 = (bf16[272,1024]{1,0:T(8,128)(2,1)S(1)}, bf16[272,1024]{1,0:T(8,128)(2,1)S(1)}, u32[]{:S(2)}, u32[]{:S(2)}) collective-permute-start(bf16[272,1024]{1,0:T(8,128)(2,1)S(1)} %get-tuple-element.79), channel_id=1, source_target_pairs={{0,6},{2,0},{4,2},{6,4},{1,7},{3,1},{5,3},{7,5},{8,14},{10,8},{12,... | collective-permute-start | bytes 1671176 | tf_op jit(solution)/shard_map/ppermute | solution.py:28
  188.8 1.7 collective-permute-start.21
  190.5 1.9 collective-permute-start.22
  192.7 2.2 collective-permute-done.15
  195.0 12.5 %collective-permute-done.16 = bf16[272,1024]{1,0:T(8,128)(2,1)S(1)} collective-permute-done((bf16[272,1024]{1,0:T(8,128)(2,1)S(1)}, bf16[272,1024]{1,0:T(8,128)(2,1)S(1)}, u32[]{:S(2)}, u32[]{:S(2)}) %collective-permute-start.16) | collective-permute-done | bytes 557088 | tf_op jit(solution)/shard_map/ppermute | solution.py:28
  207.5 3.2 %collective-permute-start.27 = (bf16[128,512]{1,0:T(8,128)(2,1)S(1)}, bf16[128,512]{1,0:T(8,128)(2,1)S(1)}, u32[]{:S(2)}, u32[]{:S(2)}) collective-permute-start(bf16[128,512]{1,0:T(8,128)(2,1)S(1)} %get-tuple-element.86), channel_id=1, source_target_pairs={{0,64},{8,72},{16,80},{24,88},{32,96},{40,104},{48,112},{56,120},{... | collective-permute-start | bytes 393224 | tf_op jit(solution)/shard_map/ppermute | solution.py:294
  211.7 1.1 fusion.36
  212.8 2.7 %collective-permute-start.29 = (bf16[128,512]{1,0:T(8,128)(2,1)S(1)}, bf16[128,512]{1,0:T(8,128)(2,1)S(1)}, u32[]{:S(2)}, u32[]{:S(2)}) collective-permute-start(bf16[128,512]{1,0:T(8,128)(2,1)S(1)} %get-tuple-element.87), channel_id=1, source_target_pairs={{0,96},{8,104},{16,112},{24,120},{32,0},{40,8},{48,16},{56,24},{64... | collective-permute-start | bytes 393224 | tf_op jit(solution)/shard_map/ppermute | solution.py:294
  215.5 1.3 collective-permute-done.28
  219.1 1.8 convert_reduce_fusion
  (146 shorter events, 23.2 us)
Async XLA Ops:
  7.2 17.8 %copy-start = (bf16[1024,896]{1,0:T(8,128)(2,1)S(1)}, bf16[1024,896]{1,0:T(8,128)(2,1)}, u32[]{:S(2)}) copy-start(bf16[1024,896]{1,0:T(8,128)(2,1)} %param.18) | copy-start | bytes 5505028
  7.2 12.5 %copy-start.7 = (bf16[128,1024]{1,0:T(8,128)(2,1)S(1)}, bf16[128,1024]{1,0:T(8,128)(2,1)}, u32[]{:S(2)}) copy-start(bf16[128,1024]{1,0:T(8,128)(2,1)} %param.12) | copy-start | bytes 786436
  7.2 23.0 %copy-start.12 = (bf16[1024]{0:T(1024)(128)(2,1)S(1)}, bf16[1024]{0:T(1024)(128)(2,1)}, u32[]{:S(2)}) copy-start(bf16[1024]{0:T(1024)(128)(2,1)} %param.16) | copy-start | bytes 6148
  7.2 16.4 %copy-start.14 = (s32[24]{0:T(128)S(1)}, s32[24]{0:T(128)}, u32[]{:S(2)}) copy-start(s32[24]{0:T(128)} %param.15) | copy-start | bytes 292
  7.2 23.0 %copy-start.13 = (bf16[896]{0:T(1024)(128)(2,1)S(1)}, bf16[896]{0:T(1024)(128)(2,1)}, u32[]{:S(2)}) copy-start(bf16[896]{0:T(1024)(128)(2,1)} %param.17) | copy-start | bytes 5380
  7.2 26.5 %copy-start.9 = (bf16[6,128,896]{2,1,0:T(8,128)(2,1)S(1)}, bf16[6,128,896]{2,1,0:T(8,128)(2,1)}, u32[]{:S(2)}) copy-start(bf16[6,128,896]{2,1,0:T(8,128)(2,1)} %param.14) | copy-start | bytes 4128772
  7.2 80.2 %all-gather.3.cloned.1.call-start = ((), (), s32[]{:S(2)}) async-start(), calls=%async_computation.3 | async-start | bytes 10543104 | tf_op jit(solution)/shard_map/all_gather | solution.py:326
  14.1 207.5 %reduce-scatter.2.cloned.1.call-start = ((), (), s32[]{:S(2)}) async-start(), calls=%async_computation.2 | async-start | bytes 6881280 | tf_op jit(solution)/shard_map/reduce_scatter | solution.py:392
  16.6 22.9 %collective-permute-start.8 = (bf16[144,1024]{1,0:T(8,128)(2,1)}, bf16[144,1024]{1,0:T(8,128)(2,1)}, u32[]{:S(2)}, u32[]{:S(2)}) collective-permute-start(bf16[144,1024]{1,0:T(8,128)(2,1)} %pad_maximum_fusion.5), channel_id=1, source_target_pairs={{0,6},{2,0},{4,2},{6,4},{1,7},{3,1},{5,3},{7,5},{8,14},{10,8},{12,... | collective-permute-start | bytes 884744 | tf_op jit(solution)/shard_map/ppermute | solution.py:28
  19.7 23.3 %collective-permute-start.10 = (bf16[144,1024]{1,0:T(8,128)(2,1)}, bf16[144,1024]{1,0:T(8,128)(2,1)}, u32[]{:S(2)}, u32[]{:S(2)}) collective-permute-start(bf16[144,1024]{1,0:T(8,128)(2,1)} %pad_maximum_fusion.5), channel_id=1, source_target_pairs={{0,2},{2,4},{4,6},{6,0},{1,3},{3,5},{5,7},{7,1},{8,10},{10,12},{12... | collective-permute-start | bytes 884744 | tf_op jit(solution)/shard_map/ppermute | solution.py:28
  19.8 5.1 %collective-permute-start = (bf16[1,1024]{1,0:T(2,128)(2,1)S(1)}, bf16[1,1024]{1,0:T(2,128)(2,1)S(1)}, u32[]{:S(2)}, u32[]{:S(2)}) collective-permute-start(bf16[1,1024]{1,0:T(2,128)(2,1)S(1)} %get-tuple-element.101), channel_id=1, source_target_pairs={{0,8},{8,16},{16,24},{24,32},{32,40},{40,48},{48,56},{56,64},{64,7... | collective-permute-start | bytes 6152 | tf_op jit(solution)/shard_map/ppermute | solution.py:337
  23.7 12.7 %copy-start.15 = (bf16[896,896]{1,0:T(8,128)(2,1)S(1)}, bf16[896,896]{1,0:T(8,128)(2,1)}, u32[]{:S(2)}) copy-start(bf16[896,896]{1,0:T(8,128)(2,1)} %param.19) | copy-start | bytes 4816900
  25.3 5.0 %collective-permute-start.1 = (f32[2,896]{1,0:T(2,128)S(1)}, f32[2,896]{1,0:T(2,128)S(1)}, u32[]{:S(2)}, u32[]{:S(2)}) collective-permute-start(f32[2,896]{1,0:T(2,128)S(1)} %fusion.43), channel_id=1, source_target_pairs={{0,2},{2,4},{4,6},{6,0},{1,3},{3,5},{5,7},{7,1},{8,10},{10,12},{12... | collective-permute-start | bytes 21512 | tf_op jit(solution)/shard_map/ppermute | solution.py:28
  25.9 5.8 %collective-permute-start.2 = (f32[2,896]{1,0:T(2,128)S(1)}, f32[2,896]{1,0:T(2,128)S(1)}, u32[]{:S(2)}, u32[]{:S(2)}) collective-permute-start(f32[2,896]{1,0:T(2,128)S(1)} %fusion.43), channel_id=1, source_target_pairs={{0,4},{2,6},{4,0},{6,2},{1,5},{3,7},{5,1},{7,3},{8,12},{10,14},{12... | collective-permute-start | bytes 21512 | tf_op jit(solution)/shard_map/ppermute | solution.py:28
  30.0 3.7 %collective-permute-start.3 = (f32[2,896]{1,0:T(2,128)S(1)}, f32[2,896]{1,0:T(2,128)S(1)}, u32[]{:S(2)}, u32[]{:S(2)}) collective-permute-start(f32[2,896]{1,0:T(2,128)S(1)} %fusion.43), channel_id=1, source_target_pairs={{0,6},{2,0},{4,2},{6,4},{1,7},{3,1},{5,3},{7,5},{8,14},{10,8},{12,... | collective-permute-start | bytes 21512 | tf_op jit(solution)/shard_map/ppermute | solution.py:28
  33.7 35.1 %collective-permute-start.4 = (bf16[6,128,896]{2,1,0:T(8,128)(2,1)S(1)}, bf16[6,128,896]{2,1,0:T(8,128)(2,1)S(1)}, u32[]{:S(2)}, u32[]{:S(2)}) collective-permute-start(bf16[6,128,896]{2,1,0:T(8,128)(2,1)S(1)} %copy-done.9), channel_id=1, source_target_pairs={{0,6},{2,0},{4,2},{6,4},{1,7},{3,1},{5,3},{7,5},{8,14},{10,8},{12,... | collective-permute-start | bytes 4128776 | tf_op jit(solution)/shard_map/ppermute | solution.py:28
  35.1 34.3 %collective-permute-start.6 = (bf16[6,128,896]{2,1,0:T(8,128)(2,1)S(1)}, bf16[6,128,896]{2,1,0:T(8,128)(2,1)S(1)}, u32[]{:S(2)}, u32[]{:S(2)}) collective-permute-start(bf16[6,128,896]{2,1,0:T(8,128)(2,1)S(1)} %copy-done.9), channel_id=1, source_target_pairs={{0,2},{2,4},{4,6},{6,0},{1,3},{3,5},{5,7},{7,1},{8,10},{10,12},{12... | collective-permute-start | bytes 4128776 | tf_op jit(solution)/shard_map/ppermute | solution.py:28
  40.4 25.7 %collective-permute-start.9 = (bf16[72,1024]{1,0:T(8,128)(2,1)S(1)}, bf16[72,1024]{1,0:T(8,128)(2,1)S(1)}, u32[]{:S(2)}, u32[]{:S(2)}) collective-permute-start(bf16[72,1024]{1,0:T(8,128)(2,1)S(1)} %slice.186), channel_id=1, source_target_pairs={{0,6},{2,0},{4,2},{6,4},{1,7},{3,1},{5,3},{7,5},{8,14},{10,8},{12,... | collective-permute-start | bytes 442376 | tf_op jit(solution)/shard_map/ppermute | solution.py:28
  43.9 24.2 %collective-permute-start.11 = (bf16[72,1024]{1,0:T(8,128)(2,1)S(1)}, bf16[72,1024]{1,0:T(8,128)(2,1)S(1)}, u32[]{:S(2)}, u32[]{:S(2)}) collective-permute-start(bf16[72,1024]{1,0:T(8,128)(2,1)S(1)} %slice.188), channel_id=1, source_target_pairs={{0,2},{2,4},{4,6},{6,0},{1,3},{3,5},{5,7},{7,1},{8,10},{10,12},{12... | collective-permute-start | bytes 442376 | tf_op jit(solution)/shard_map/ppermute | solution.py:28
  68.9 13.6 %collective-permute-start.5 = (bf16[3,128,896]{2,1,0:T(8,128)(2,1)S(1)}, bf16[3,128,896]{2,1,0:T(8,128)(2,1)S(1)}, u32[]{:S(2)}, u32[]{:S(2)}) collective-permute-start(bf16[3,128,896]{2,1,0:T(8,128)(2,1)S(1)} %slice.182), channel_id=1, source_target_pairs={{0,6},{2,0},{4,2},{6,4},{1,7},{3,1},{5,3},{7,5},{8,14},{10,8},{12,... | collective-permute-start | bytes 2064392 | tf_op jit(solution)/shard_map/ppermute | solution.py:28
  69.4 17.9 %collective-permute-start.7 = (bf16[3,128,896]{2,1,0:T(8,128)(2,1)S(1)}, bf16[3,128,896]{2,1,0:T(8,128)(2,1)S(1)}, u32[]{:S(2)}, u32[]{:S(2)}) collective-permute-start(bf16[3,128,896]{2,1,0:T(8,128)(2,1)S(1)} %slice.183), channel_id=1, source_target_pairs={{0,2},{2,4},{4,6},{6,0},{1,3},{3,5},{5,7},{7,1},{8,10},{10,12},{12... | collective-permute-start | bytes 2064392 | tf_op jit(solution)/shard_map/ppermute | solution.py:28
  78.6 8.9 %copy-start.10 = (bf16[128,1024]{1,0:T(8,128)(2,1)S(1)}, bf16[128,1024]{1,0:T(8,128)(2,1)}, u32[]{:S(2)}) copy-start(bf16[128,1024]{1,0:T(8,128)(2,1)} %param.13) | copy-start | bytes 786436
  87.5 21.7 %collective-permute-start.12 = (bf16[128,1024]{1,0:T(8,128)(2,1)S(1)}, bf16[128,1024]{1,0:T(8,128)(2,1)S(1)}, u32[]{:S(2)}, u32[]{:S(2)}) collective-permute-start(bf16[128,1024]{1,0:T(8,128)(2,1)S(1)} %copy-done.10), channel_id=1, source_target_pairs={{0,6},{2,0},{4,2},{6,4},{1,7},{3,1},{5,3},{7,5},{8,14},{10,8},{12,... | collective-permute-start | bytes 786440 | tf_op jit(solution)/shard_map/ppermute | solution.py:28
  87.6 21.6 %collective-permute-start.13 = (bf16[128,1024]{1,0:T(8,128)(2,1)S(1)}, bf16[128,1024]{1,0:T(8,128)(2,1)S(1)}, u32[]{:S(2)}, u32[]{:S(2)}) collective-permute-start(bf16[128,1024]{1,0:T(8,128)(2,1)S(1)} %copy-done.10), channel_id=1, source_target_pairs={{0,4},{2,6},{4,0},{6,2},{1,5},{3,7},{5,1},{7,3},{8,12},{10,14},{12... | collective-permute-start | bytes 786440 | tf_op jit(solution)/shard_map/ppermute | solution.py:28
  87.7 21.5 %collective-permute-start.14 = (bf16[128,1024]{1,0:T(8,128)(2,1)S(1)}, bf16[128,1024]{1,0:T(8,128)(2,1)S(1)}, u32[]{:S(2)}, u32[]{:S(2)}) collective-permute-start(bf16[128,1024]{1,0:T(8,128)(2,1)S(1)} %copy-done.10), channel_id=1, source_target_pairs={{0,2},{2,4},{4,6},{6,0},{1,3},{3,5},{5,7},{7,1},{8,10},{10,12},{12... | collective-permute-start | bytes 786440 | tf_op jit(solution)/shard_map/ppermute | solution.py:28
  129.9 14.8 %copy-start.2 = (bf16[4,128,512]{2,1,0:T(8,128)(2,1)}, bf16[4,128,512]{2,1,0:T(8,128)(2,1)S(1)}, u32[]{:S(2)}) copy-start(bf16[4,128,512]{2,1,0:T(8,128)(2,1)S(1)} %get-tuple-element.50) | copy-start | bytes 1572868
  129.9 33.0 %collective-permute-start.18 = (bf16[4,128,512]{2,1,0:T(8,128)(2,1)}, bf16[4,128,512]{2,1,0:T(8,128)(2,1)}, u32[]{:S(2)}, u32[]{:S(2)}) collective-permute-start(bf16[4,128,512]{2,1,0:T(8,128)(2,1)} %get-tuple-element.46), channel_id=1, source_target_pairs={{0,64},{8,72},{16,80},{24,88},{32,96},{40,104},{48,112},{56,120},{... | collective-permute-start | bytes 1572872 | tf_op jit(solution)/shard_map/ppermute | solution.py:294
  135.6 30.1 %collective-permute-start.19 = (bf16[4,128,512]{2,1,0:T(8,128)(2,1)}, bf16[4,128,512]{2,1,0:T(8,128)(2,1)}, u32[]{:S(2)}, u32[]{:S(2)}) collective-permute-start(bf16[4,128,512]{2,1,0:T(8,128)(2,1)} %get-tuple-element.47), channel_id=1, source_target_pairs={{0,32},{8,40},{16,48},{24,56},{32,64},{40,72},{48,80},{56,88},{64,... | collective-permute-start | bytes 1572872 | tf_op jit(solution)/shard_map/ppermute | solution.py:294
  136.5 32.8 %collective-permute-start.20 = (bf16[4,128,512]{2,1,0:T(8,128)(2,1)}, bf16[4,128,512]{2,1,0:T(8,128)(2,1)}, u32[]{:S(2)}, u32[]{:S(2)}) collective-permute-start(bf16[4,128,512]{2,1,0:T(8,128)(2,1)} %get-tuple-element.48), channel_id=1, source_target_pairs={{0,96},{8,104},{16,112},{24,120},{32,0},{40,8},{48,16},{56,24},{64... | collective-permute-start | bytes 1572872 | tf_op jit(solution)/shard_map/ppermute | solution.py:294
  138.9 5.9 %copy-start.17 = (bf16[16,128,896]{2,1,0:T(8,128)(2,1)S(1)}, bf16[16,128,896]{2,1,0:T(8,128)(2,1)}, u32[]{:S(2)}) copy-start(bf16[16,128,896]{2,1,0:T(8,128)(2,1)} %get-tuple-element.53) | copy-start | bytes 11010052
  138.9 5.9 %copy-start.18 = (bf16[2048,512]{1,0:T(8,128)(2,1)S(1)}, bf16[2048,512]{1,0:T(8,128)(2,1)}, u32[]{:S(2)}) copy-start(bf16[2048,512]{1,0:T(8,128)(2,1)} %get-tuple-element.55) | copy-start | bytes 6291460
  148.3 4.6 %copy-start.3 = (bf16[4,128,512]{2,1,0:T(8,128)(2,1)S(1)}, bf16[4,128,512]{2,1,0:T(8,128)(2,1)}, u32[]{:S(2)}) copy-start(bf16[4,128,512]{2,1,0:T(8,128)(2,1)} %copy-done.2) | copy-start | bytes 1572868
  148.3 70.8 %all-to-all-start = ((bf16[16,112,512]{2,1,0:T(8,128)(2,1)}), bf16[16,112,512]{2,1,0:T(8,128)(2,1)}, u32[]{:S(2)}, u32[]{:S(2)}) async-start(bf16[16,112,512]{2,1,0:T(8,128)(2,1)} %pad_maximum_fusion), calls=%async_computation.1 | async-start | bytes 3670016 | tf_op jit(solution)/shard_map/all_to_all | solution.py:53
  152.8 32.6 %collective-permute-start.24 = (bf16[4,128,512]{2,1,0:T(8,128)(2,1)S(1)}, bf16[4,128,512]{2,1,0:T(8,128)(2,1)S(1)}, u32[]{:S(2)}, u32[]{:S(2)}) collective-permute-start(bf16[4,128,512]{2,1,0:T(8,128)(2,1)S(1)} %copy-done.3), channel_id=1, source_target_pairs={{0,16},{8,24},{16,0},{24,8},{32,48},{40,56},{48,32},{56,40},{64,80... | collective-permute-start | bytes 1572872 | tf_op jit(solution)/shard_map/ppermute | solution.py:298
  156.2 32.6 %collective-permute-start.25 = (bf16[4,128,512]{2,1,0:T(8,128)(2,1)S(1)}, bf16[4,128,512]{2,1,0:T(8,128)(2,1)S(1)}, u32[]{:S(2)}, u32[]{:S(2)}) collective-permute-start(bf16[4,128,512]{2,1,0:T(8,128)(2,1)S(1)} %get-tuple-element.51), channel_id=1, source_target_pairs={{0,8},{8,16},{16,24},{24,0},{32,40},{40,48},{48,56},{56,32},{64,72... | collective-permute-start | bytes 1572872 | tf_op jit(solution)/shard_map/ppermute | solution.py:298
  162.9 27.6 %collective-permute-start.26 = (bf16[4,128,512]{2,1,0:T(8,128)(2,1)S(1)}, bf16[4,128,512]{2,1,0:T(8,128)(2,1)S(1)}, u32[]{:S(2)}, u32[]{:S(2)}) collective-permute-start(bf16[4,128,512]{2,1,0:T(8,128)(2,1)S(1)} %get-tuple-element.52), channel_id=1, source_target_pairs={{0,24},{8,0},{16,8},{24,16},{32,56},{40,32},{48,40},{56,48},{64,88... | collective-permute-start | bytes 1572872 | tf_op jit(solution)/shard_map/ppermute | solution.py:298
  165.7 29.2 %collective-permute-start.15 = (bf16[272,1024]{1,0:T(8,128)(2,1)S(1)}, bf16[272,1024]{1,0:T(8,128)(2,1)S(1)}, u32[]{:S(2)}, u32[]{:S(2)}) collective-permute-start(bf16[272,1024]{1,0:T(8,128)(2,1)S(1)} %get-tuple-element.78), channel_id=1, source_target_pairs={{0,4},{2,6},{4,0},{6,2},{1,5},{3,7},{5,1},{7,3},{8,12},{10,14},{12... | collective-permute-start | bytes 1671176 | tf_op jit(solution)/shard_map/ppermute | solution.py:28
  169.3 38.2 %collective-permute-start.16 = (bf16[272,1024]{1,0:T(8,128)(2,1)S(1)}, bf16[272,1024]{1,0:T(8,128)(2,1)S(1)}, u32[]{:S(2)}, u32[]{:S(2)}) collective-permute-start(bf16[272,1024]{1,0:T(8,128)(2,1)S(1)} %get-tuple-element.80), channel_id=1, source_target_pairs={{0,2},{2,4},{4,6},{6,0},{1,3},{3,5},{5,7},{7,1},{8,10},{10,12},{12... | collective-permute-start | bytes 1671176 | tf_op jit(solution)/shard_map/ppermute | solution.py:28
  185.4 25.3 %collective-permute-start.17 = (bf16[272,1024]{1,0:T(8,128)(2,1)S(1)}, bf16[272,1024]{1,0:T(8,128)(2,1)S(1)}, u32[]{:S(2)}, u32[]{:S(2)}) collective-permute-start(bf16[272,1024]{1,0:T(8,128)(2,1)S(1)} %get-tuple-element.79), channel_id=1, source_target_pairs={{0,6},{2,0},{4,2},{6,4},{1,7},{3,1},{5,3},{7,5},{8,14},{10,8},{12,... | collective-permute-start | bytes 1671176 | tf_op jit(solution)/shard_map/ppermute | solution.py:28
  188.8 24.0 %collective-permute-start.21 = (bf16[128,512]{1,0:T(8,128)(2,1)S(1)}, bf16[128,512]{1,0:T(8,128)(2,1)S(1)}, u32[]{:S(2)}, u32[]{:S(2)}) collective-permute-start(bf16[128,512]{1,0:T(8,128)(2,1)S(1)} %get-tuple-element.83), channel_id=1, source_target_pairs={{0,16},{8,24},{16,0},{24,8},{32,48},{40,56},{48,32},{56,40},{64,80... | collective-permute-start | bytes 393224 | tf_op jit(solution)/shard_map/ppermute | solution.py:298
  190.5 24.9 %collective-permute-start.22 = (bf16[128,512]{1,0:T(8,128)(2,1)S(1)}, bf16[128,512]{1,0:T(8,128)(2,1)S(1)}, u32[]{:S(2)}, u32[]{:S(2)}) collective-permute-start(bf16[128,512]{1,0:T(8,128)(2,1)S(1)} %get-tuple-element.85), channel_id=1, source_target_pairs={{0,8},{8,16},{16,24},{24,0},{32,40},{40,48},{48,56},{56,32},{64,72... | collective-permute-start | bytes 393224 | tf_op jit(solution)/shard_map/ppermute | solution.py:298
  192.4 19.3 %copy-start.8 = (bf16[128,1024]{1,0:T(8,128)(2,1)S(1)}, bf16[128,1024]{1,0:T(8,128)(2,1)}, u32[]{:S(2)}) copy-start(bf16[128,1024]{1,0:T(8,128)(2,1)} %param.12) | copy-start | bytes 786436
  192.4 19.3 %copy-start.11 = (bf16[128,1024]{1,0:T(8,128)(2,1)S(1)}, bf16[128,1024]{1,0:T(8,128)(2,1)}, u32[]{:S(2)}) copy-start(bf16[128,1024]{1,0:T(8,128)(2,1)} %param.13) | copy-start | bytes 786436
  194.9 20.6 %collective-permute-start.23 = (bf16[128,512]{1,0:T(8,128)(2,1)S(1)}, bf16[128,512]{1,0:T(8,128)(2,1)S(1)}, u32[]{:S(2)}, u32[]{:S(2)}) collective-permute-start(bf16[128,512]{1,0:T(8,128)(2,1)S(1)} %get-tuple-element.84), channel_id=1, source_target_pairs={{0,24},{8,0},{16,8},{24,16},{32,56},{40,32},{48,40},{56,48},{64,88... | collective-permute-start | bytes 393224 | tf_op jit(solution)/shard_map/ppermute | solution.py:298
  207.5 8.0 %collective-permute-start.27 = (bf16[128,512]{1,0:T(8,128)(2,1)S(1)}, bf16[128,512]{1,0:T(8,128)(2,1)S(1)}, u32[]{:S(2)}, u32[]{:S(2)}) collective-permute-start(bf16[128,512]{1,0:T(8,128)(2,1)S(1)} %get-tuple-element.86), channel_id=1, source_target_pairs={{0,64},{8,72},{16,80},{24,88},{32,96},{40,104},{48,112},{56,120},{... | collective-permute-start | bytes 393224 | tf_op jit(solution)/shard_map/ppermute | solution.py:294
  210.7 6.2 %collective-permute-start.28 = (bf16[128,512]{1,0:T(8,128)(2,1)S(1)}, bf16[128,512]{1,0:T(8,128)(2,1)S(1)}, u32[]{:S(2)}, u32[]{:S(2)}) collective-permute-start(bf16[128,512]{1,0:T(8,128)(2,1)S(1)} %get-tuple-element.88), channel_id=1, source_target_pairs={{0,32},{8,40},{16,48},{24,56},{32,64},{40,72},{48,80},{56,88},{64,... | collective-permute-start | bytes 393224 | tf_op jit(solution)/shard_map/ppermute | solution.py:294
  212.8 5.2 %collective-permute-start.29 = (bf16[128,512]{1,0:T(8,128)(2,1)S(1)}, bf16[128,512]{1,0:T(8,128)(2,1)S(1)}, u32[]{:S(2)}, u32[]{:S(2)}) collective-permute-start(bf16[128,512]{1,0:T(8,128)(2,1)S(1)} %get-tuple-element.87), channel_id=1, source_target_pairs={{0,96},{8,104},{16,112},{24,120},{32,0},{40,8},{48,16},{56,24},{64... | collective-permute-start | bytes 393224 | tf_op jit(solution)/shard_map/ppermute | solution.py:294
  215.5 6.1 %copy-start.1 = (bf16[1024,896]{1,0:T(8,128)(2,1)S(1)}, bf16[1024,896]{1,0:T(8,128)(2,1)}, u32[]{:S(2)}) copy-start(bf16[1024,896]{1,0:T(8,128)(2,1)} %param.18) | copy-start | bytes 5505028
  (4 other events, 10.6 us)
Sparse Core Ops, SparseCore 0:
  14.2 59.7 all-gather.2
  127.3 85.1 reduce-scatter.1
where the time goes:
time: 231 us; the launch traced here: 228 us
  waiting for transfers between devices  65.6 us (28%)
  starting transfers between devices  57.9 us (25%)
  Pallas kernels  41.6 us (18%)
  matrix products  19.8 us (9%)
  local copies, waits for them, and re-layouts  15.1 us (7%)
  between operations  14.7 us (6%)
  other arithmetic  13.6 us (6%)
    ppermute x17, waiting for transfers between devices, shift(): return lax.ppermute(x, 'nbr', [(i, (i + by) % n) for i in range(n)])  47.5 us
    ppermute x17, starting transfers between devices, shift(): return lax.ppermute(x, 'nbr', [(i, (i + by) % n) for i in range(n)])  23.6 us
    ppermute x6, starting transfers between devices, along_x(): lax.ppermute(share, 'seq', [(i, (i // 4 + by) % 4 * 4 + i % 4) for i in r...  15.4 us
    ppermute x6, waiting for transfers between devices, along_z(): lax.ppermute(share, 'seq', [(i, i // 4 * 4 + (i + by) % 4) for i in range...  14.9 us
    pallas_call x1, Pallas kernels, backward(): pl.pallas_call(backward_kernel, in_specs=[SMEM] + [VMEM] * 7, out_specs=[...  14.1 us
    pallas_call x1, Pallas kernels, forward(): pl.pallas_call(forward_kernel, in_specs=[SMEM] + [VMEM] * 7, out_specs=[V...  11.6 us
    dot_general x4, matrix products, encode(): jnp.dot(enc_normed.reshape(-1, width), w_enc, preferred_element_type=F32)  11.6 us
    ppermute x6, starting transfers between devices, along_z(): lax.ppermute(share, 'seq', [(i, i // 4 * 4 + (i + by) % 4) for i in range...  10.4 us
  transfers between devices with their start and end apart: 33, of which 13 were waited for; matrix products, arithmetic and copies ran while one was open for 18% of the time, Pallas kernels for 10%

commit v1 on v0

v1 whole, which is shorter than its diff:
```python
import jax
import jax.numpy as jnp
from jax import lax
from jax.experimental import pallas as pl
from jax.experimental.pallas import tpu as pltpu
from jax.sharding import PartitionSpec as P

HD = 128
CLEN = 64
NLEN = 128
KMAX = 8
F32 = jnp.float32
BF16 = jnp.bfloat16
VMEM = pl.BlockSpec(memory_space=pltpu.VMEM)
SMEM = pl.BlockSpec(memory_space=pltpu.SMEM)


def dot(a, b, dims=((1,), (0,))):
    return lax.dot_general(a, b, (dims, ((), ())), preferred_element_type=F32)


NT = ((1,), (1,))
TN = ((0,), (0,))


def shift(x, by):
    n = lax.axis_size("nbr")
    return lax.ppermute(x, "nbr", [(i, (i + by) % n) for i in range(n)])


def ring_gather(x):
    half = x.shape[0] // 2
    right = shift(x, -1)
    left = shift(x, 1)
    far_a = shift(right[:half], -1)
    far_b = shift(left[half:], 1)
    return right, far_a, far_b, left


def scattered(parts):
    return [parts[0]] + [shift(parts[r], r) for r in (2, 1, 3)]


def total(shares):
    return sum(x.astype(F32) for x in shares)


def sum_small(x):
    return x + shift(x, 1) + shift(x, 2) + shift(x, 3)


def exchange(parts):
    return lax.all_to_all(parts, "seq", split_axis=0, concat_axis=0, tiled=True)


def rms_scale(values):
    return lax.rsqrt(jnp.mean(values * values, axis=-1, keepdims=True) + 1e-06)


def cost(products, moved):
    return pl.CostEstimate(flops=2 * products, transcendentals=0, bytes_accessed=moved)


def project_kernel(n_ref, x, d, w, o):
    wq = w[:, :128].reshape(1024, 512)
    wo = w[:, 128:].reshape(1024, 512)
    tokens = x.shape[0]
    o[0, :tokens] = dot(x[...], wq).astype(BF16)
    o[0, tokens:] = dot(d[...], wo).astype(BF16)


def project(n, normed, dout, weights):
    tokens, feats = normed.shape
    return pl.pallas_call(
        project_kernel,
        grid_spec=pltpu.PrefetchScalarGridSpec(
            num_scalar_prefetch=1,
            grid=(4,),
            in_specs=[
                pl.BlockSpec((tokens, feats), lambda r, n: (0, 0)),
                pl.BlockSpec((tokens, feats), lambda r, n: (0, 0)),
                pl.BlockSpec((8, 256, 512), lambda r, n: ((n[0] + r) % 4, 0, 0)),
            ],
            out_specs=pl.BlockSpec((1, 2 * tokens, 512), lambda r, n: (r, 0, 0)),
        ),
        out_shape=jax.ShapeDtypeStruct((4, 2 * tokens, 512), BF16),
        cost_estimate=cost(2 * tokens * 4096 * 512, 12 << 20),
        compiler_params=pltpu.CompilerParams(vmem_limit_bytes=24 << 20),
        name="project",
    )(n, normed, dout, weights)


def keys_kernel(tab, e0, e1, e2, e3, wk, wv, enc, kb, vb):
    tables = ((e0, 0), (e1, 6), (e2, 12), (e3, 18))

    def pick(j, carry):
        src = tab[j]

        @pl.when(src < 0)
        def _():
            enc[j] = jnp.zeros(enc.shape[1:], BF16)

        for ref, first in tables:

            @pl.when((src >= first) & (src < first + ref.shape[0]))
            def _(ref=ref, first=first):
                enc[j] = ref[src - first]

        return carry

    lax.fori_loop(0, 2 * KMAX, pick, 0)

    def kv(c, carry):
        x = enc[pl.ds(4 * c, 4)].reshape(4 * NLEN, enc.shape[2])
        rows = pl.ds(pl.multiple_of(c * 512, 512), 512)
        kb[rows, :] = dot(x, wk[...]).astype(BF16)
        vb[rows, :] = dot(x, wv[...]).astype(BF16)
        return carry

    lax.fori_loop(0, 4, kv, 0)


def keys_values(tab, blocks, wk, wv):
    rows = 2 * KMAX * NLEN
    flat = jax.ShapeDtypeStruct((rows, wk.shape[1]), BF16)
    return pl.pallas_call(
        keys_kernel,
        in_specs=[SMEM] + [VMEM] * 6,
        out_specs=[VMEM] * 3,
        out_shape=[pltpu.HBM((2 * KMAX, NLEN, wk.shape[0]), BF16), flat, flat],
        cost_estimate=cost(2048 * 896 * 1024, 16 << 20),
        compiler_params=pltpu.CompilerParams(vmem_limit_bytes=26 << 20),
        name="keys_values",
    )(tab, *blocks, wk, wv)


def attend_kernel(tab, inv, kb, vb, q, dc, wk, wv, ctx, dq, dk, dv, out, de):
    factor = HD ** (-0.5)
    heads = q.shape[1] // HD
    keys = KMAX * NLEN
    for c in range(2):
        limit = tab[2 * KMAX + c] * NLEN
        allowed = lax.broadcasted_iota(jnp.int32, (CLEN, keys), 1) < limit
        toks = slice(c * CLEN, (c + 1) * CLEN)
        rows = slice(c * keys, (c + 1) * keys)
        for h in range(heads):
            cols = slice(h * HD, (h + 1) * HD)
            qh, dh = q[toks, cols], dc[toks, cols]
            s = jnp.where(allowed, dot(qh, kb[rows, cols], NT) * factor, -1e30)
            w = jnp.exp(s - jnp.max(s, axis=-1, keepdims=True))
            p = w / jnp.sum(w, axis=-1, keepdims=True)
            pb = p.astype(BF16)
            ctx[toks, cols] = dot(pb, vb[rows, cols]).astype(BF16)
            dp = dot(dh, vb[rows, cols], NT)
            rd = jnp.sum(p * dp, axis=-1, keepdims=True)
            ds = (p * (dp - rd) * factor).astype(BF16)
            dq[toks, cols] = dot(ds, kb[rows, cols]).astype(BF16)
            dk[rows, cols] = dot(ds, qh, TN).astype(BF16)
            dv[rows, cols] = dot(pb, dh, TN).astype(BF16)

    def grad(c, carry):
        rows = pl.ds(pl.multiple_of(c * 512, 512), 512)
        part = dot(dk[rows, :], wk[...], NT) + dot(dv[rows, :], wv[...], NT)
        de[pl.ds(4 * c, 4)] = part.astype(BF16).reshape(4, NLEN, wk.shape[0])
        return carry

    lax.fori_loop(0, 4, grad, 0)

    def place(i, carry):
        src = inv[i]

        @pl.when(src < 0)
        def _():
            out[i] = jnp.zeros(out.shape[1:], BF16)

        @pl.when(src >= 0)
        def _():
            out[i] = de[src]

        return carry

    lax.fori_loop(0, out.shape[0], place, 0)


def attend(tab, inv, kb, vb, q, dc, wk, wv):
    width = wk.shape[0]
    same = jax.ShapeDtypeStruct(q.shape, BF16)
    flat = pltpu.HBM(kb.shape, BF16)
    return pl.pallas_call(
        attend_kernel,
        in_specs=[SMEM, SMEM] + [VMEM] * 6,
        out_specs=[VMEM] * 5,
        out_shape=[same, same, flat, flat, pltpu.HBM((inv.shape[0], NLEN, width), BF16)],
        scratch_shapes=[pltpu.VMEM((2 * KMAX, NLEN, width), BF16)],
        cost_estimate=cost(2048 * 896 * 1024, 40 << 20),
        compiler_params=pltpu.CompilerParams(vmem_limit_bytes=34 << 20),
        name="attend",
    )(tab, inv, kb, vb, q, dc, wk, wv)


def finish_kernel(n_ref, x, hid, dout, gain, rstd, stat, w, out, dhid, oa, na):
    step = pl.program_id(0)
    tokens = hid.shape[0]
    wq = w[:, :128].reshape(1024, 512)
    wo = w[:, 128:].reshape(1024, 512)
    o_part = dot(x[0, :tokens], wo, NT)
    n_part = dot(x[0, tokens : 2 * tokens], wq, NT)

    @pl.when(step == 0)
    def _():
        oa[...] = o_part
        na[...] = n_part

    @pl.when((step > 0) & (step < 3))
    def _():
        oa[...] += o_part
        na[...] += n_part

    @pl.when(step == 3)
    def _():
        own = hid[...].astype(F32)
        scale = rstd[...]
        out[...] = (own + (oa[...] + o_part)).astype(BF16)
        scaled = gain[...].astype(F32) * (na[...] + n_part)
        grad = dout[...].astype(F32) + scale * scaled - own * (scale * scale * scale) * stat[...]
        dhid[...] = grad.astype(BF16)


def finish(n, x, hidden, dout, gain, rstd, stat, weights):
    tokens, feats = hidden.shape
    whole = pl.BlockSpec((tokens, feats), lambda r, n: (0, 0))
    column = pl.BlockSpec((tokens, 1), lambda r, n: (0, 0))
    return pl.pallas_call(
        finish_kernel,
        grid_spec=pltpu.PrefetchScalarGridSpec(
            num_scalar_prefetch=1,
            grid=(4,),
            in_specs=[
                pl.BlockSpec((1, x.shape[1], 512), lambda r, n: (r, 0, 0)),
                whole,
                whole,
                pl.BlockSpec((1, feats), lambda r, n: (0, 0)),
                column,
                column,
                pl.BlockSpec((8, 256, 512), lambda r, n: ((n[0] + r) % 4, 0, 0)),
            ],
            out_specs=[whole, whole],
            scratch_shapes=[pltpu.VMEM((tokens, feats), F32)] * 2,
        ),
        out_shape=[jax.ShapeDtypeStruct((tokens, feats), BF16)] * 2,
        cost_estimate=cost(2 * tokens * 4096 * 512, 12 << 20),
        compiler_params=pltpu.CompilerParams(vmem_limit_bytes=24 << 20),
        name="finish",
    )(n, x, hidden, dout, gain[None], rstd, stat, weights)


def outer_kernel(at, d, ctx, a0, a1, a2, a3, b0, b1, b2, b3):
    n, x, z = at[0], at[1], at[2]
    upper, lower = (a0, a1, a2, a3), (b0, b1, b2, b3)
    half = a0.shape[1]
    for i in range(4):
        block = lax.rem(x + i + 4 - n, 4)
        for j in range(4):
            first = pl.multiple_of(lax.rem(z + j, 4) * 2 * half, 2 * half)
            part = dot(d[block, :, pl.ds(first, 2 * half)], ctx[...], TN).astype(BF16)
            upper[i][j] = part[:half]
            lower[j][i] = part[half:]


def outer(at, dout, ctx):
    share = jax.ShapeDtypeStruct((4, 128, ctx.shape[1]), BF16)
    return pl.pallas_call(
        outer_kernel,
        in_specs=[SMEM, VMEM, VMEM],
        out_specs=[VMEM] * 8,
        out_shape=[share] * 8,
        cost_estimate=cost(ctx.shape[0] * 4096 * 512, 6 << 20),
        compiler_params=pltpu.CompilerParams(vmem_limit_bytes=24 << 20),
        name="outer",
    )(at, dout, ctx)


def along_x(share, by):
    return lax.ppermute(share, "seq", [(i, (i // 4 + by) % 4 * 4 + i % 4) for i in range(16)])


def along_z(share, by):
    return lax.ppermute(share, "seq", [(i, i // 4 * 4 + (i + by) % 4) for i in range(16)])


def slot_tables(slot_span, n):
    slots = slot_span.shape[0]
    ids = jnp.arange(slots, dtype=jnp.int32)
    before = ids[None, :] < ids[:, None]
    same = slot_span[None, :] == slot_span[:, None]
    rank = jnp.sum(same & before, axis=1, dtype=jnp.int32)
    where = jnp.where(slot_span >= 0, slot_span * KMAX + rank, -1).astype(jnp.int32)
    spot = jnp.arange(2 * KMAX, dtype=jnp.int32)
    hit = where[None, :] == spot[:, None]
    relative = (ids + slots - 6 * n) % slots
    source = jnp.sum(jnp.where(hit, relative[None, :] + 1, 0), axis=1, dtype=jnp.int32) - 1
    counts = jnp.sum(slot_span[None, :] == jnp.arange(2)[:, None], axis=1, dtype=jnp.int32)
    return jnp.concatenate([source, counts]), where


def body(hidden, d_out, nbr_emb, slot_span, dec_gain, enc_gain, w_cond, w_enc, w_q, w_k, w_v, w_o):
    n = lax.axis_index("nbr")
    b = lax.axis_index("batch")
    n1 = n.astype(jnp.int32).reshape(1)
    tokens, feats = hidden.shape
    spans = tokens // CLEN

    q_half = lax.dynamic_slice_in_dim(w_q, b * 128, 128, axis=0)
    o_half = lax.dynamic_slice_in_dim(w_o, b * 128, 128, axis=1).T
    kv_half = jnp.where(b == 0, w_k, w_v)
    swap = [
        ((4 * i + j) * 4 + k, (4 * k + j) * 4 + i)
        for i in range(4)
        for j in range(4)
        for k in range(4)
    ]
    qo_half = lax.ppermute(jnp.concatenate([q_half, o_half], axis=0), ("seq", "nbr"), swap)
    weights = lax.all_gather(
        jnp.concatenate([qo_half, kv_half], axis=0), ("seq", "batch"), axis=0
    )

    hf = hidden.astype(F32)
    pooled = jnp.mean(hf.reshape(spans, CLEN, feats), axis=1).astype(BF16)
    squares = jnp.sum(hf * hf, axis=-1)
    length = lax.axis_size("seq")
    carried = lax.ppermute(
        pooled[spans - 1 :], "seq", [(i, i + 1) for i in range(length - 1)]
    )
    previous = jnp.concatenate([carried, pooled[: spans - 1]], axis=0)
    width = nbr_emb.shape[2]
    small = jnp.concatenate(
        [
            jnp.dot(previous, w_cond, preferred_element_type=F32),
            jnp.pad(squares, (0, width - tokens))[None],
        ],
        axis=0,
    )
    small = sum_small(small)
    condition = small[:spans]
    rstd = lax.rsqrt(small[spans, :tokens] / (4 * feats) + 1e-06)[:, None]
    normed = (hf * rstd * dec_gain.astype(F32)).astype(BF16)

    nbr_emb = lax.optimization_barrier((nbr_emb, condition))[0]
    e1, e2a, e2b, e3 = ring_gather(nbr_emb)
    later = lax.optimization_barrier((d_out, e1, e3))[0]
    d2, d1, d3 = (shift(later, r) for r in (2, -1, 1))
    dout_rel = jnp.stack([d_out, d1, d2, d3])

    tab, inv = slot_tables(slot_span, n)
    rel_span = jnp.roll(slot_span.reshape(4, 6), -n, axis=0).reshape(-1)

    def encode(block, first):
        own = lax.slice_in_dim(rel_span, first, first + block.shape[0])
        own = own[:, None, None]
        cond = jnp.where(own == 0, condition[0], jnp.where(own == 1, condition[1], 0.0))
        x = block.astype(F32) + cond
        enc_normed = (x * rms_scale(x) * enc_gain.astype(F32)).astype(BF16)
        width = x.shape[2]
        mixed = jnp.dot(
            enc_normed.reshape(-1, width), w_enc, preferred_element_type=F32
        ).reshape(x.shape)
        return (x + jax.nn.silu(mixed)).astype(BF16)


    pairs = weights.reshape(16, 2, 312, 512)
    weights = pltpu.with_memory_space_constraint(weights, pltpu.HBM)
    wk = pairs[:, 0, 256:].reshape(-1, 512)
    wv = pairs[:, 1, 256:].reshape(-1, 512)

    normed, dout_rel = lax.optimization_barrier((normed, dout_rel))
    shares = scattered(project(n1, normed, d_out, weights))
    both = total(shares).astype(BF16)
    query, d_ctx = both[:tokens], both[tokens:]
    e2 = jnp.concatenate([e2a, e2b], axis=0)
    encoded = [encode(nbr_emb, 0), encode(e1, 6), encode(e2, 12), encode(e3, 18)]
    enc, keys, values = keys_values(tab, encoded, wk, wv)
    ctx, d_query, d_key, d_value, parts = attend(
        tab, inv, keys, values, query, d_ctx, wk, wv
    )
    d_enc = lax.psum_scatter(parts, "nbr", scatter_dimension=0, tiled=True)

    inner = jnp.sum(d_query.astype(F32) * query.astype(F32), axis=-1).astype(BF16)
    more = jnp.broadcast_to(jnp.pad(inner, (0, ctx.shape[1] - tokens))[None], (16, ctx.shape[1]))
    local = jnp.concatenate([ctx, d_query, more], axis=0)
    heads = jnp.stack([local, shift(local, -1), shift(local, 2), shift(local, 1)])
    stat = jnp.sum(heads[:, 2 * tokens, :tokens].astype(F32), axis=0)[:, None]
    stat = stat / (rstd * (4 * feats))
    out, d_hidden = finish(n1, heads, hidden, d_out, dec_gain, rstd, stat, weights)

    place = lax.axis_index("seq").astype(jnp.int32)
    at = jnp.stack([n.astype(jnp.int32), place // 4, place % 4])
    d_wo_parts = outer(at, dout_rel, ctx)
    upper = [along_x(d_wo_parts[i], i) for i in (2, 1, 3)]
    lower = [along_z(d_wo_parts[4 + i], i) for i in (2, 1, 3)]
    upper = total([d_wo_parts[0]] + upper).astype(BF16)
    lower = total([d_wo_parts[4]] + lower).astype(BF16)
    upper = total([upper[0]] + [along_z(upper[i], i) for i in (2, 1, 3)])
    lower = total([lower[0]] + [along_x(lower[i], i) for i in (2, 1, 3)])
    d_wo = jnp.concatenate([upper, lower], axis=0).T

    rows = enc.reshape(-1, enc.shape[2])
    d_wk_part = dot(rows, d_key, TN).astype(BF16).reshape(16, -1, 512)
    d_wv_part = dot(rows, d_value, TN).astype(BF16).reshape(16, -1, 512)
    d_wkv_parts = jnp.concatenate([d_wk_part, d_wv_part], axis=1)
    d_wkv = jnp.sum(exchange(d_wkv_parts).astype(F32), axis=0)
    d_wk, d_wv = d_wkv[:56], d_wkv[56:]

    return (out, d_hidden, d_enc, d_wo, d_wk, d_wv)


def solution(mesh):
    placed = (
        P(("batch", "seq"), "nbr"),
        P(("batch", "seq"), "nbr"),
        P(("batch", "seq", "nbr"), None, None),
        P(("batch", "seq")),
        P("nbr"),
        P(),
        P("nbr", None),
        P(),
        P("seq", "nbr"),
        P("seq", "nbr"),
        P("seq", "nbr"),
        P("nbr", "seq"),
    )
    return jax.shard_map(
        body,
        mesh=mesh,
        in_specs=placed,
        out_specs=(
            P(("batch", "seq"), "nbr"),
            P(("batch", "seq"), "nbr"),
            P(("batch", "seq", "nbr"), None, None),
            P(("batch", "nbr"), "seq"),
            P(("batch", "seq"), "nbr"),
            P(("batch", "seq"), "nbr"),
        ),
        check_vma=False,
    )
```

time: 231 us -> 237 us (1.026)
  starting transfers between devices: 57.9 us -> 71 us
  waiting for transfers between devices: 65.6 us -> 54.3 us
  other arithmetic: 13.6 us -> 19.6 us
  local copies, waits for them, and re-layouts: 15.1 us -> 11.8 us
  matrix products: 19.8 us -> 22.8 us
    ppermute x6, waiting for transfers between devices: 2.44 us -> 22.7 us  [along_x(): lax.ppermute(share, 'seq', [(i, (i // 4 + by) % 4 * 4 + i % 4) for i in r...]
    ppermute x17 -> x16, waiting for transfers between devices: 47.5 us -> 31.1 us  [shift(): return lax.ppermute(x, 'nbr', [(i, (i + by) % n) for i in range(n)])]
    ppermute x6, waiting for transfers between devices: 14.9 us -> 0.02 us  [along_z(): lax.ppermute(share, 'seq', [(i, i // 4 * 4 + (i + by) % 4) for i in range...]
    ppermute x17 -> x16, starting transfers between devices: 23.6 us -> 33.7 us  [shift(): return lax.ppermute(x, 'nbr', [(i, (i + by) % n) for i in range(n)])]
    slice x8 -> x1, local copies, waits for them, and re-layouts: 4.43 us -> 0.02 us  [body(): query, d_ctx = (both[:tokens], both[tokens:])]
    ppermute x6, starting transfers between devices: 15.4 us -> 11.5 us  [along_x(): lax.ppermute(share, 'seq', [(i, (i // 4 + by) % 4 * 4 + i % 4) for i in r...]
    dot_general x4, matrix products: 11.6 us -> 15.4 us  [encode(): jnp.dot(enc_normed.reshape(-1, width), w_enc, preferred_element_type=F32)]
    ppermute x0 -> x1, starting transfers between devices: none -> 3.58 us  [body(): lax.ppermute(jnp.concatenate([q_half, o_half], axis=0), ('seq', 'nbr'), s...]
  transfers between devices with their start and end apart: 33 -> 33, of which waited for: 13 -> 9; matrix products, arithmetic and copies ran while one was open for 18% -> 19% of each run, Pallas kernels for 10% -> 8%
where the time goes in v1:
time: 237 us; the launch traced here: 235 us
  starting transfers between devices  71 us (30%)
  waiting for transfers between devices  54.3 us (23%)
  Pallas kernels  40.6 us (17%)
  matrix products  22.8 us (10%)
  other arithmetic  19.6 us (8%)
  between operations  14.6 us (6%)
  local copies, waits for them, and re-layouts  11.8 us (5%)
    ppermute x16, starting transfers between devices, shift(): return lax.ppermute(x, 'nbr', [(i, (i + by) % n) for i in range(n)])  33.7 us
    ppermute x16, waiting for transfers between devices, shift(): return lax.ppermute(x, 'nbr', [(i, (i + by) % n) for i in range(n)])  31.1 us
    ppermute x6, waiting for transfers between devices, along_x(): lax.ppermute(share, 'seq', [(i, (i // 4 + by) % 4 * 4 + i % 4) for i in r...  22.7 us
    pallas_call x1, Pallas kernels, attend(): pl.pallas_call(attend_kernel, in_specs=[SMEM, SMEM] + [VMEM] * 6, out_spe...  17.5 us
    dot_general x4, matrix products, encode(): jnp.dot(enc_normed.reshape(-1, width), w_enc, preferred_element_type=F32)  15.4 us
    ppermute x6, starting transfers between devices, along_z(): lax.ppermute(share, 'seq', [(i, i // 4 * 4 + (i + by) % 4) for i in range...  12.6 us
    ppermute x6, starting transfers between devices, along_x(): lax.ppermute(share, 'seq', [(i, (i // 4 + by) % 4 * 4 + i % 4) for i in r...  11.5 us
    pallas_call x1, Pallas kernels, keys_values(): pl.pallas_call(keys_kernel, in_specs=[SMEM] + [VMEM] * 6, out_specs=[VMEM...  8.07 us
  transfers between devices with their start and end apart: 33, of which 9 were waited for; matrix products, arithmetic and copies ran while one was open for 19% of the time, Pallas kernels for 8%

profile of v1, /device:TPU:0, one launch (start us, length us, event | category | flops | bytes accessed | tf_op | source)
XLA Modules:
  0.0 234.6 jit_solution(12351505045642600963)
XLA Ops:
  7.3 1.7 constant_dynamic-slice_fusion
  9.0 1.7 copy.44
  11.6 1.6 pad_maximum_fusion.7
  13.2 3.6 %collective-permute-start.8 = (bf16[256,512]{1,0:T(8,128)(2,1)}, bf16[256,512]{1,0:T(8,128)(2,1)}, u32[]{:S(2)}, u32[]{:S(2)}) collective-permute-start(bf16[256,512]{1,0:T(8,128)(2,1)} %pad_maximum_fusion.7), channel_id=1, source_target_pairs={{0,0},{2,32},{4,64},{6,96},{8,8},{10,40},{12,72},{14,104},{16,16},... | collective-permute-start | bytes 786440 | tf_op jit(solution)/shard_map/ppermute | solution.py:322
  17.6 1.7 pad_maximum_fusion.5
  19.4 17.9 %collective-permute-start.4 = (bf16[6,128,896]{2,1,0:T(8,128)(2,1)}, bf16[6,128,896]{2,1,0:T(8,128)(2,1)}, u32[]{:S(2)}, u32[]{:S(2)}) collective-permute-start(bf16[6,128,896]{2,1,0:T(8,128)(2,1)} %param.14), channel_id=1, source_target_pairs={{0,6},{2,0},{4,2},{6,4},{1,7},{3,1},{5,3},{7,5},{8,14},{10,8},{12,... | collective-permute-start | bytes 4128776 | tf_op jit(solution)/shard_map/ppermute | solution.py:28
  38.4 3.8 %collective-permute-start = (bf16[1,1024]{1,0:T(2,128)(2,1)S(1)}, bf16[1,1024]{1,0:T(2,128)(2,1)S(1)}, u32[]{:S(2)}, u32[]{:S(2)}) collective-permute-start(bf16[1,1024]{1,0:T(2,128)(2,1)S(1)} %get-tuple-element.97), channel_id=1, source_target_pairs={{0,8},{8,16},{16,24},{24,32},{32,40},{40,48},{48,56},{56,64},{64,7... | collective-permute-start | bytes 6152 | tf_op jit(solution)/shard_map/ppermute | solution.py:331
  44.0 4.7 %collective-permute-start.2 = (f32[3,896]{1,0:T(4,128)S(1)}, f32[3,896]{1,0:T(4,128)S(1)}, u32[]{:S(2)}, u32[]{:S(2)}) collective-permute-start(f32[3,896]{1,0:T(4,128)S(1)} %pad_maximum_fusion.8), channel_id=1, source_target_pairs={{0,4},{2,6},{4,0},{6,2},{1,5},{3,7},{5,1},{7,3},{8,12},{10,14},{12... | collective-permute-start | bytes 32264 | tf_op jit(solution)/shard_map/ppermute | solution.py:28
  48.8 21.9 %collective-permute-done.1 = f32[3,896]{1,0:T(4,128)S(1)} collective-permute-done((f32[3,896]{1,0:T(4,128)S(1)}, f32[3,896]{1,0:T(4,128)S(1)}, u32[]{:S(2)}, u32[]{:S(2)}) %collective-permute-start.1) | collective-permute-done | bytes 10784 | tf_op jit(solution)/shard_map/ppermute | solution.py:28
  71.5 2.1 add_convert_fusion.3.e0
  75.7 1.2 slice.137
  76.8 2.7 %collective-permute-start.5 = (bf16[3,128,896]{2,1,0:T(8,128)(2,1)S(1)}, bf16[3,128,896]{2,1,0:T(8,128)(2,1)S(1)}, u32[]{:S(2)}, u32[]{:S(2)}) collective-permute-start(bf16[3,128,896]{2,1,0:T(8,128)(2,1)S(1)} %slice.137), channel_id=1, source_target_pairs={{0,6},{2,0},{4,2},{6,4},{1,7},{3,1},{5,3},{7,5},{8,14},{10,8},{12,... | collective-permute-start | bytes 2064392 | tf_op jit(solution)/shard_map/ppermute | solution.py:28
  79.6 1.2 slice.138
  81.0 1.8 multiply_reduce_fusion
  82.8 1.8 multiply_reduce_fusion.2
  84.6 5.1 %add_convert_fusion.e3 = bf16[6,128,896]{2,1,0:T(8,128)(2,1)} fusion(bf16[6,128,896]{2,1,0:T(8,128)(2,1)} %collective-permute-done.6, bf16[896,896]{1,0:T(8,128)(2,1)S(1)} %copy-done.14, f32[6,128]{1,0:T(8,128)S(1)} %add_rsqrt_fusion, f32[6,896]{1,0:T(8,128)S(1)} %get-tuple-element.93, f32[896]{0:T(1024)S(1)} %convert_element_type.173), kind=kOutput, calls=%fused_computation.1 | convolution fusion | flops 1242071040 | bytes 4386304 | tf_op jit(solution)/shard_map/dot_general | solution.py:364
  89.7 5.0 %add_convert_fusion.2.e1 = bf16[6,128,896]{2,1,0:T(8,128)(2,1)} fusion(bf16[6,128,896]{2,1,0:T(8,128)(2,1)} %collective-permute-done.4, bf16[896,896]{1,0:T(8,128)(2,1)S(1)} %copy-done.14, f32[6,128]{1,0:T(8,128)S(1)} %add_rsqrt_fusion.2, f32[6,896]{1,0:T(8,128)S(1)} %get-tuple-element.94, f32[896]{0:T(1024)S(1)} %convert_element_type.173), kind=kOutput, calls=%fused_computation.9 | convolution fusion | flops 1242071040 | bytes 4386304 | tf_op jit(solution)/shard_map/dot_general | solution.py:364
  94.8 5.7 %collective-permute-done.5 = bf16[3,128,896]{2,1,0:T(8,128)(2,1)S(1)} collective-permute-done((bf16[3,128,896]{2,1,0:T(8,128)(2,1)S(1)}, bf16[3,128,896]{2,1,0:T(8,128)(2,1)S(1)}, u32[]{:S(2)}, u32[]{:S(2)}) %collective-permute-start.5) | collective-permute-done | bytes 688160 | tf_op jit(solution)/shard_map/ppermute | solution.py:28
  100.5 1.9 collective-permute-done.7
  102.9 3.2 %add_convert_fusion.1.e2 = bf16[6,128,896]{2,1,0:T(8,128)(2,1)} fusion(bf16[896,896]{1,0:T(8,128)(2,1)S(1)} %copy-done.14, f32[6,128]{1,0:T(8,128)S(1)} %add_rsqrt_fusion.1, f32[6,896]{1,0:T(8,128)S(1)} %get-tuple-element.95, f32[896]{0:T(1024)S(1)} %convert_element_type.173, bf16[3,128,896]{2,1,0:T(8,128)(2,1)S(1)} %collective-permute-done.7, ...), kind=kOutput, calls=%fused_computation.5 | convolution fusion | flops 1243447296 | bytes 4386304 | tf_op jit(solution)/shard_map/dot_general | solution.py:364
  106.1 4.9 %project.1 = bf16[4,256,512]{2,1,0:T(8,128)(2,1)S(1)} custom-call(s32[1]{0:T(128)} %bitcast.n_ref, bf16[128,1024]{1,0:T(8,128)(2,1)S(1)} %multiply_convert_fusion.16.x, bf16[128,1024]{1,0:T(8,128)(2,1)S(1)} %copy-done.3, bf16[32,312,512]{2,1,0:T(8,128)(2,1)} %bitcast.105), custom_call_target="tpu_custom_call" | custom-call | flops 1073741824 | bytes 12582912 | tf_op jit(solution)/shard_map/project/pallas_call | solution.py:74
  112.6 2.4 %collective-permute-start.14 = (bf16[256,512]{1,0:T(8,128)(2,1)S(1)}, bf16[256,512]{1,0:T(8,128)(2,1)S(1)}, u32[]{:S(2)}, u32[]{:S(2)}) collective-permute-start(bf16[256,512]{1,0:T(8,128)(2,1)S(1)} %get-tuple-element.77), channel_id=1, source_target_pairs={{0,6},{2,0},{4,2},{6,4},{1,7},{3,1},{5,3},{7,5},{8,14},{10,8},{12,... | collective-permute-start | bytes 786440 | tf_op jit(solution)/shard_map/ppermute | solution.py:28
  115.0 1.6 fusion.50
  116.6 8.1 %keys_values.1 = (bf16[16,128,896]{2,1,0:T(8,128)(2,1)}, bf16[2048,512]{1,0:T(8,128)(2,1)S(1)}, bf16[2048,512]{1,0:T(8,128)(2,1)S(1)}) custom-call(s32[18]{0:T(128)S(1)} %pad_add_fusion.1.tab, bf16[6,128,896]{2,1,0:T(8,128)(2,1)S(1)} %add_convert_fusion.3.e0, bf16[6,128,896]{2,1,0:T(8,128)(2,1)S(1)} %copy-done.7, bf16[6,128,896]{2,1,0:T(8,128)(2,1)S(1)} %copy-done.8, ...), custom_call_target="tpu_custom_call" | custom-call | flops 3758096384 | bytes 16777216 | tf_op jit(solution)/shard_map/keys_values/pallas_call | solution.py:126
  124.7 1.5 collective-permute-done.13
  126.4 17.5 %attend.1 = (bf16[128,512]{1,0:T(8,128)(2,1)S(1)}, bf16[128,512]{1,0:T(8,128)(2,1)S(1)}, bf16[2048,512]{1,0:T(8,128)(2,1)}, bf16[2048,512]{1,0:T(8,128)(2,1)}, bf16[24,128,896]{2,1,0:T(8,128)(2,1)}) custom-call(s32[18]{0:T(128)S(1)} %pad_add_fusion.1.tab, s32[24]{0:T(128)S(1)} %get-tuple-element.107.inv, bf16[2048,512]{1,0:T(8,128)(2,1)S(1)} %get-tuple-element.27.kb, ...), custom_call_target="tpu_custom_call" | custom-call | flops 3758096384 | bytes 41943040 | tf_op jit(solution)/shard_map/attend/pallas_call | solution.py:189
  147.1 4.9 %convolution_convert_fusion.1 = bf16[896,512]{1,0:T(8,128)(2,1)S(1)} fusion(bf16[2048,896]{1,0:T(8,128)(2,1)} %bitcast.115, bf16[2048,512]{1,0:T(8,128)(2,1)} %get-tuple-element.46), kind=kOutput, calls=%fused_computation.27 | convolution fusion | flops 1879506944 | bytes 6684672 | tf_op jit(solution)/shard_map/dot_general | solution.py:19
  152.5 2.1 convolution_convert_fusion
  154.6 1.5 pad_maximum_fusion
  156.1 5.7 %all-to-all-start = ((bf16[16,112,512]{2,1,0:T(8,128)(2,1)}), bf16[16,112,512]{2,1,0:T(8,128)(2,1)}, u32[]{:S(2)}, u32[]{:S(2)}) async-start(bf16[16,112,512]{2,1,0:T(8,128)(2,1)} %pad_maximum_fusion), calls=%async_computation.1 | async-start | bytes 3670016 | tf_op jit(solution)/shard_map/all_to_all | solution.py:53
  161.7 2.9 %outer.1 = (bf16[4,128,512]{2,1,0:T(8,128)(2,1)S(1)}, bf16[4,128,512]{2,1,0:T(8,128)(2,1)}, bf16[4,128,512]{2,1,0:T(8,128)(2,1)}, bf16[4,128,512]{2,1,0:T(8,128)...) custom-call(s32[3]{0:T(128)S(1)} %pad_add_fusion.2.at, ...), custom_call_target="tpu_custom_call" | custom-call | flops 536870912 | bytes 6291456 | tf_op jit(solution)/shard_map/outer/pallas_call | solution.py:272
  165.5 3.4 %collective-permute-start.18 = (bf16[4,128,512]{2,1,0:T(8,128)(2,1)}, bf16[4,128,512]{2,1,0:T(8,128)(2,1)}, u32[]{:S(2)}, u32[]{:S(2)}) collective-permute-start(bf16[4,128,512]{2,1,0:T(8,128)(2,1)} %get-tuple-element.38), channel_id=1, source_target_pairs={{0,64},{8,72},{16,80},{24,88},{32,96},{40,104},{48,112},{56,120},{... | collective-permute-start | bytes 1572872 | tf_op jit(solution)/shard_map/ppermute | solution.py:284
  169.4 2.7 %collective-permute-start.20 = (bf16[4,128,512]{2,1,0:T(8,128)(2,1)}, bf16[4,128,512]{2,1,0:T(8,128)(2,1)}, u32[]{:S(2)}, u32[]{:S(2)}) collective-permute-start(bf16[4,128,512]{2,1,0:T(8,128)(2,1)} %get-tuple-element.40), channel_id=1, source_target_pairs={{0,96},{8,104},{16,112},{24,120},{32,0},{40,8},{48,16},{56,24},{64... | collective-permute-start | bytes 1572872 | tf_op jit(solution)/shard_map/ppermute | solution.py:284
  172.1 3.0 %collective-permute-start.24 = (bf16[4,128,512]{2,1,0:T(8,128)(2,1)}, bf16[4,128,512]{2,1,0:T(8,128)(2,1)}, u32[]{:S(2)}, u32[]{:S(2)}) collective-permute-start(bf16[4,128,512]{2,1,0:T(8,128)(2,1)} %get-tuple-element.42), channel_id=1, source_target_pairs={{0,16},{8,24},{16,0},{24,8},{32,48},{40,56},{48,32},{56,40},{64,80... | collective-permute-start | bytes 1572872 | tf_op jit(solution)/shard_map/ppermute | solution.py:288
  175.6 1.3 pad_maximum_fusion.2.x
  177.1 7.2 %finish.1 = (bf16[128,1024]{1,0:T(8,128)(2,1)}, bf16[128,1024]{1,0:T(8,128)(2,1)}) custom-call(s32[1]{0:T(128)} %bitcast.n_ref, bf16[4,272,512]{2,1,0:T(8,128)(2,1)S(1)} %pad_maximum_fusion.2.x, bf16[128,1024]{1,0:T(8,128)(2,1)S(1)} %copy-done.2, bf16[128,1024]{1,0:T(8,128)(2,1)S(1)} %copy-done.3, bf16[1,1024]{1,0:T(2,128)(2,1)S(1)} %broadcast_in_dim.141.gain, ...), custom_call_target="tpu_custom_call" | custom-call | flops 1073741824 | bytes 12582912 | tf_op jit(solution)/shard_map/finish/pallas_call | solution.py:233
  184.3 13.7 %collective-permute-done.18 = bf16[4,128,512]{2,1,0:T(8,128)(2,1)} collective-permute-done((bf16[4,128,512]{2,1,0:T(8,128)(2,1)}, bf16[4,128,512]{2,1,0:T(8,128)(2,1)}, u32[]{:S(2)}, u32[]{:S(2)}) %collective-permute-start.18) | collective-permute-done | bytes 524320 | tf_op jit(solution)/shard_map/ppermute | solution.py:284
  197.9 2.7 %collective-permute-start.26 = (bf16[4,128,512]{2,1,0:T(8,128)(2,1)S(1)}, bf16[4,128,512]{2,1,0:T(8,128)(2,1)S(1)}, u32[]{:S(2)}, u32[]{:S(2)}) collective-permute-start(bf16[4,128,512]{2,1,0:T(8,128)(2,1)S(1)} %copy-done.5), channel_id=1, source_target_pairs={{0,24},{8,0},{16,8},{24,16},{32,56},{40,32},{48,40},{56,48},{64,88... | collective-permute-start | bytes 1572872 | tf_op jit(solution)/shard_map/ppermute | solution.py:288
  200.7 6.0 %collective-permute-done.19 = bf16[4,128,512]{2,1,0:T(8,128)(2,1)} collective-permute-done((bf16[4,128,512]{2,1,0:T(8,128)(2,1)}, bf16[4,128,512]{2,1,0:T(8,128)(2,1)}, u32[]{:S(2)}, u32[]{:S(2)}) %collective-permute-start.19) | collective-permute-done | bytes 524320 | tf_op jit(solution)/shard_map/ppermute | solution.py:284
  206.7 1.6 add_convert_fusion.5
  208.3 3.1 %collective-permute-start.21 = (bf16[128,512]{1,0:T(8,128)(2,1)S(1)}, bf16[128,512]{1,0:T(8,128)(2,1)S(1)}, u32[]{:S(2)}, u32[]{:S(2)}) collective-permute-start(bf16[128,512]{1,0:T(8,128)(2,1)S(1)} %get-tuple-element.79), channel_id=1, source_target_pairs={{0,16},{8,24},{16,0},{24,8},{32,48},{40,56},{48,32},{56,40},{64,80... | collective-permute-start | bytes 393224 | tf_op jit(solution)/shard_map/ppermute | solution.py:288
  212.0 2.7 %collective-permute-start.23 = (bf16[128,512]{1,0:T(8,128)(2,1)S(1)}, bf16[128,512]{1,0:T(8,128)(2,1)S(1)}, u32[]{:S(2)}, u32[]{:S(2)}) collective-permute-start(bf16[128,512]{1,0:T(8,128)(2,1)S(1)} %get-tuple-element.80), channel_id=1, source_target_pairs={{0,24},{8,0},{16,8},{24,16},{32,56},{40,32},{48,40},{56,48},{64,88... | collective-permute-start | bytes 393224 | tf_op jit(solution)/shard_map/ppermute | solution.py:288
  214.7 1.5 add_convert_fusion.4
  216.2 1.7 collective-permute-start.27
  218.0 3.1 %collective-permute-start.29 = (bf16[128,512]{1,0:T(8,128)(2,1)S(1)}, bf16[128,512]{1,0:T(8,128)(2,1)S(1)}, u32[]{:S(2)}, u32[]{:S(2)}) collective-permute-start(bf16[128,512]{1,0:T(8,128)(2,1)S(1)} %get-tuple-element.83), channel_id=1, source_target_pairs={{0,96},{8,104},{16,112},{24,120},{32,0},{40,8},{48,16},{56,24},{64... | collective-permute-start | bytes 393224 | tf_op jit(solution)/shard_map/ppermute | solution.py:284
  221.2 1.6 collective-permute-done.27
  222.8 1.4 collective-permute-done.28
  225.3 1.8 convert_reduce_fusion
  (133 shorter events, 18.4 us)
Async XLA Ops:
  7.2 36.4 %copy-start = (bf16[1024,896]{1,0:T(8,128)(2,1)S(1)}, bf16[1024,896]{1,0:T(8,128)(2,1)}, u32[]{:S(2)}) copy-start(bf16[1024,896]{1,0:T(8,128)(2,1)} %param.18) | copy-start | bytes 5505028
  7.2 63.7 %copy-start.9 = (bf16[6,128,896]{2,1,0:T(8,128)(2,1)S(1)}, bf16[6,128,896]{2,1,0:T(8,128)(2,1)}, u32[]{:S(2)}) copy-start(bf16[6,128,896]{2,1,0:T(8,128)(2,1)} %param.14) | copy-start | bytes 4128772
  7.2 35.5 %copy-start.2 = (bf16[128,1024]{1,0:T(8,128)(2,1)S(1)}, bf16[128,1024]{1,0:T(8,128)(2,1)}, u32[]{:S(2)}) copy-start(bf16[128,1024]{1,0:T(8,128)(2,1)} %hid.1) | copy-start | bytes 786436
  7.2 35.0 %copy-start.13 = (s32[24]{0:T(128)S(1)}, s32[24]{0:T(128)}, u32[]{:S(2)}) copy-start(s32[24]{0:T(128)} %param.15) | copy-start | bytes 292
  7.2 41.5 %copy-start.11 = (bf16[1024]{0:T(1024)(128)(2,1)S(1)}, bf16[1024]{0:T(1024)(128)(2,1)}, u32[]{:S(2)}) copy-start(bf16[1024]{0:T(1024)(128)(2,1)} %param.16) | copy-start | bytes 6148
  7.2 41.5 %copy-start.12 = (bf16[896]{0:T(1024)(128)(2,1)S(1)}, bf16[896]{0:T(1024)(128)(2,1)}, u32[]{:S(2)}) copy-start(bf16[896]{0:T(1024)(128)(2,1)} %param.17) | copy-start | bytes 5380
  7.2 98.9 %all-gather.3.cloned.1.call-start = ((), (), s32[]{:S(2)}) async-start(), calls=%async_computation.3 | async-start | bytes 10543104 | tf_op jit(solution)/shard_map/all_gather | solution.py:323
  13.2 4.4 %collective-permute-start.8 = (bf16[256,512]{1,0:T(8,128)(2,1)}, bf16[256,512]{1,0:T(8,128)(2,1)}, u32[]{:S(2)}, u32[]{:S(2)}) collective-permute-start(bf16[256,512]{1,0:T(8,128)(2,1)} %pad_maximum_fusion.7), channel_id=1, source_target_pairs={{0,0},{2,32},{4,64},{6,96},{8,8},{10,40},{12,72},{14,104},{16,16},... | collective-permute-start | bytes 786440 | tf_op jit(solution)/shard_map/ppermute | solution.py:322
  19.4 208.4 %reduce-scatter.2.cloned.1.call-start = ((), (), s32[]{:S(2)}) async-start(), calls=%async_computation.2 | async-start | bytes 6881280 | tf_op jit(solution)/shard_map/reduce_scatter | solution.py:385
  19.4 54.2 %collective-permute-start.4 = (bf16[6,128,896]{2,1,0:T(8,128)(2,1)}, bf16[6,128,896]{2,1,0:T(8,128)(2,1)}, u32[]{:S(2)}, u32[]{:S(2)}) collective-permute-start(bf16[6,128,896]{2,1,0:T(8,128)(2,1)} %param.14), channel_id=1, source_target_pairs={{0,6},{2,0},{4,2},{6,4},{1,7},{3,1},{5,3},{7,5},{8,14},{10,8},{12,... | collective-permute-start | bytes 4128776 | tf_op jit(solution)/shard_map/ppermute | solution.py:28
  37.3 36.2 %collective-permute-start.6 = (bf16[6,128,896]{2,1,0:T(8,128)(2,1)}, bf16[6,128,896]{2,1,0:T(8,128)(2,1)}, u32[]{:S(2)}, u32[]{:S(2)}) collective-permute-start(bf16[6,128,896]{2,1,0:T(8,128)(2,1)} %param.14), channel_id=1, source_target_pairs={{0,2},{2,4},{4,6},{6,0},{1,3},{3,5},{5,7},{7,1},{8,10},{10,12},{12... | collective-permute-start | bytes 4128776 | tf_op jit(solution)/shard_map/ppermute | solution.py:28
  38.4 5.1 %collective-permute-start = (bf16[1,1024]{1,0:T(2,128)(2,1)S(1)}, bf16[1,1024]{1,0:T(2,128)(2,1)S(1)}, u32[]{:S(2)}, u32[]{:S(2)}) collective-permute-start(bf16[1,1024]{1,0:T(2,128)(2,1)S(1)} %get-tuple-element.97), channel_id=1, source_target_pairs={{0,8},{8,16},{16,24},{24,32},{32,40},{40,48},{48,56},{56,64},{64,7... | collective-permute-start | bytes 6152 | tf_op jit(solution)/shard_map/ppermute | solution.py:331
  42.3 29.1 %copy-start.10 = (bf16[6,128,896]{2,1,0:T(8,128)(2,1)S(1)}, bf16[6,128,896]{2,1,0:T(8,128)(2,1)}, u32[]{:S(2)}) copy-start(bf16[6,128,896]{2,1,0:T(8,128)(2,1)} %param.14) | copy-start | bytes 4128772
  42.3 29.1 %copy-start.14 = (bf16[896,896]{1,0:T(8,128)(2,1)S(1)}, bf16[896,896]{1,0:T(8,128)(2,1)}, u32[]{:S(2)}) copy-start(bf16[896,896]{1,0:T(8,128)(2,1)} %param.19) | copy-start | bytes 4816900
  43.9 26.8 %collective-permute-start.1 = (f32[3,896]{1,0:T(4,128)S(1)}, f32[3,896]{1,0:T(4,128)S(1)}, u32[]{:S(2)}, u32[]{:S(2)}) collective-permute-start(f32[3,896]{1,0:T(4,128)S(1)} %pad_maximum_fusion.8), channel_id=1, source_target_pairs={{0,2},{2,4},{4,6},{6,0},{1,3},{3,5},{5,7},{7,1},{8,10},{10,12},{12... | collective-permute-start | bytes 32264 | tf_op jit(solution)/shard_map/ppermute | solution.py:28
  44.0 26.7 %collective-permute-start.2 = (f32[3,896]{1,0:T(4,128)S(1)}, f32[3,896]{1,0:T(4,128)S(1)}, u32[]{:S(2)}, u32[]{:S(2)}) collective-permute-start(f32[3,896]{1,0:T(4,128)S(1)} %pad_maximum_fusion.8), channel_id=1, source_target_pairs={{0,4},{2,6},{4,0},{6,2},{1,5},{3,7},{5,1},{7,3},{8,12},{10,14},{12... | collective-permute-start | bytes 32264 | tf_op jit(solution)/shard_map/ppermute | solution.py:28
  48.7 22.0 %collective-permute-start.3 = (f32[3,896]{1,0:T(4,128)S(1)}, f32[3,896]{1,0:T(4,128)S(1)}, u32[]{:S(2)}, u32[]{:S(2)}) collective-permute-start(f32[3,896]{1,0:T(4,128)S(1)} %pad_maximum_fusion.8), channel_id=1, source_target_pairs={{0,6},{2,0},{4,2},{6,4},{1,7},{3,1},{5,3},{7,5},{8,14},{10,8},{12,... | collective-permute-start | bytes 32264 | tf_op jit(solution)/shard_map/ppermute | solution.py:28
  73.6 21.1 %collective-permute-start.9 = (bf16[128,1024]{1,0:T(8,128)(2,1)S(1)}, bf16[128,1024]{1,0:T(8,128)(2,1)S(1)}, u32[]{:S(2)}, u32[]{:S(2)}) collective-permute-start(bf16[128,1024]{1,0:T(8,128)(2,1)S(1)} %copy-done.3), channel_id=1, source_target_pairs={{0,6},{2,0},{4,2},{6,4},{1,7},{3,1},{5,3},{7,5},{8,14},{10,8},{12,... | collective-permute-start | bytes 786440 | tf_op jit(solution)/shard_map/ppermute | solution.py:28
  73.9 20.8 %collective-permute-start.10 = (bf16[128,1024]{1,0:T(8,128)(2,1)S(1)}, bf16[128,1024]{1,0:T(8,128)(2,1)S(1)}, u32[]{:S(2)}, u32[]{:S(2)}) collective-permute-start(bf16[128,1024]{1,0:T(8,128)(2,1)S(1)} %copy-done.3), channel_id=1, source_target_pairs={{0,4},{2,6},{4,0},{6,2},{1,5},{3,7},{5,1},{7,3},{8,12},{10,14},{12... | collective-permute-start | bytes 786440 | tf_op jit(solution)/shard_map/ppermute | solution.py:28
  74.7 20.0 %collective-permute-start.11 = (bf16[128,1024]{1,0:T(8,128)(2,1)S(1)}, bf16[128,1024]{1,0:T(8,128)(2,1)S(1)}, u32[]{:S(2)}, u32[]{:S(2)}) collective-permute-start(bf16[128,1024]{1,0:T(8,128)(2,1)S(1)} %copy-done.3), channel_id=1, source_target_pairs={{0,2},{2,4},{4,6},{6,0},{1,3},{3,5},{5,7},{7,1},{8,10},{10,12},{12... | collective-permute-start | bytes 786440 | tf_op jit(solution)/shard_map/ppermute | solution.py:28
  76.8 23.7 %collective-permute-start.5 = (bf16[3,128,896]{2,1,0:T(8,128)(2,1)S(1)}, bf16[3,128,896]{2,1,0:T(8,128)(2,1)S(1)}, u32[]{:S(2)}, u32[]{:S(2)}) collective-permute-start(bf16[3,128,896]{2,1,0:T(8,128)(2,1)S(1)} %slice.137), channel_id=1, source_target_pairs={{0,6},{2,0},{4,2},{6,4},{1,7},{3,1},{5,3},{7,5},{8,14},{10,8},{12,... | collective-permute-start | bytes 2064392 | tf_op jit(solution)/shard_map/ppermute | solution.py:28
  80.8 21.7 %collective-permute-start.7 = (bf16[3,128,896]{2,1,0:T(8,128)(2,1)S(1)}, bf16[3,128,896]{2,1,0:T(8,128)(2,1)S(1)}, u32[]{:S(2)}, u32[]{:S(2)}) collective-permute-start(bf16[3,128,896]{2,1,0:T(8,128)(2,1)S(1)} %slice.138), channel_id=1, source_target_pairs={{0,2},{2,4},{4,6},{6,0},{1,3},{3,5},{5,7},{7,1},{8,10},{10,12},{12... | collective-permute-start | bytes 2064392 | tf_op jit(solution)/shard_map/ppermute | solution.py:28
  111.0 5.6 %copy-start.6 = (bf16[6,128,896]{2,1,0:T(8,128)(2,1)S(1)}, bf16[6,128,896]{2,1,0:T(8,128)(2,1)}, u32[]{:S(2)}) copy-start(bf16[6,128,896]{2,1,0:T(8,128)(2,1)} %add_convert_fusion.e3) | copy-start | bytes 4128772
  111.0 5.6 %copy-start.7 = (bf16[6,128,896]{2,1,0:T(8,128)(2,1)S(1)}, bf16[6,128,896]{2,1,0:T(8,128)(2,1)}, u32[]{:S(2)}) copy-start(bf16[6,128,896]{2,1,0:T(8,128)(2,1)} %add_convert_fusion.2.e1) | copy-start | bytes 4128772
  111.0 5.6 %copy-start.8 = (bf16[6,128,896]{2,1,0:T(8,128)(2,1)S(1)}, bf16[6,128,896]{2,1,0:T(8,128)(2,1)}, u32[]{:S(2)}) copy-start(bf16[6,128,896]{2,1,0:T(8,128)(2,1)} %add_convert_fusion.1.e2) | copy-start | bytes 4128772
  111.1 13.6 %collective-permute-start.12 = (bf16[256,512]{1,0:T(8,128)(2,1)S(1)}, bf16[256,512]{1,0:T(8,128)(2,1)S(1)}, u32[]{:S(2)}, u32[]{:S(2)}) collective-permute-start(bf16[256,512]{1,0:T(8,128)(2,1)S(1)} %get-tuple-element.76), channel_id=1, source_target_pairs={{0,4},{2,6},{4,0},{6,2},{1,5},{3,7},{5,1},{7,3},{8,12},{10,14},{12... | collective-permute-start | bytes 786440 | tf_op jit(solution)/shard_map/ppermute | solution.py:28
  111.8 14.4 %collective-permute-start.13 = (bf16[256,512]{1,0:T(8,128)(2,1)S(1)}, bf16[256,512]{1,0:T(8,128)(2,1)S(1)}, u32[]{:S(2)}, u32[]{:S(2)}) collective-permute-start(bf16[256,512]{1,0:T(8,128)(2,1)S(1)} %get-tuple-element.78), channel_id=1, source_target_pairs={{0,2},{2,4},{4,6},{6,0},{1,3},{3,5},{5,7},{7,1},{8,10},{10,12},{12... | collective-permute-start | bytes 786440 | tf_op jit(solution)/shard_map/ppermute | solution.py:28
  112.6 13.6 %collective-permute-start.14 = (bf16[256,512]{1,0:T(8,128)(2,1)S(1)}, bf16[256,512]{1,0:T(8,128)(2,1)S(1)}, u32[]{:S(2)}, u32[]{:S(2)}) collective-permute-start(bf16[256,512]{1,0:T(8,128)(2,1)S(1)} %get-tuple-element.77), channel_id=1, source_target_pairs={{0,6},{2,0},{4,2},{6,4},{1,7},{3,1},{5,3},{7,5},{8,14},{10,8},{12,... | collective-permute-start | bytes 786440 | tf_op jit(solution)/shard_map/ppermute | solution.py:28
  145.1 24.4 %collective-permute-start.15 = (bf16[272,512]{1,0:T(8,128)(2,1)}, bf16[272,512]{1,0:T(8,128)(2,1)}, u32[]{:S(2)}, u32[]{:S(2)}) collective-permute-start(bf16[272,512]{1,0:T(8,128)(2,1)} %get-tuple-element.86), channel_id=1, source_target_pairs={{0,6},{2,0},{4,2},{6,4},{1,7},{3,1},{5,3},{7,5},{8,14},{10,8},{12,... | collective-permute-start | bytes 835592 | tf_op jit(solution)/shard_map/ppermute | solution.py:28
  145.9 26.2 %collective-permute-start.16 = (bf16[272,512]{1,0:T(8,128)(2,1)}, bf16[272,512]{1,0:T(8,128)(2,1)}, u32[]{:S(2)}, u32[]{:S(2)}) collective-permute-start(bf16[272,512]{1,0:T(8,128)(2,1)} %get-tuple-element.86), channel_id=1, source_target_pairs={{0,4},{2,6},{4,0},{6,2},{1,5},{3,7},{5,1},{7,3},{8,12},{10,14},{12... | collective-permute-start | bytes 835592 | tf_op jit(solution)/shard_map/ppermute | solution.py:28
  146.2 28.9 %collective-permute-start.17 = (bf16[272,512]{1,0:T(8,128)(2,1)}, bf16[272,512]{1,0:T(8,128)(2,1)}, u32[]{:S(2)}, u32[]{:S(2)}) collective-permute-start(bf16[272,512]{1,0:T(8,128)(2,1)} %get-tuple-element.86), channel_id=1, source_target_pairs={{0,2},{2,4},{4,6},{6,0},{1,3},{3,5},{5,7},{7,1},{8,10},{10,12},{12... | collective-permute-start | bytes 835592 | tf_op jit(solution)/shard_map/ppermute | solution.py:28
  147.1 4.9 %copy-start.15 = (bf16[16,128,896]{2,1,0:T(8,128)(2,1)S(1)}, bf16[16,128,896]{2,1,0:T(8,128)(2,1)}, u32[]{:S(2)}) copy-start(bf16[16,128,896]{2,1,0:T(8,128)(2,1)} %get-tuple-element.45) | copy-start | bytes 11010052
  147.1 5.4 %copy-start.16 = (bf16[2048,512]{1,0:T(8,128)(2,1)S(1)}, bf16[2048,512]{1,0:T(8,128)(2,1)}, u32[]{:S(2)}) copy-start(bf16[2048,512]{1,0:T(8,128)(2,1)} %get-tuple-element.47) | copy-start | bytes 6291460
  156.1 69.2 %all-to-all-start = ((bf16[16,112,512]{2,1,0:T(8,128)(2,1)}), bf16[16,112,512]{2,1,0:T(8,128)(2,1)}, u32[]{:S(2)}, u32[]{:S(2)}) async-start(bf16[16,112,512]{2,1,0:T(8,128)(2,1)} %pad_maximum_fusion), calls=%async_computation.1 | async-start | bytes 3670016 | tf_op jit(solution)/shard_map/all_to_all | solution.py:53
  165.5 32.5 %collective-permute-start.18 = (bf16[4,128,512]{2,1,0:T(8,128)(2,1)}, bf16[4,128,512]{2,1,0:T(8,128)(2,1)}, u32[]{:S(2)}, u32[]{:S(2)}) collective-permute-start(bf16[4,128,512]{2,1,0:T(8,128)(2,1)} %get-tuple-element.38), channel_id=1, source_target_pairs={{0,64},{8,72},{16,80},{24,88},{32,96},{40,104},{48,112},{56,120},{... | collective-permute-start | bytes 1572872 | tf_op jit(solution)/shard_map/ppermute | solution.py:284
  168.8 37.8 %collective-permute-start.19 = (bf16[4,128,512]{2,1,0:T(8,128)(2,1)}, bf16[4,128,512]{2,1,0:T(8,128)(2,1)}, u32[]{:S(2)}, u32[]{:S(2)}) collective-permute-start(bf16[4,128,512]{2,1,0:T(8,128)(2,1)} %get-tuple-element.39), channel_id=1, source_target_pairs={{0,32},{8,40},{16,48},{24,56},{32,64},{40,72},{48,80},{56,88},{64,... | collective-permute-start | bytes 1572872 | tf_op jit(solution)/shard_map/ppermute | solution.py:284
  169.4 37.2 %collective-permute-start.20 = (bf16[4,128,512]{2,1,0:T(8,128)(2,1)}, bf16[4,128,512]{2,1,0:T(8,128)(2,1)}, u32[]{:S(2)}, u32[]{:S(2)}) collective-permute-start(bf16[4,128,512]{2,1,0:T(8,128)(2,1)} %get-tuple-element.40), channel_id=1, source_target_pairs={{0,96},{8,104},{16,112},{24,120},{32,0},{40,8},{48,16},{56,24},{64... | collective-permute-start | bytes 1572872 | tf_op jit(solution)/shard_map/ppermute | solution.py:284
  172.1 39.9 %collective-permute-start.24 = (bf16[4,128,512]{2,1,0:T(8,128)(2,1)}, bf16[4,128,512]{2,1,0:T(8,128)(2,1)}, u32[]{:S(2)}, u32[]{:S(2)}) collective-permute-start(bf16[4,128,512]{2,1,0:T(8,128)(2,1)} %get-tuple-element.42), channel_id=1, source_target_pairs={{0,16},{8,24},{16,0},{24,8},{32,48},{40,56},{48,32},{56,40},{64,80... | collective-permute-start | bytes 1572872 | tf_op jit(solution)/shard_map/ppermute | solution.py:288
  175.1 39.6 %collective-permute-start.25 = (bf16[4,128,512]{2,1,0:T(8,128)(2,1)}, bf16[4,128,512]{2,1,0:T(8,128)(2,1)}, u32[]{:S(2)}, u32[]{:S(2)}) collective-permute-start(bf16[4,128,512]{2,1,0:T(8,128)(2,1)} %get-tuple-element.43), channel_id=1, source_target_pairs={{0,8},{8,16},{16,24},{24,0},{32,40},{40,48},{48,56},{56,32},{64,72... | collective-permute-start | bytes 1572872 | tf_op jit(solution)/shard_map/ppermute | solution.py:288
  177.1 20.9 %copy-start.5 = (bf16[4,128,512]{2,1,0:T(8,128)(2,1)S(1)}, bf16[4,128,512]{2,1,0:T(8,128)(2,1)}, u32[]{:S(2)}) copy-start(bf16[4,128,512]{2,1,0:T(8,128)(2,1)} %copy-done.4) | copy-start | bytes 1572868
  197.9 16.8 %collective-permute-start.26 = (bf16[4,128,512]{2,1,0:T(8,128)(2,1)S(1)}, bf16[4,128,512]{2,1,0:T(8,128)(2,1)S(1)}, u32[]{:S(2)}, u32[]{:S(2)}) collective-permute-start(bf16[4,128,512]{2,1,0:T(8,128)(2,1)S(1)} %copy-done.5), channel_id=1, source_target_pairs={{0,24},{8,0},{16,8},{24,16},{32,56},{40,32},{48,40},{56,48},{64,88... | collective-permute-start | bytes 1572872 | tf_op jit(solution)/shard_map/ppermute | solution.py:288
  208.3 9.6 %collective-permute-start.21 = (bf16[128,512]{1,0:T(8,128)(2,1)S(1)}, bf16[128,512]{1,0:T(8,128)(2,1)S(1)}, u32[]{:S(2)}, u32[]{:S(2)}) collective-permute-start(bf16[128,512]{1,0:T(8,128)(2,1)S(1)} %get-tuple-element.79), channel_id=1, source_target_pairs={{0,16},{8,24},{16,0},{24,8},{32,48},{40,56},{48,32},{56,40},{64,80... | collective-permute-start | bytes 393224 | tf_op jit(solution)/shard_map/ppermute | solution.py:288
  211.5 9.7 %collective-permute-start.22 = (bf16[128,512]{1,0:T(8,128)(2,1)S(1)}, bf16[128,512]{1,0:T(8,128)(2,1)S(1)}, u32[]{:S(2)}, u32[]{:S(2)}) collective-permute-start(bf16[128,512]{1,0:T(8,128)(2,1)S(1)} %get-tuple-element.81), channel_id=1, source_target_pairs={{0,8},{8,16},{16,24},{24,0},{32,40},{40,48},{48,56},{56,32},{64,72... | collective-permute-start | bytes 393224 | tf_op jit(solution)/shard_map/ppermute | solution.py:288
  212.0 9.2 %collective-permute-start.23 = (bf16[128,512]{1,0:T(8,128)(2,1)S(1)}, bf16[128,512]{1,0:T(8,128)(2,1)S(1)}, u32[]{:S(2)}, u32[]{:S(2)}) collective-permute-start(bf16[128,512]{1,0:T(8,128)(2,1)S(1)} %get-tuple-element.80), channel_id=1, source_target_pairs={{0,24},{8,0},{16,8},{24,16},{32,56},{40,32},{48,40},{56,48},{64,88... | collective-permute-start | bytes 393224 | tf_op jit(solution)/shard_map/ppermute | solution.py:288
  216.2 6.6 %collective-permute-start.27 = (bf16[128,512]{1,0:T(8,128)(2,1)S(1)}, bf16[128,512]{1,0:T(8,128)(2,1)S(1)}, u32[]{:S(2)}, u32[]{:S(2)}) collective-permute-start(bf16[128,512]{1,0:T(8,128)(2,1)S(1)} %get-tuple-element.82), channel_id=1, source_target_pairs={{0,64},{8,72},{16,80},{24,88},{32,96},{40,104},{48,112},{56,120},{... | collective-permute-start | bytes 393224 | tf_op jit(solution)/shard_map/ppermute | solution.py:284
  217.9 6.3 %collective-permute-start.28 = (bf16[128,512]{1,0:T(8,128)(2,1)S(1)}, bf16[128,512]{1,0:T(8,128)(2,1)S(1)}, u32[]{:S(2)}, u32[]{:S(2)}) collective-permute-start(bf16[128,512]{1,0:T(8,128)(2,1)S(1)} %get-tuple-element.84), channel_id=1, source_target_pairs={{0,32},{8,40},{16,48},{24,56},{32,64},{40,72},{48,80},{56,88},{64,... | collective-permute-start | bytes 393224 | tf_op jit(solution)/shard_map/ppermute | solution.py:284
  218.0 6.2 %collective-permute-start.29 = (bf16[128,512]{1,0:T(8,128)(2,1)S(1)}, bf16[128,512]{1,0:T(8,128)(2,1)S(1)}, u32[]{:S(2)}, u32[]{:S(2)}) collective-permute-start(bf16[128,512]{1,0:T(8,128)(2,1)S(1)} %get-tuple-element.83), channel_id=1, source_target_pairs={{0,96},{8,104},{16,112},{24,120},{32,0},{40,8},{48,16},{56,24},{64... | collective-permute-start | bytes 393224 | tf_op jit(solution)/shard_map/ppermute | solution.py:284
  221.1 6.7 %copy-start.1 = (bf16[1024,896]{1,0:T(8,128)(2,1)S(1)}, bf16[1024,896]{1,0:T(8,128)(2,1)}, u32[]{:S(2)}) copy-start(bf16[1024,896]{1,0:T(8,128)(2,1)} %param.18) | copy-start | bytes 5505028
  (2 other events, 2.9 us)
Sparse Core Ops, SparseCore 0:
  19.5 71.9 all-gather.2
  144.0 62.8 reduce-scatter.1

commit v2 on v1

--- a/solution.py
+++ b/solution.py
@@ -62,11 +62,15 @@
 
 
 def project_kernel(n_ref, x, d, w, o):
-    wq = w[:, :128].reshape(1024, 512)
-    wo = w[:, 128:].reshape(1024, 512)
     tokens = x.shape[0]
-    o[0, :tokens] = dot(x[...], wq).astype(BF16)
-    o[0, tokens:] = dot(d[...], wo).astype(BF16)
+    q = jnp.zeros((tokens, 512), F32)
+    dc = jnp.zeros((tokens, 512), F32)
+    for s in range(4):
+        cols = slice(256 * s, 256 * s + 256)
+        q += dot(x[:, cols], w[2 * s])
+        dc += dot(d[:, cols], w[2 * s + 1])
+    o[0, :tokens] = q.astype(BF16)
+    o[0, tokens:] = dc.astype(BF16)
 
 
 def project(n, normed, dout, weights):
@@ -79,7 +83,7 @@
             in_specs=[
                 pl.BlockSpec((tokens, feats), lambda r, n: (0, 0)),
                 pl.BlockSpec((tokens, feats), lambda r, n: (0, 0)),
-                pl.BlockSpec((8, 256, 512), lambda r, n: ((n[0] + r) % 4, 0, 0)),
+                pl.BlockSpec((8, 256, 512), lambda r, n: ((2 * n[0] + r) % 4, 0, 0)),
             ],
             out_specs=pl.BlockSpec((1, 2 * tokens, 512), lambda r, n: (r, 0, 0)),
         ),
@@ -201,10 +205,9 @@
 def finish_kernel(n_ref, x, hid, dout, gain, rstd, stat, w, out, dhid, oa, na):
     step = pl.program_id(0)
     tokens = hid.shape[0]
-    wq = w[:, :128].reshape(1024, 512)
-    wo = w[:, 128:].reshape(1024, 512)
-    o_part = dot(x[0, :tokens], wo, NT)
-    n_part = dot(x[0, tokens : 2 * tokens], wq, NT)
+    o_part = jnp.concatenate([dot(x[0, :tokens], w[2 * s + 1], NT) for s in range(4)], axis=1)
+    dq = x[0, tokens : 2 * tokens]
+    n_part = jnp.concatenate([dot(dq, w[2 * s], NT) for s in range(4)], axis=1)
 
     @pl.when(step == 0)
     def _():
@@ -242,7 +245,7 @@
                 pl.BlockSpec((1, feats), lambda r, n: (0, 0)),
                 column,
                 column,
-                pl.BlockSpec((8, 256, 512), lambda r, n: ((n[0] + r) % 4, 0, 0)),
+                pl.BlockSpec((8, 256, 512), lambda r, n: ((2 * n[0] + r) % 4, 0, 0)),
             ],
             out_specs=[whole, whole],
             scratch_shapes=[pltpu.VMEM((tokens, feats), F32)] * 2,
@@ -254,30 +257,29 @@
     )(n, x, hidden, dout, gain[None], rstd, stat, weights)
 
 
-def outer_kernel(at, d, ctx, a0, a1, a2, a3, b0, b1, b2, b3):
-    n, x, z = at[0], at[1], at[2]
-    upper, lower = (a0, a1, a2, a3), (b0, b1, b2, b3)
-    half = a0.shape[1]
-    for i in range(4):
-        block = lax.rem(x + i + 4 - n, 4)
-        for j in range(4):
-            first = pl.multiple_of(lax.rem(z + j, 4) * 2 * half, 2 * half)
-            part = dot(d[block, :, pl.ds(first, 2 * half)], ctx[...], TN).astype(BF16)
-            upper[i][j] = part[:half]
-            lower[j][i] = part[half:]
-
-
-def outer(at, dout, ctx):
-    share = jax.ShapeDtypeStruct((4, 128, ctx.shape[1]), BF16)
+def outer_kernel(n_ref, d, ctx, o):
+    for s in range(4):
+        o[s] = dot(d[0, :, 256 * s : 256 * s + 256], ctx[...], TN).astype(BF16)
+
+
+def outer(n, dout, ctx):
+    tokens = ctx.shape[0]
     return pl.pallas_call(
         outer_kernel,
-        in_specs=[SMEM, VMEM, VMEM],
-        out_specs=[VMEM] * 8,
-        out_shape=[share] * 8,
-        cost_estimate=cost(ctx.shape[0] * 4096 * 512, 6 << 20),
-        compiler_params=pltpu.CompilerParams(vmem_limit_bytes=24 << 20),
+        grid_spec=pltpu.PrefetchScalarGridSpec(
+            num_scalar_prefetch=1,
+            grid=(4,),
+            in_specs=[
+                pl.BlockSpec((1, tokens, 1024), lambda r, n: (r, 0, 0)),
+                pl.BlockSpec((tokens, 512), lambda r, n: (0, 0)),
+            ],
+            out_specs=pl.BlockSpec((4, 256, 512), lambda r, n: ((n[0] + r) % 4, 0, 0)),
+        ),
+        out_shape=pltpu.HBM((16, 256, 512), BF16),
+        cost_estimate=cost(tokens * 4096 * 512, 6 << 20),
+        compiler_params=pltpu.CompilerParams(vmem_limit_bytes=16 << 20),
         name="outer",
-    )(at, dout, ctx)
+    )(n, dout, ctx)
 
 
 def along_x(share, by):
@@ -310,16 +312,14 @@
     tokens, feats = hidden.shape
     spans = tokens // CLEN
 
-    q_half = lax.dynamic_slice_in_dim(w_q, b * 128, 128, axis=0)
-    o_half = lax.dynamic_slice_in_dim(w_o, b * 128, 128, axis=1).T
     kv_half = jnp.where(b == 0, w_k, w_v)
     swap = [
-        ((4 * i + j) * 4 + k, (4 * k + j) * 4 + i)
+        ((4 * i + j) * 4 + k, ((i + k) % 4 * 4 + j) * 4 + i)
         for i in range(4)
         for j in range(4)
         for k in range(4)
     ]
-    qo_half = lax.ppermute(jnp.concatenate([q_half, o_half], axis=0), ("seq", "nbr"), swap)
+    qo_half = lax.ppermute(jnp.where(b == 0, w_q, w_o.T), ("seq", "nbr"), swap)
     weights = lax.all_gather(
         jnp.concatenate([qo_half, kv_half], axis=0), ("seq", "batch"), axis=0
     )
@@ -392,23 +392,23 @@
     stat = stat / (rstd * (4 * feats))
     out, d_hidden = finish(n1, heads, hidden, d_out, dec_gain, rstd, stat, weights)
 
-    place = lax.axis_index("seq").astype(jnp.int32)
-    at = jnp.stack([n.astype(jnp.int32), place // 4, place % 4])
-    d_wo_parts = outer(at, dout_rel, ctx)
-    upper = [along_x(d_wo_parts[i], i) for i in (2, 1, 3)]
-    lower = [along_z(d_wo_parts[4 + i], i) for i in (2, 1, 3)]
-    upper = total([d_wo_parts[0]] + upper).astype(BF16)
-    lower = total([d_wo_parts[4]] + lower).astype(BF16)
-    upper = total([upper[0]] + [along_z(upper[i], i) for i in (2, 1, 3)])
-    lower = total([lower[0]] + [along_x(lower[i], i) for i in (2, 1, 3)])
-    d_wo = jnp.concatenate([upper, lower], axis=0).T
+    d_wo = jnp.sum(exchange(outer(n1, dout_rel, ctx)).astype(F32), axis=0).T
 
     rows = enc.reshape(-1, enc.shape[2])
-    d_wk_part = dot(rows, d_key, TN).astype(BF16).reshape(16, -1, 512)
-    d_wv_part = dot(rows, d_value, TN).astype(BF16).reshape(16, -1, 512)
-    d_wkv_parts = jnp.concatenate([d_wk_part, d_wv_part], axis=1)
-    d_wkv = jnp.sum(exchange(d_wkv_parts).astype(F32), axis=0)
-    d_wk, d_wv = d_wkv[:56], d_wkv[56:]
+    place = lax.axis_index("seq")
+    px, pz = place // 4, place % 4
+
+    def block(parts, i, dim):
+        return lax.dynamic_index_in_dim(parts, i % 4, dim, keepdims=False)
+
+    wk_parts = dot(rows, d_key, TN).astype(BF16).reshape(4, 4, -1, 512)
+    wv_parts = dot(rows, d_value, TN).astype(BF16).reshape(4, 4, -1, 512)
+    wk_sum = [block(wk_parts, px, 0)] + [along_x(block(wk_parts, px + i, 0), i) for i in (2, 1, 3)]
+    wv_sum = [block(wv_parts, pz, 1)] + [along_z(block(wv_parts, pz + i, 1), i) for i in (2, 1, 3)]
+    wk_sum, wv_sum = total(wk_sum).astype(BF16), total(wv_sum).astype(BF16)
+    d_wk = [block(wk_sum, pz, 0)] + [along_z(block(wk_sum, pz + i, 0), i) for i in (2, 1, 3)]
+    d_wv = [block(wv_sum, px, 0)] + [along_x(block(wv_sum, px + i, 0), i) for i in (2, 1, 3)]
+    d_wk, d_wv = total(d_wk), total(d_wv)
 
     return (out, d_hidden, d_enc, d_wo, d_wk, d_wv)
 

time: 237 us -> 250 us (1.055)
  waiting for transfers between devices: 54.3 us -> 75.7 us
  other arithmetic: 19.6 us -> 14.3 us
  local copies, waits for them, and re-layouts: 11.8 us -> 7.57 us
    ppermute x6, waiting for transfers between devices: 0.02 us -> 36.9 us  [along_z(): lax.ppermute(share, 'seq', [(i, i // 4 * 4 + (i + by) % 4) for i in range...]
    ppermute x6, waiting for transfers between devices: 22.7 us -> 7.94 us  [along_x(): lax.ppermute(share, 'seq', [(i, (i // 4 + by) % 4 * 4 + i % 4) for i in r...]
    ppermute x6, starting transfers between devices: 11.5 us -> 21.4 us  [along_x(): lax.ppermute(share, 'seq', [(i, (i // 4 + by) % 4 * 4 + i % 4) for i in r...]
    concatenate x2 -> x0, other arithmetic: 3.08 us -> none  [the longest x1 1.63 us: body(): jnp.concatenate([q_half, o_half], axis=0)]
    ppermute x1, starting transfers between devices: 3.58 us -> 0.68 us  [body(): qo_half = lax.ppermute(jnp.where(b == 0, w_q, w_o.T), ('seq', 'nbr'), swap)]
    convert_element_type x2, other arithmetic: 3.11 us -> 0.25 us  [body(): wk_sum, wv_sum = (total(wk_sum).astype(BF16), total(wv_sum).astype(BF16))]
    ppermute x16, starting transfers between devices: 33.7 us -> 30.9 us  [shift(): return lax.ppermute(x, 'nbr', [(i, (i + by) % n) for i in range(n)])]
    ppermute x6, starting transfers between devices: 12.6 us -> 9.83 us  [along_z(): lax.ppermute(share, 'seq', [(i, i // 4 * 4 + (i + by) % 4) for i in range...]
  transfers between devices with their start and end apart: 33 -> 33, of which waited for: 9 -> 9; matrix products, arithmetic and copies ran while one was open for 19% -> 16% of each run, Pallas kernels for 8% -> 7%
where the time goes in v2:
time: 250 us; the launch traced here: 249 us
  waiting for transfers between devices  75.7 us (30%)
  starting transfers between devices  72.3 us (29%)
  Pallas kernels  41.5 us (17%)
  matrix products  22.6 us (9%)
  between operations  14.8 us (6%)
  other arithmetic  14.3 us (6%)
  local copies, waits for them, and re-layouts  7.57 us (3%)
    ppermute x6, waiting for transfers between devices, along_z(): lax.ppermute(share, 'seq', [(i, i // 4 * 4 + (i + by) % 4) for i in range...  36.9 us
    ppermute x16, starting transfers between devices, shift(): return lax.ppermute(x, 'nbr', [(i, (i + by) % n) for i in range(n)])  30.9 us
    ppermute x16, waiting for transfers between devices, shift(): return lax.ppermute(x, 'nbr', [(i, (i + by) % n) for i in range(n)])  30.3 us
    ppermute x6, starting transfers between devices, along_x(): lax.ppermute(share, 'seq', [(i, (i // 4 + by) % 4 * 4 + i % 4) for i in r...  21.4 us
    pallas_call x1, Pallas kernels, attend(): pl.pallas_call(attend_kernel, in_specs=[SMEM, SMEM] + [VMEM] * 6, out_spe...  17.7 us
    dot_general x4, matrix products, encode(): jnp.dot(enc_normed.reshape(-1, width), w_enc, preferred_element_type=F32)  15.3 us
    ppermute x6, starting transfers between devices, along_z(): lax.ppermute(share, 'seq', [(i, i // 4 * 4 + (i + by) % 4) for i in range...  9.83 us
    pallas_call x1, Pallas kernels, keys_values(): pl.pallas_call(keys_kernel, in_specs=[SMEM] + [VMEM] * 6, out_specs=[VMEM...  8.17 us
  transfers between devices with their start and end apart: 33, of which 9 were waited for; matrix products, arithmetic and copies ran while one was open for 16% of the time, Pallas kernels for 7%

profile of v2, /device:TPU:0, one launch (start us, length us, event | category | flops | bytes accessed | tf_op | source)
XLA Modules:
  0.0 249.0 jit_solution(16835450072826158356)
XLA Ops:
  7.3 1.9 copy.45
  9.2 1.1 bitcast_select_fusion
  11.0 0.8 broadcast_select_fusion
  11.8 0.7 pad_maximum_fusion.4
  12.7 15.1 %collective-permute-start.4 = (bf16[6,128,896]{2,1,0:T(8,128)(2,1)}, bf16[6,128,896]{2,1,0:T(8,128)(2,1)}, u32[]{:S(2)}, u32[]{:S(2)}) collective-permute-start(bf16[6,128,896]{2,1,0:T(8,128)(2,1)} %param.14), channel_id=1, source_target_pairs={{0,6},{2,0},{4,2},{6,4},{1,7},{3,1},{5,3},{7,5},{8,14},{10,8},{12,... | collective-permute-start | bytes 4128776 | tf_op jit(solution)/shard_map/ppermute | solution.py:28
  27.8 1.0 bitcast_reduce_fusion
  28.8 3.8 %collective-permute-start = (bf16[1,1024]{1,0:T(2,128)(2,1)S(1)}, bf16[1,1024]{1,0:T(2,128)(2,1)S(1)}, u32[]{:S(2)}, u32[]{:S(2)}) collective-permute-start(bf16[1,1024]{1,0:T(2,128)(2,1)S(1)} %get-tuple-element.79), channel_id=1, source_target_pairs={{0,8},{8,16},{16,24},{24,32},{32,40},{40,48},{48,56},{56,64},{64,7... | collective-permute-start | bytes 6152 | tf_op jit(solution)/shard_map/ppermute | solution.py:331
  34.4 4.7 %collective-permute-start.2 = (f32[3,896]{1,0:T(4,128)S(1)}, f32[3,896]{1,0:T(4,128)S(1)}, u32[]{:S(2)}, u32[]{:S(2)}) collective-permute-start(f32[3,896]{1,0:T(4,128)S(1)} %pad_maximum_fusion.6), channel_id=1, source_target_pairs={{0,4},{2,6},{4,0},{6,2},{1,5},{3,7},{5,1},{7,3},{8,12},{10,14},{12... | collective-permute-start | bytes 32264 | tf_op jit(solution)/shard_map/ppermute | solution.py:28
  39.2 21.3 %collective-permute-done.1 = f32[3,896]{1,0:T(4,128)S(1)} collective-permute-done((f32[3,896]{1,0:T(4,128)S(1)}, f32[3,896]{1,0:T(4,128)S(1)}, u32[]{:S(2)}, u32[]{:S(2)}) %collective-permute-start.1) | collective-permute-done | bytes 10784 | tf_op jit(solution)/shard_map/ppermute | solution.py:28
  61.3 2.1 add_convert_fusion.3.e0
  63.7 0.7 collective-permute-start.10
  64.4 1.0 collective-permute-start.11
  65.5 1.2 slice.97
  66.6 2.7 %collective-permute-start.5 = (bf16[3,128,896]{2,1,0:T(8,128)(2,1)S(1)}, bf16[3,128,896]{2,1,0:T(8,128)(2,1)S(1)}, u32[]{:S(2)}, u32[]{:S(2)}) collective-permute-start(bf16[3,128,896]{2,1,0:T(8,128)(2,1)S(1)} %slice.97), channel_id=1, source_target_pairs={{0,6},{2,0},{4,2},{6,4},{1,7},{3,1},{5,3},{7,5},{8,14},{10,8},{12,... | collective-permute-start | bytes 2064392 | tf_op jit(solution)/shard_map/ppermute | solution.py:28
  69.4 1.2 slice.98
  70.8 1.9 multiply_reduce_fusion
  72.7 1.9 multiply_reduce_fusion.2
  74.7 5.2 %add_convert_fusion.e3 = bf16[6,128,896]{2,1,0:T(8,128)(2,1)} fusion(bf16[6,128,896]{2,1,0:T(8,128)(2,1)} %collective-permute-done.6, bf16[896,896]{1,0:T(8,128)(2,1)S(1)} %copy-done.12, f32[6,128]{1,0:T(8,128)S(1)} %add_rsqrt_fusion, f32[6,896]{1,0:T(8,128)S(1)} %get-tuple-element.75, f32[896]{0:T(1024)S(1)} %convert_element_type.179), kind=kOutput, calls=%fused_computation.1 | convolution fusion | flops 1242071040 | bytes 4386304 | tf_op jit(solution)/shard_map/dot_general | solution.py:364
  79.8 4.9 %add_convert_fusion.2.e1 = bf16[6,128,896]{2,1,0:T(8,128)(2,1)} fusion(bf16[6,128,896]{2,1,0:T(8,128)(2,1)} %collective-permute-done.4, bf16[896,896]{1,0:T(8,128)(2,1)S(1)} %copy-done.12, f32[6,128]{1,0:T(8,128)S(1)} %add_rsqrt_fusion.2, f32[6,896]{1,0:T(8,128)S(1)} %get-tuple-element.76, f32[896]{0:T(1024)S(1)} %convert_element_type.179), kind=kOutput, calls=%fused_computation.9 | convolution fusion | flops 1242071040 | bytes 4386304 | tf_op jit(solution)/shard_map/dot_general | solution.py:364
  84.9 4.8 %collective-permute-done.5 = bf16[3,128,896]{2,1,0:T(8,128)(2,1)S(1)} collective-permute-done((bf16[3,128,896]{2,1,0:T(8,128)(2,1)S(1)}, bf16[3,128,896]{2,1,0:T(8,128)(2,1)S(1)}, u32[]{:S(2)}, u32[]{:S(2)}) %collective-permute-start.5) | collective-permute-done | bytes 688160 | tf_op jit(solution)/shard_map/ppermute | solution.py:28
  89.6 1.9 collective-permute-done.7
  92.0 3.2 %add_convert_fusion.1.e2 = bf16[6,128,896]{2,1,0:T(8,128)(2,1)} fusion(bf16[896,896]{1,0:T(8,128)(2,1)S(1)} %copy-done.12, f32[6,128]{1,0:T(8,128)S(1)} %add_rsqrt_fusion.1, f32[6,896]{1,0:T(8,128)S(1)} %get-tuple-element.77, f32[896]{0:T(1024)S(1)} %convert_element_type.179, bf16[3,128,896]{2,1,0:T(8,128)(2,1)S(1)} %collective-permute-done.7, ...), kind=kOutput, calls=%fused_computation.5 | convolution fusion | flops 1243447296 | bytes 4386304 | tf_op jit(solution)/shard_map/dot_general | solution.py:364
  95.2 1.6 fusion.56
  96.8 5.3 %project.1 = bf16[4,256,512]{2,1,0:T(8,128)(2,1)S(1)} custom-call(s32[1]{0:T(128)} %bitcast.n_ref, bf16[128,1024]{1,0:T(8,128)(2,1)S(1)} %multiply_convert_fusion.16.x, bf16[128,1024]{1,0:T(8,128)(2,1)S(1)} %copy-done.3, bf16[32,312,512]{2,1,0:T(8,128)(2,1)} %bitcast.120), custom_call_target="tpu_custom_call" | custom-call | flops 1073741824 | bytes 12582912 | tf_op jit(solution)/shard_map/project/pallas_call | solution.py:78
  102.8 0.9 collective-permute-start.13
  103.7 2.4 collective-permute-start.14
  106.0 8.2 %keys_values.1 = (bf16[16,128,896]{2,1,0:T(8,128)(2,1)}, bf16[2048,512]{1,0:T(8,128)(2,1)S(1)}, bf16[2048,512]{1,0:T(8,128)(2,1)S(1)}) custom-call(s32[18]{0:T(128)S(1)} %pad_add_fusion.1.tab, bf16[6,128,896]{2,1,0:T(8,128)(2,1)S(1)} %add_convert_fusion.3.e0, bf16[6,128,896]{2,1,0:T(8,128)(2,1)S(1)} %copy-done.5, bf16[6,128,896]{2,1,0:T(8,128)(2,1)S(1)} %copy-done.6, ...), custom_call_target="tpu_custom_call" | custom-call | flops 3758096384 | bytes 16777216 | tf_op jit(solution)/shard_map/keys_values/pallas_call | solution.py:130
  114.2 2.3 collective-permute-done.13
  116.7 17.7 %attend.1 = (bf16[128,512]{1,0:T(8,128)(2,1)S(1)}, bf16[128,512]{1,0:T(8,128)(2,1)S(1)}, bf16[2048,512]{1,0:T(8,128)(2,1)}, bf16[2048,512]{1,0:T(8,128)(2,1)}, bf16[24,128,896]{2,1,0:T(8,128)(2,1)}) custom-call(s32[18]{0:T(128)S(1)} %pad_add_fusion.1.tab, s32[24]{0:T(128)S(1)} %get-tuple-element.89.inv, bf16[2048,512]{1,0:T(8,128)(2,1)S(1)} %get-tuple-element.19.kb, ...), custom_call_target="tpu_custom_call" | custom-call | flops 3758096384 | bytes 41943040 | tf_op jit(solution)/shard_map/attend/pallas_call | solution.py:193
  134.4 3.4 %outer.1 = bf16[16,256,512]{2,1,0:T(8,128)(2,1)} custom-call(s32[1]{0:T(128)} %bitcast.n_ref, bf16[4,128,1024]{2,1,0:T(8,128)(2,1)S(1)} %pad_maximum_fusion.2.d, bf16[128,512]{1,0:T(8,128)(2,1)S(1)} %get-tuple-element.23.ctx), custom_call_target="tpu_custom_call" | custom-call | flops 536870912 | bytes 6291456 | tf_op jit(solution)/shard_map/outer/pallas_call | solution.py:267
  137.8 5.7 %all-to-all-start = ((bf16[16,256,512]{2,1,0:T(8,128)(2,1)}), bf16[16,256,512]{2,1,0:T(8,128)(2,1)}, u32[]{:S(2)}, u32[]{:S(2)}) async-start(bf16[16,256,512]{2,1,0:T(8,128)(2,1)} %outer.1), calls=%async_computation.1 | async-start | bytes 8388608 | tf_op jit(solution)/shard_map/all_to_all | solution.py:53
  144.6 1.4 collective-permute-start.16
  146.0 4.9 %convolution_convert_fusion = bf16[896,512]{1,0:T(8,128)(2,1)S(1)} fusion(bf16[2048,896]{1,0:T(8,128)(2,1)} %bitcast.134, bf16[2048,512]{1,0:T(8,128)(2,1)} %get-tuple-element.31), kind=kOutput, calls=%fused_computation.25 | convolution fusion | flops 1879506944 | bytes 6684672 | tf_op jit(solution)/shard_map/dot_general | solution.py:19
  151.0 3.3 %collective-permute-start.24 = (bf16[4,56,512]{2,1,0:T(8,128)(2,1)S(1)}, bf16[4,56,512]{2,1,0:T(8,128)(2,1)S(1)}, u32[]{:S(2)}, u32[]{:S(2)}) collective-permute-start(bf16[4,56,512]{2,1,0:T(8,128)(2,1)S(1)} %get-tuple-element.57), channel_id=1, source_target_pairs={{0,16},{8,24},{16,0},{24,8},{32,48},{40,56},{48,32},{56,40},{64,80... | collective-permute-start | bytes 688136 | tf_op jit(solution)/shard_map/ppermute | solution.py:290
  154.8 2.7 %collective-permute-start.26 = (bf16[4,56,512]{2,1,0:T(8,128)(2,1)S(1)}, bf16[4,56,512]{2,1,0:T(8,128)(2,1)S(1)}, u32[]{:S(2)}, u32[]{:S(2)}) collective-permute-start(bf16[4,56,512]{2,1,0:T(8,128)(2,1)S(1)} %get-tuple-element.58), channel_id=1, source_target_pairs={{0,24},{8,0},{16,8},{24,16},{32,56},{40,32},{48,40},{56,48},{64,88... | collective-permute-start | bytes 688136 | tf_op jit(solution)/shard_map/ppermute | solution.py:290
  157.5 2.1 convolution_convert_fusion.1
  159.7 35.3 %collective-permute-done.24 = bf16[4,56,512]{2,1,0:T(8,128)(2,1)S(1)} collective-permute-done((bf16[4,56,512]{2,1,0:T(8,128)(2,1)S(1)}, bf16[4,56,512]{2,1,0:T(8,128)(2,1)S(1)}, u32[]{:S(2)}, u32[]{:S(2)}) %collective-permute-start.24) | collective-permute-done | bytes 229408 | tf_op jit(solution)/shard_map/ppermute | solution.py:290
  195.0 8.9 %collective-permute-start.18 = (bf16[4,56,512]{2,1,0:T(8,128)(2,1)S(1)}, bf16[4,56,512]{2,1,0:T(8,128)(2,1)S(1)}, u32[]{:S(2)}, u32[]{:S(2)}) collective-permute-start(bf16[4,56,512]{2,1,0:T(8,128)(2,1)S(1)} %get-tuple-element.60), channel_id=1, source_target_pairs={{0,64},{8,72},{16,80},{24,88},{32,96},{40,104},{48,112},{56,120},{... | collective-permute-start | bytes 688136 | tf_op jit(solution)/shard_map/ppermute | solution.py:286
  203.9 5.2 %collective-permute-start.19 = (bf16[4,56,512]{2,1,0:T(8,128)(2,1)S(1)}, bf16[4,56,512]{2,1,0:T(8,128)(2,1)S(1)}, u32[]{:S(2)}, u32[]{:S(2)}) collective-permute-start(bf16[4,56,512]{2,1,0:T(8,128)(2,1)S(1)} %get-tuple-element.62), channel_id=1, source_target_pairs={{0,32},{8,40},{16,48},{24,56},{32,64},{40,72},{48,80},{56,88},{64,... | collective-permute-start | bytes 688136 | tf_op jit(solution)/shard_map/ppermute | solution.py:286
  209.2 4.0 %collective-permute-done.18 = bf16[4,56,512]{2,1,0:T(8,128)(2,1)S(1)} collective-permute-done((bf16[4,56,512]{2,1,0:T(8,128)(2,1)S(1)}, bf16[4,56,512]{2,1,0:T(8,128)(2,1)S(1)}, u32[]{:S(2)}, u32[]{:S(2)}) %collective-permute-start.18) | collective-permute-done | bytes 229408 | tf_op jit(solution)/shard_map/ppermute | solution.py:286
  213.2 4.0 %collective-permute-done.19 = bf16[4,56,512]{2,1,0:T(8,128)(2,1)S(1)} collective-permute-done((bf16[4,56,512]{2,1,0:T(8,128)(2,1)S(1)}, bf16[4,56,512]{2,1,0:T(8,128)(2,1)S(1)}, u32[]{:S(2)}, u32[]{:S(2)}) %collective-permute-start.19) | collective-permute-done | bytes 229408 | tf_op jit(solution)/shard_map/ppermute | solution.py:286
  217.2 3.9 %collective-permute-start.27 = (bf16[56,512]{1,0:T(8,128)(2,1)S(1)}, bf16[56,512]{1,0:T(8,128)(2,1)S(1)}, u32[]{:S(2)}, u32[]{:S(2)}) collective-permute-start(bf16[56,512]{1,0:T(8,128)(2,1)S(1)} %get-tuple-element.67), channel_id=1, source_target_pairs={{0,64},{8,72},{16,80},{24,88},{32,96},{40,104},{48,112},{56,120},{... | collective-permute-start | bytes 172040 | tf_op jit(solution)/shard_map/ppermute | solution.py:286
  221.5 3.1 %collective-permute-start.29 = (bf16[56,512]{1,0:T(8,128)(2,1)S(1)}, bf16[56,512]{1,0:T(8,128)(2,1)S(1)}, u32[]{:S(2)}, u32[]{:S(2)}) collective-permute-start(bf16[56,512]{1,0:T(8,128)(2,1)S(1)} %get-tuple-element.68), channel_id=1, source_target_pairs={{0,96},{8,104},{16,112},{24,120},{32,0},{40,8},{48,16},{56,24},{64... | collective-permute-start | bytes 172040 | tf_op jit(solution)/shard_map/ppermute | solution.py:286
  225.0 7.0 %finish.1 = (bf16[128,1024]{1,0:T(8,128)(2,1)}, bf16[128,1024]{1,0:T(8,128)(2,1)}) custom-call(s32[1]{0:T(128)} %bitcast.n_ref, bf16[4,272,512]{2,1,0:T(8,128)(2,1)S(1)} %pad_maximum_fusion.1.x, bf16[128,1024]{1,0:T(8,128)(2,1)S(1)} %copy-done.2, bf16[128,1024]{1,0:T(8,128)(2,1)S(1)} %copy-done.3, bf16[1,1024]{1,0:T(2,128)(2,1)S(1)} %broadcast_in_dim.141.gain, ...), custom_call_target="tpu_custom_call" | custom-call | flops 1073741824 | bytes 12582912 | tf_op jit(solution)/shard_map/finish/pallas_call | solution.py:236
  232.0 3.2 %collective-permute-start.23 = (bf16[56,512]{1,0:T(8,128)(2,1)S(1)}, bf16[56,512]{1,0:T(8,128)(2,1)S(1)}, u32[]{:S(2)}, u32[]{:S(2)}) collective-permute-start(bf16[56,512]{1,0:T(8,128)(2,1)S(1)} %get-tuple-element.71), channel_id=1, source_target_pairs={{0,24},{8,0},{16,8},{24,16},{32,56},{40,32},{48,40},{56,48},{64,88... | collective-permute-start | bytes 172040 | tf_op jit(solution)/shard_map/ppermute | solution.py:290
  236.0 1.6 collective-permute-done.23
  238.3 2.8 %convert_reduce_fusion = f32[256,512]{1,0:T(8,128)S(1)} fusion(bf16[16,256,512]{2,1,0:T(8,128)(2,1)} %all-to-all-done), kind=kLoop, calls=%fused_computation | loop fusion | flops 4063232 | bytes 4718592 | tf_op jit(solution)/shard_map/reduce_sum | solution.py:395
  241.1 1.0 copy.51
  (125 shorter events, 9.3 us)
Async XLA Ops:
  7.2 26.8 %copy-start = (bf16[1024,896]{1,0:T(8,128)(2,1)S(1)}, bf16[1024,896]{1,0:T(8,128)(2,1)}, u32[]{:S(2)}) copy-start(bf16[1024,896]{1,0:T(8,128)(2,1)} %param.18) | copy-start | bytes 5505028
  7.2 53.4 %copy-start.7 = (bf16[6,128,896]{2,1,0:T(8,128)(2,1)S(1)}, bf16[6,128,896]{2,1,0:T(8,128)(2,1)}, u32[]{:S(2)}) copy-start(bf16[6,128,896]{2,1,0:T(8,128)(2,1)} %param.14) | copy-start | bytes 4128772
  7.2 25.9 %copy-start.2 = (bf16[128,1024]{1,0:T(8,128)(2,1)S(1)}, bf16[128,1024]{1,0:T(8,128)(2,1)}, u32[]{:S(2)}) copy-start(bf16[128,1024]{1,0:T(8,128)(2,1)} %hid.1) | copy-start | bytes 786436
  7.2 25.4 %copy-start.11 = (s32[24]{0:T(128)S(1)}, s32[24]{0:T(128)}, u32[]{:S(2)}) copy-start(s32[24]{0:T(128)} %param.15) | copy-start | bytes 292
  7.2 31.9 %copy-start.10 = (bf16[896]{0:T(1024)(128)(2,1)S(1)}, bf16[896]{0:T(1024)(128)(2,1)}, u32[]{:S(2)}) copy-start(bf16[896]{0:T(1024)(128)(2,1)} %param.17) | copy-start | bytes 5380
  7.2 31.9 %copy-start.9 = (bf16[1024]{0:T(1024)(128)(2,1)S(1)}, bf16[1024]{0:T(1024)(128)(2,1)}, u32[]{:S(2)}) copy-start(bf16[1024]{0:T(1024)(128)(2,1)} %param.16) | copy-start | bytes 6148
  7.2 87.9 %all-gather.3.cloned.1.call-start = ((), (), s32[]{:S(2)}) async-start(), calls=%async_computation.3 | async-start | bytes 10543104 | tf_op jit(solution)/shard_map/all_gather | solution.py:323
  10.3 1.5 collective-permute-start.8
  12.6 229.5 %reduce-scatter.2.cloned.1.call-start = ((), (), s32[]{:S(2)}) async-start(), calls=%async_computation.2 | async-start | bytes 6881280 | tf_op jit(solution)/shard_map/reduce_scatter | solution.py:385
  12.7 50.7 %collective-permute-start.4 = (bf16[6,128,896]{2,1,0:T(8,128)(2,1)}, bf16[6,128,896]{2,1,0:T(8,128)(2,1)}, u32[]{:S(2)}, u32[]{:S(2)}) collective-permute-start(bf16[6,128,896]{2,1,0:T(8,128)(2,1)} %param.14), channel_id=1, source_target_pairs={{0,6},{2,0},{4,2},{6,4},{1,7},{3,1},{5,3},{7,5},{8,14},{10,8},{12,... | collective-permute-start | bytes 4128776 | tf_op jit(solution)/shard_map/ppermute | solution.py:28
  27.8 35.6 %collective-permute-start.6 = (bf16[6,128,896]{2,1,0:T(8,128)(2,1)}, bf16[6,128,896]{2,1,0:T(8,128)(2,1)}, u32[]{:S(2)}, u32[]{:S(2)}) collective-permute-start(bf16[6,128,896]{2,1,0:T(8,128)(2,1)} %param.14), channel_id=1, source_target_pairs={{0,2},{2,4},{4,6},{6,0},{1,3},{3,5},{5,7},{7,1},{8,10},{10,12},{12... | collective-permute-start | bytes 4128776 | tf_op jit(solution)/shard_map/ppermute | solution.py:28
  28.8 5.1 %collective-permute-start = (bf16[1,1024]{1,0:T(2,128)(2,1)S(1)}, bf16[1,1024]{1,0:T(2,128)(2,1)S(1)}, u32[]{:S(2)}, u32[]{:S(2)}) collective-permute-start(bf16[1,1024]{1,0:T(2,128)(2,1)S(1)} %get-tuple-element.79), channel_id=1, source_target_pairs={{0,8},{8,16},{16,24},{24,32},{32,40},{40,48},{48,56},{56,64},{64,7... | collective-permute-start | bytes 6152 | tf_op jit(solution)/shard_map/ppermute | solution.py:331
  32.7 28.5 %copy-start.8 = (bf16[6,128,896]{2,1,0:T(8,128)(2,1)S(1)}, bf16[6,128,896]{2,1,0:T(8,128)(2,1)}, u32[]{:S(2)}) copy-start(bf16[6,128,896]{2,1,0:T(8,128)(2,1)} %param.14) | copy-start | bytes 4128772
  32.7 28.5 %copy-start.12 = (bf16[896,896]{1,0:T(8,128)(2,1)S(1)}, bf16[896,896]{1,0:T(8,128)(2,1)}, u32[]{:S(2)}) copy-start(bf16[896,896]{1,0:T(8,128)(2,1)} %param.19) | copy-start | bytes 4816900
  34.3 26.2 %collective-permute-start.1 = (f32[3,896]{1,0:T(4,128)S(1)}, f32[3,896]{1,0:T(4,128)S(1)}, u32[]{:S(2)}, u32[]{:S(2)}) collective-permute-start(f32[3,896]{1,0:T(4,128)S(1)} %pad_maximum_fusion.6), channel_id=1, source_target_pairs={{0,2},{2,4},{4,6},{6,0},{1,3},{3,5},{5,7},{7,1},{8,10},{10,12},{12... | collective-permute-start | bytes 32264 | tf_op jit(solution)/shard_map/ppermute | solution.py:28
  34.4 26.1 %collective-permute-start.2 = (f32[3,896]{1,0:T(4,128)S(1)}, f32[3,896]{1,0:T(4,128)S(1)}, u32[]{:S(2)}, u32[]{:S(2)}) collective-permute-start(f32[3,896]{1,0:T(4,128)S(1)} %pad_maximum_fusion.6), channel_id=1, source_target_pairs={{0,4},{2,6},{4,0},{6,2},{1,5},{3,7},{5,1},{7,3},{8,12},{10,14},{12... | collective-permute-start | bytes 32264 | tf_op jit(solution)/shard_map/ppermute | solution.py:28
  39.1 21.4 %collective-permute-start.3 = (f32[3,896]{1,0:T(4,128)S(1)}, f32[3,896]{1,0:T(4,128)S(1)}, u32[]{:S(2)}, u32[]{:S(2)}) collective-permute-start(f32[3,896]{1,0:T(4,128)S(1)} %pad_maximum_fusion.6), channel_id=1, source_target_pairs={{0,6},{2,0},{4,2},{6,4},{1,7},{3,1},{5,3},{7,5},{8,14},{10,8},{12,... | collective-permute-start | bytes 32264 | tf_op jit(solution)/shard_map/ppermute | solution.py:28
  61.2 2.1 copy-start.3
  63.4 21.4 %collective-permute-start.9 = (bf16[128,1024]{1,0:T(8,128)(2,1)S(1)}, bf16[128,1024]{1,0:T(8,128)(2,1)S(1)}, u32[]{:S(2)}, u32[]{:S(2)}) collective-permute-start(bf16[128,1024]{1,0:T(8,128)(2,1)S(1)} %copy-done.3), channel_id=1, source_target_pairs={{0,6},{2,0},{4,2},{6,4},{1,7},{3,1},{5,3},{7,5},{8,14},{10,8},{12,... | collective-permute-start | bytes 786440 | tf_op jit(solution)/shard_map/ppermute | solution.py:28
  63.7 21.0 %collective-permute-start.10 = (bf16[128,1024]{1,0:T(8,128)(2,1)S(1)}, bf16[128,1024]{1,0:T(8,128)(2,1)S(1)}, u32[]{:S(2)}, u32[]{:S(2)}) collective-permute-start(bf16[128,1024]{1,0:T(8,128)(2,1)S(1)} %copy-done.3), channel_id=1, source_target_pairs={{0,4},{2,6},{4,0},{6,2},{1,5},{3,7},{5,1},{7,3},{8,12},{10,14},{12... | collective-permute-start | bytes 786440 | tf_op jit(solution)/shard_map/ppermute | solution.py:28
  64.4 20.3 %collective-permute-start.11 = (bf16[128,1024]{1,0:T(8,128)(2,1)S(1)}, bf16[128,1024]{1,0:T(8,128)(2,1)S(1)}, u32[]{:S(2)}, u32[]{:S(2)}) collective-permute-start(bf16[128,1024]{1,0:T(8,128)(2,1)S(1)} %copy-done.3), channel_id=1, source_target_pairs={{0,2},{2,4},{4,6},{6,0},{1,3},{3,5},{5,7},{7,1},{8,10},{10,12},{12... | collective-permute-start | bytes 786440 | tf_op jit(solution)/shard_map/ppermute | solution.py:28
  66.6 23.0 %collective-permute-start.5 = (bf16[3,128,896]{2,1,0:T(8,128)(2,1)S(1)}, bf16[3,128,896]{2,1,0:T(8,128)(2,1)S(1)}, u32[]{:S(2)}, u32[]{:S(2)}) collective-permute-start(bf16[3,128,896]{2,1,0:T(8,128)(2,1)S(1)} %slice.97), channel_id=1, source_target_pairs={{0,6},{2,0},{4,2},{6,4},{1,7},{3,1},{5,3},{7,5},{8,14},{10,8},{12,... | collective-permute-start | bytes 2064392 | tf_op jit(solution)/shard_map/ppermute | solution.py:28
  70.5 21.0 %collective-permute-start.7 = (bf16[3,128,896]{2,1,0:T(8,128)(2,1)S(1)}, bf16[3,128,896]{2,1,0:T(8,128)(2,1)S(1)}, u32[]{:S(2)}, u32[]{:S(2)}) collective-permute-start(bf16[3,128,896]{2,1,0:T(8,128)(2,1)S(1)} %slice.98), channel_id=1, source_target_pairs={{0,2},{2,4},{4,6},{6,0},{1,3},{3,5},{5,7},{7,1},{8,10},{10,12},{12... | collective-permute-start | bytes 2064392 | tf_op jit(solution)/shard_map/ppermute | solution.py:28
  96.8 9.3 %copy-start.4 = (bf16[6,128,896]{2,1,0:T(8,128)(2,1)S(1)}, bf16[6,128,896]{2,1,0:T(8,128)(2,1)}, u32[]{:S(2)}) copy-start(bf16[6,128,896]{2,1,0:T(8,128)(2,1)} %add_convert_fusion.e3) | copy-start | bytes 4128772
  96.8 9.3 %copy-start.5 = (bf16[6,128,896]{2,1,0:T(8,128)(2,1)S(1)}, bf16[6,128,896]{2,1,0:T(8,128)(2,1)}, u32[]{:S(2)}) copy-start(bf16[6,128,896]{2,1,0:T(8,128)(2,1)} %add_convert_fusion.2.e1) | copy-start | bytes 4128772
  96.8 9.2 %copy-start.6 = (bf16[6,128,896]{2,1,0:T(8,128)(2,1)S(1)}, bf16[6,128,896]{2,1,0:T(8,128)(2,1)}, u32[]{:S(2)}) copy-start(bf16[6,128,896]{2,1,0:T(8,128)(2,1)} %add_convert_fusion.1.e2) | copy-start | bytes 4128772
  102.1 12.1 %collective-permute-start.12 = (bf16[256,512]{1,0:T(8,128)(2,1)S(1)}, bf16[256,512]{1,0:T(8,128)(2,1)S(1)}, u32[]{:S(2)}, u32[]{:S(2)}) collective-permute-start(bf16[256,512]{1,0:T(8,128)(2,1)S(1)} %get-tuple-element.54), channel_id=1, source_target_pairs={{0,4},{2,6},{4,0},{6,2},{1,5},{3,7},{5,1},{7,3},{8,12},{10,14},{12... | collective-permute-start | bytes 786440 | tf_op jit(solution)/shard_map/ppermute | solution.py:28
  102.8 13.7 %collective-permute-start.13 = (bf16[256,512]{1,0:T(8,128)(2,1)S(1)}, bf16[256,512]{1,0:T(8,128)(2,1)S(1)}, u32[]{:S(2)}, u32[]{:S(2)}) collective-permute-start(bf16[256,512]{1,0:T(8,128)(2,1)S(1)} %get-tuple-element.56), channel_id=1, source_target_pairs={{0,2},{2,4},{4,6},{6,0},{1,3},{3,5},{5,7},{7,1},{8,10},{10,12},{12... | collective-permute-start | bytes 786440 | tf_op jit(solution)/shard_map/ppermute | solution.py:28
  103.7 12.8 %collective-permute-start.14 = (bf16[256,512]{1,0:T(8,128)(2,1)S(1)}, bf16[256,512]{1,0:T(8,128)(2,1)S(1)}, u32[]{:S(2)}, u32[]{:S(2)}) collective-permute-start(bf16[256,512]{1,0:T(8,128)(2,1)S(1)} %get-tuple-element.55), channel_id=1, source_target_pairs={{0,6},{2,0},{4,2},{6,4},{1,7},{3,1},{5,3},{7,5},{8,14},{10,8},{12,... | collective-permute-start | bytes 786440 | tf_op jit(solution)/shard_map/ppermute | solution.py:28
  137.8 100.5 %all-to-all-start = ((bf16[16,256,512]{2,1,0:T(8,128)(2,1)}), bf16[16,256,512]{2,1,0:T(8,128)(2,1)}, u32[]{:S(2)}, u32[]{:S(2)}) async-start(bf16[16,256,512]{2,1,0:T(8,128)(2,1)} %outer.1), calls=%async_computation.1 | async-start | bytes 8388608 | tf_op jit(solution)/shard_map/all_to_all | solution.py:53
  143.9 77.5 %collective-permute-start.15 = (bf16[272,512]{1,0:T(8,128)(2,1)S(1)}, bf16[272,512]{1,0:T(8,128)(2,1)S(1)}, u32[]{:S(2)}, u32[]{:S(2)}) collective-permute-start(bf16[272,512]{1,0:T(8,128)(2,1)S(1)} %get-tuple-element.64), channel_id=1, source_target_pairs={{0,6},{2,0},{4,2},{6,4},{1,7},{3,1},{5,3},{7,5},{8,14},{10,8},{12,... | collective-permute-start | bytes 835592 | tf_op jit(solution)/shard_map/ppermute | solution.py:28
  144.6 80.0 %collective-permute-start.16 = (bf16[272,512]{1,0:T(8,128)(2,1)S(1)}, bf16[272,512]{1,0:T(8,128)(2,1)S(1)}, u32[]{:S(2)}, u32[]{:S(2)}) collective-permute-start(bf16[272,512]{1,0:T(8,128)(2,1)S(1)} %get-tuple-element.64), channel_id=1, source_target_pairs={{0,4},{2,6},{4,0},{6,2},{1,5},{3,7},{5,1},{7,3},{8,12},{10,14},{12... | collective-permute-start | bytes 835592 | tf_op jit(solution)/shard_map/ppermute | solution.py:28
  146.0 11.5 %copy-start.13 = (bf16[16,128,896]{2,1,0:T(8,128)(2,1)S(1)}, bf16[16,128,896]{2,1,0:T(8,128)(2,1)}, u32[]{:S(2)}) copy-start(bf16[16,128,896]{2,1,0:T(8,128)(2,1)} %get-tuple-element.29) | copy-start | bytes 11010052
  146.0 11.5 %copy-start.14 = (bf16[2048,512]{1,0:T(8,128)(2,1)S(1)}, bf16[2048,512]{1,0:T(8,128)(2,1)}, u32[]{:S(2)}) copy-start(bf16[2048,512]{1,0:T(8,128)(2,1)} %get-tuple-element.30) | copy-start | bytes 6291460
  151.0 44.0 %collective-permute-start.24 = (bf16[4,56,512]{2,1,0:T(8,128)(2,1)S(1)}, bf16[4,56,512]{2,1,0:T(8,128)(2,1)S(1)}, u32[]{:S(2)}, u32[]{:S(2)}) collective-permute-start(bf16[4,56,512]{2,1,0:T(8,128)(2,1)S(1)} %get-tuple-element.57), channel_id=1, source_target_pairs={{0,16},{8,24},{16,0},{24,8},{32,48},{40,56},{48,32},{56,40},{64,80... | collective-permute-start | bytes 688136 | tf_op jit(solution)/shard_map/ppermute | solution.py:290
  154.3 49.6 %collective-permute-start.25 = (bf16[4,56,512]{2,1,0:T(8,128)(2,1)S(1)}, bf16[4,56,512]{2,1,0:T(8,128)(2,1)S(1)}, u32[]{:S(2)}, u32[]{:S(2)}) collective-permute-start(bf16[4,56,512]{2,1,0:T(8,128)(2,1)S(1)} %get-tuple-element.59), channel_id=1, source_target_pairs={{0,8},{8,16},{16,24},{24,0},{32,40},{40,48},{48,56},{56,32},{64,72... | collective-permute-start | bytes 688136 | tf_op jit(solution)/shard_map/ppermute | solution.py:290
  154.8 54.2 %collective-permute-start.26 = (bf16[4,56,512]{2,1,0:T(8,128)(2,1)S(1)}, bf16[4,56,512]{2,1,0:T(8,128)(2,1)S(1)}, u32[]{:S(2)}, u32[]{:S(2)}) collective-permute-start(bf16[4,56,512]{2,1,0:T(8,128)(2,1)S(1)} %get-tuple-element.58), channel_id=1, source_target_pairs={{0,24},{8,0},{16,8},{24,16},{32,56},{40,32},{48,40},{56,48},{64,88... | collective-permute-start | bytes 688136 | tf_op jit(solution)/shard_map/ppermute | solution.py:290
  195.0 18.2 %collective-permute-start.18 = (bf16[4,56,512]{2,1,0:T(8,128)(2,1)S(1)}, bf16[4,56,512]{2,1,0:T(8,128)(2,1)S(1)}, u32[]{:S(2)}, u32[]{:S(2)}) collective-permute-start(bf16[4,56,512]{2,1,0:T(8,128)(2,1)S(1)} %get-tuple-element.60), channel_id=1, source_target_pairs={{0,64},{8,72},{16,80},{24,88},{32,96},{40,104},{48,112},{56,120},{... | collective-permute-start | bytes 688136 | tf_op jit(solution)/shard_map/ppermute | solution.py:286
  203.9 13.3 %collective-permute-start.19 = (bf16[4,56,512]{2,1,0:T(8,128)(2,1)S(1)}, bf16[4,56,512]{2,1,0:T(8,128)(2,1)S(1)}, u32[]{:S(2)}, u32[]{:S(2)}) collective-permute-start(bf16[4,56,512]{2,1,0:T(8,128)(2,1)S(1)} %get-tuple-element.62), channel_id=1, source_target_pairs={{0,32},{8,40},{16,48},{24,56},{32,64},{40,72},{48,80},{56,88},{64,... | collective-permute-start | bytes 688136 | tf_op jit(solution)/shard_map/ppermute | solution.py:286
  209.1 12.0 %collective-permute-start.20 = (bf16[4,56,512]{2,1,0:T(8,128)(2,1)S(1)}, bf16[4,56,512]{2,1,0:T(8,128)(2,1)S(1)}, u32[]{:S(2)}, u32[]{:S(2)}) collective-permute-start(bf16[4,56,512]{2,1,0:T(8,128)(2,1)S(1)} %get-tuple-element.61), channel_id=1, source_target_pairs={{0,96},{8,104},{16,112},{24,120},{32,0},{40,8},{48,16},{56,24},{64... | collective-permute-start | bytes 688136 | tf_op jit(solution)/shard_map/ppermute | solution.py:286
  213.2 11.4 %collective-permute-start.17 = (bf16[272,512]{1,0:T(8,128)(2,1)S(1)}, bf16[272,512]{1,0:T(8,128)(2,1)S(1)}, u32[]{:S(2)}, u32[]{:S(2)}) collective-permute-start(bf16[272,512]{1,0:T(8,128)(2,1)S(1)} %get-tuple-element.64), channel_id=1, source_target_pairs={{0,2},{2,4},{4,6},{6,0},{1,3},{3,5},{5,7},{7,1},{8,10},{10,12},{12... | collective-permute-start | bytes 835592 | tf_op jit(solution)/shard_map/ppermute | solution.py:28
  217.2 14.9 %collective-permute-start.27 = (bf16[56,512]{1,0:T(8,128)(2,1)S(1)}, bf16[56,512]{1,0:T(8,128)(2,1)S(1)}, u32[]{:S(2)}, u32[]{:S(2)}) collective-permute-start(bf16[56,512]{1,0:T(8,128)(2,1)S(1)} %get-tuple-element.67), channel_id=1, source_target_pairs={{0,64},{8,72},{16,80},{24,88},{32,96},{40,104},{48,112},{56,120},{... | collective-permute-start | bytes 172040 | tf_op jit(solution)/shard_map/ppermute | solution.py:286
  221.1 14.2 %collective-permute-start.28 = (bf16[56,512]{1,0:T(8,128)(2,1)S(1)}, bf16[56,512]{1,0:T(8,128)(2,1)S(1)}, u32[]{:S(2)}, u32[]{:S(2)}) collective-permute-start(bf16[56,512]{1,0:T(8,128)(2,1)S(1)} %get-tuple-element.69), channel_id=1, source_target_pairs={{0,32},{8,40},{16,48},{24,56},{32,64},{40,72},{48,80},{56,88},{64,... | collective-permute-start | bytes 172040 | tf_op jit(solution)/shard_map/ppermute | solution.py:286
  221.5 13.8 %collective-permute-start.29 = (bf16[56,512]{1,0:T(8,128)(2,1)S(1)}, bf16[56,512]{1,0:T(8,128)(2,1)S(1)}, u32[]{:S(2)}, u32[]{:S(2)}) collective-permute-start(bf16[56,512]{1,0:T(8,128)(2,1)S(1)} %get-tuple-element.68), channel_id=1, source_target_pairs={{0,96},{8,104},{16,112},{24,120},{32,0},{40,8},{48,16},{56,24},{64... | collective-permute-start | bytes 172040 | tf_op jit(solution)/shard_map/ppermute | solution.py:286
  224.6 11.4 %collective-permute-start.21 = (bf16[56,512]{1,0:T(8,128)(2,1)S(1)}, bf16[56,512]{1,0:T(8,128)(2,1)S(1)}, u32[]{:S(2)}, u32[]{:S(2)}) collective-permute-start(bf16[56,512]{1,0:T(8,128)(2,1)S(1)} %get-tuple-element.70), channel_id=1, source_target_pairs={{0,16},{8,24},{16,0},{24,8},{32,48},{40,56},{48,32},{56,40},{64,80... | collective-permute-start | bytes 172040 | tf_op jit(solution)/shard_map/ppermute | solution.py:290
  224.6 11.4 %collective-permute-start.22 = (bf16[56,512]{1,0:T(8,128)(2,1)S(1)}, bf16[56,512]{1,0:T(8,128)(2,1)S(1)}, u32[]{:S(2)}, u32[]{:S(2)}) collective-permute-start(bf16[56,512]{1,0:T(8,128)(2,1)S(1)} %get-tuple-element.72), channel_id=1, source_target_pairs={{0,8},{8,16},{16,24},{24,0},{32,40},{40,48},{48,56},{56,32},{64,72... | collective-permute-start | bytes 172040 | tf_op jit(solution)/shard_map/ppermute | solution.py:290
  232.0 5.6 %collective-permute-start.23 = (bf16[56,512]{1,0:T(8,128)(2,1)S(1)}, bf16[56,512]{1,0:T(8,128)(2,1)S(1)}, u32[]{:S(2)}, u32[]{:S(2)}) collective-permute-start(bf16[56,512]{1,0:T(8,128)(2,1)S(1)} %get-tuple-element.71), channel_id=1, source_target_pairs={{0,24},{8,0},{16,8},{24,16},{32,56},{40,32},{48,40},{56,48},{64,88... | collective-permute-start | bytes 172040 | tf_op jit(solution)/shard_map/ppermute | solution.py:290
  237.6 4.5 %copy-start.1 = (bf16[1024,896]{1,0:T(8,128)(2,1)S(1)}, bf16[1024,896]{1,0:T(8,128)(2,1)}, u32[]{:S(2)}) copy-start(bf16[1024,896]{1,0:T(8,128)(2,1)} %param.18) | copy-start | bytes 5505028
Sparse Core Ops, SparseCore 0:
  12.7 69.7 all-gather.2
  134.5 66.4 reduce-scatter.1

commit v3 on v2

--- a/solution.py
+++ b/solution.py
@@ -49,10 +49,6 @@
     return x + shift(x, 1) + shift(x, 2) + shift(x, 3)
 
 
-def exchange(parts):
-    return lax.all_to_all(parts, "seq", split_axis=0, concat_axis=0, tiled=True)
-
-
 def rms_scale(values):
     return lax.rsqrt(jnp.mean(values * values, axis=-1, keepdims=True) + 1e-06)
 
@@ -61,14 +57,14 @@
     return pl.CostEstimate(flops=2 * products, transcendentals=0, bytes_accessed=moved)
 
 
-def project_kernel(n_ref, x, d, w, o):
+def project_kernel(n_ref, x, d, wq, wo, o):
     tokens = x.shape[0]
     q = jnp.zeros((tokens, 512), F32)
     dc = jnp.zeros((tokens, 512), F32)
     for s in range(4):
         cols = slice(256 * s, 256 * s + 256)
-        q += dot(x[:, cols], w[2 * s])
-        dc += dot(d[:, cols], w[2 * s + 1])
+        q += dot(x[:, cols], wq[s, 0])
+        dc += dot(d[:, cols], wo[s, 0])
     o[0, :tokens] = q.astype(BF16)
     o[0, tokens:] = dc.astype(BF16)
 
@@ -83,7 +79,8 @@
             in_specs=[
                 pl.BlockSpec((tokens, feats), lambda r, n: (0, 0)),
                 pl.BlockSpec((tokens, feats), lambda r, n: (0, 0)),
-                pl.BlockSpec((8, 256, 512), lambda r, n: ((2 * n[0] + r) % 4, 0, 0)),
+                pl.BlockSpec((4, 1, 256, 512), lambda r, n: ((2 * n[0] + r) % 4, 0, 0, 0)),
+                pl.BlockSpec((4, 1, 256, 512), lambda r, n: ((4 - r) % 4, 1, 0, 0)),
             ],
             out_specs=pl.BlockSpec((1, 2 * tokens, 512), lambda r, n: (r, 0, 0)),
         ),
@@ -91,7 +88,7 @@
         cost_estimate=cost(2 * tokens * 4096 * 512, 12 << 20),
         compiler_params=pltpu.CompilerParams(vmem_limit_bytes=24 << 20),
         name="project",
-    )(n, normed, dout, weights)
+    )(n, normed, dout, weights, weights)
 
 
 def keys_kernel(tab, e0, e1, e2, e3, wk, wv, enc, kb, vb):
@@ -202,12 +199,12 @@
     )(tab, inv, kb, vb, q, dc, wk, wv)
 
 
-def finish_kernel(n_ref, x, hid, dout, gain, rstd, stat, w, out, dhid, oa, na):
+def finish_kernel(n_ref, x, hid, dout, gain, rstd, stat, wq, wo, out, dhid, oa, na):
     step = pl.program_id(0)
     tokens = hid.shape[0]
-    o_part = jnp.concatenate([dot(x[0, :tokens], w[2 * s + 1], NT) for s in range(4)], axis=1)
+    o_part = jnp.concatenate([dot(x[0, :tokens], wo[s, 0], NT) for s in range(4)], axis=1)
     dq = x[0, tokens : 2 * tokens]
-    n_part = jnp.concatenate([dot(dq, w[2 * s], NT) for s in range(4)], axis=1)
+    n_part = jnp.concatenate([dot(dq, wq[s, 0], NT) for s in range(4)], axis=1)
 
     @pl.when(step == 0)
     def _():
@@ -245,7 +242,8 @@
                 pl.BlockSpec((1, feats), lambda r, n: (0, 0)),
                 column,
                 column,
-                pl.BlockSpec((8, 256, 512), lambda r, n: ((2 * n[0] + r) % 4, 0, 0)),
+                pl.BlockSpec((4, 1, 256, 512), lambda r, n: ((2 * n[0] + r) % 4, 0, 0, 0)),
+                pl.BlockSpec((4, 1, 256, 512), lambda r, n: ((4 - r) % 4, 1, 0, 0)),
             ],
             out_specs=[whole, whole],
             scratch_shapes=[pltpu.VMEM((tokens, feats), F32)] * 2,
@@ -254,40 +252,75 @@
         cost_estimate=cost(2 * tokens * 4096 * 512, 12 << 20),
         compiler_params=pltpu.CompilerParams(vmem_limit_bytes=24 << 20),
         name="finish",
-    )(n, x, hidden, dout, gain[None], rstd, stat, weights)
-
-
-def outer_kernel(n_ref, d, ctx, o):
-    for s in range(4):
-        o[s] = dot(d[0, :, 256 * s : 256 * s + 256], ctx[...], TN).astype(BF16)
-
-
-def outer(n, dout, ctx):
-    tokens = ctx.shape[0]
+    )(n, x, hidden, dout, gain[None], rstd, stat, weights, weights)
+
+
+def outer_kernel(dest, n_ref, d, ctx, o0, o1, o2, o3):
+    for i, out in enumerate((o0, o1, o2, o3)):
+
+        def share(j, carry, i=i, out=out):
+            to = dest[4 * i + j]
+            block = lax.rem(to // 4 + 4 - n_ref[0], 4)
+            first = pl.multiple_of(lax.rem(to, 4) * 256, 256)
+            out[j] = dot(d[block, :, pl.ds(first, 256)], ctx[...], TN).astype(BF16)
+            return carry
+
+        lax.fori_loop(0, 4, share, 0)
+
+
+def outer(dest, n, dout, ctx):
+    share = jax.ShapeDtypeStruct((4, 256, ctx.shape[1]), BF16)
     return pl.pallas_call(
         outer_kernel,
-        grid_spec=pltpu.PrefetchScalarGridSpec(
-            num_scalar_prefetch=1,
-            grid=(4,),
-            in_specs=[
-                pl.BlockSpec((1, tokens, 1024), lambda r, n: (r, 0, 0)),
-                pl.BlockSpec((tokens, 512), lambda r, n: (0, 0)),
-            ],
-            out_specs=pl.BlockSpec((4, 256, 512), lambda r, n: ((n[0] + r) % 4, 0, 0)),
-        ),
-        out_shape=pltpu.HBM((16, 256, 512), BF16),
-        cost_estimate=cost(tokens * 4096 * 512, 6 << 20),
+        in_specs=[SMEM, SMEM, VMEM, VMEM],
+        out_specs=[VMEM] * 4,
+        out_shape=[share] * 4,
+        cost_estimate=cost(ctx.shape[0] * 4096 * 512, 6 << 20),
         compiler_params=pltpu.CompilerParams(vmem_limit_bytes=16 << 20),
         name="outer",
-    )(n, dout, ctx)
-
-
-def along_x(share, by):
-    return lax.ppermute(share, "seq", [(i, (i // 4 + by) % 4 * 4 + i % 4) for i in range(16)])
-
-
-def along_z(share, by):
-    return lax.ppermute(share, "seq", [(i, i // 4 * 4 + (i + by) % 4) for i in range(16)])
+    )(dest, n, dout, ctx)
+
+
+def order_kernel(dest, wk, wv, o0, o1, o2, o3):
+    for i, out in enumerate((o0, o1, o2, o3)):
+        for j in range(4):
+            out[j, 0] = wk[dest[4 * i + j]]
+            out[j, 1] = wv[dest[4 * i + j]]
+
+
+def order(dest, wk, wv):
+    share = jax.ShapeDtypeStruct((4, 2) + wk.shape[1:], BF16)
+    return pl.pallas_call(
+        order_kernel,
+        in_specs=[SMEM, VMEM, VMEM],
+        out_specs=[VMEM] * 4,
+        out_shape=[share] * 4,
+        cost_estimate=cost(0, 4 << 20),
+        compiler_params=pltpu.CompilerParams(vmem_limit_bytes=16 << 20),
+        name="order",
+    )(dest, wk, wv)
+
+
+def along(share, by, first):
+    pairs = []
+    for i in range(16):
+        for core in range(2):
+            x, z = i // 4, i % 4
+            if (core == 0) == first:
+                x = (x + by) % 4
+            else:
+                z = (z + by) % 4
+            pairs.append((2 * i + core, 2 * (4 * x + z) + core))
+    return lax.ppermute(share, ("seq", "batch"), pairs)
+
+
+def first_phase(shares):
+    return [shares[0]] + [along(shares[i], i, True) for i in (2, 1, 3)]
+
+
+def second_phase(arrived):
+    near = total(arrived).astype(BF16)
+    return total([near[0]] + [along(near[j], j, False) for j in (2, 1, 3)])
 
 
 def slot_tables(slot_span, n):
@@ -313,13 +346,15 @@
     spans = tokens // CLEN
 
     kv_half = jnp.where(b == 0, w_k, w_v)
-    swap = [
-        ((4 * i + j) * 4 + k, ((i + k) % 4 * 4 + j) * 4 + i)
-        for i in range(4)
-        for j in range(4)
-        for k in range(4)
-    ]
-    qo_half = lax.ppermute(jnp.where(b == 0, w_q, w_o.T), ("seq", "nbr"), swap)
+    swap = []
+    for i in range(4):
+        for j in range(4):
+            for k in range(4):
+                for core, x in ((0, (i + k) % 4), (1, (i - k) % 4)):
+                    swap.append((((4 * i + j) * 4 + k) * 2 + core, ((4 * x + j) * 4 + i) * 2 + core))
+    qo_half = lax.ppermute(
+        jnp.where(b == 0, w_q, w_o.T), ("seq", "nbr", "batch"), swap
+    )
     weights = lax.all_gather(
         jnp.concatenate([qo_half, kv_half], axis=0), ("seq", "batch"), axis=0
     )
@@ -368,7 +403,7 @@
 
 
     pairs = weights.reshape(16, 2, 312, 512)
-    weights = pltpu.with_memory_space_constraint(weights, pltpu.HBM)
+    weights = pltpu.with_memory_space_constraint(pairs, pltpu.HBM)
     wk = pairs[:, 0, 256:].reshape(-1, 512)
     wv = pairs[:, 1, 256:].reshape(-1, 512)
 
@@ -392,23 +427,21 @@
     stat = stat / (rstd * (4 * feats))
     out, d_hidden = finish(n1, heads, hidden, d_out, dec_gain, rstd, stat, weights)
 
-    d_wo = jnp.sum(exchange(outer(n1, dout_rel, ctx)).astype(F32), axis=0).T
-
+    place = lax.axis_index("seq")
+    step = jnp.arange(4, dtype=jnp.int32)
+    one, two = step[:, None], step[None, :]
+    by_x, by_z = jnp.where(b == 0, one, two), jnp.where(b == 0, two, one)
+    dest = (place // 4 + by_x) % 4 * 4 + (place % 4 + by_z) % 4
+    dest = dest.astype(jnp.int32).reshape(-1)
+    arrived = first_phase(outer(dest, n1, dout_rel, ctx))
+    d_wo = second_phase(arrived).T
+
+    enc = lax.optimization_barrier((enc, arrived[2]))[0]
     rows = enc.reshape(-1, enc.shape[2])
-    place = lax.axis_index("seq")
-    px, pz = place // 4, place % 4
-
-    def block(parts, i, dim):
-        return lax.dynamic_index_in_dim(parts, i % 4, dim, keepdims=False)
-
-    wk_parts = dot(rows, d_key, TN).astype(BF16).reshape(4, 4, -1, 512)
-    wv_parts = dot(rows, d_value, TN).astype(BF16).reshape(4, 4, -1, 512)
-    wk_sum = [block(wk_parts, px, 0)] + [along_x(block(wk_parts, px + i, 0), i) for i in (2, 1, 3)]
-    wv_sum = [block(wv_parts, pz, 1)] + [along_z(block(wv_parts, pz + i, 1), i) for i in (2, 1, 3)]
-    wk_sum, wv_sum = total(wk_sum).astype(BF16), total(wv_sum).astype(BF16)
-    d_wk = [block(wk_sum, pz, 0)] + [along_z(block(wk_sum, pz + i, 0), i) for i in (2, 1, 3)]
-    d_wv = [block(wv_sum, px, 0)] + [along_x(block(wv_sum, px + i, 0), i) for i in (2, 1, 3)]
-    d_wk, d_wv = total(d_wk), total(d_wv)
+    wk_parts = dot(rows, d_key, TN).astype(BF16).reshape(16, -1, 512)
+    wv_parts = dot(rows, d_value, TN).astype(BF16).reshape(16, -1, 512)
+    both = second_phase(first_phase(order(dest, wk_parts, wv_parts)))
+    d_wk, d_wv = both[0], both[1]
 
     return (out, d_hidden, d_enc, d_wo, d_wk, d_wv)
 

time: 250 us -> 224 us (0.90); the launches traced: 249 us -> 220 us
  waiting for transfers between devices: 75.7 us -> 54.2 us
  starting transfers between devices: 72.3 us -> 62.2 us
  Pallas kernels: 41.5 us -> 44.5 us
  matrix products: 22.6 us -> 19.7 us
    ppermute x13, waiting for transfers between devices: 44.9 us -> 4.8 us  [the longest x12 4.8 us: along(): return lax.ppermute(share, ('seq', 'batch'), pairs)]
    ppermute x16, waiting for transfers between devices: 30.3 us -> 48.8 us  [shift(): return lax.ppermute(x, 'nbr', [(i, (i + by) % n) for i in range(n)])]
    all_to_all x1 -> x0, starting transfers between devices: 5.66 us -> none  [exchange(): return lax.all_to_all(parts, 'seq', split_axis=0, concat_axis=0, tiled=True)]
    ppermute x13, starting transfers between devices: 31.9 us -> 28.3 us  [the longest x12 27.6 us: along(): return lax.ppermute(share, ('seq', 'batch'), pairs)]
    pallas_call x1 -> x2, Pallas kernels: 3.4 us -> 6.33 us  [the longest x1 5.66 us: outer(): pl.pallas_call(outer_kernel, in_specs=[SMEM, SMEM, VMEM, VMEM], out_specs...]
    dot_general x2, matrix products: 7.01 us -> 4.16 us  [dot(): return lax.dot_general(a, b, (dims, ((), ())), preferred_element_type=F32)]
    reduce_sum x1 -> x0, other arithmetic: 2.82 us -> none  [body(): d_wo = jnp.sum(exchange(outer(n1, dout_rel, ctx)).astype(F32), axis=0).T]
  transfers between devices with their start and end apart: 33 -> 32, of which waited for: 9 -> 11; matrix products, arithmetic and copies ran while one was open for 16% -> 17% of each run, Pallas kernels for 7% -> 10%
where the time goes in v3:
time: 224 us; the launch traced here: 220 us
  starting transfers between devices  62.2 us (28%)
  waiting for transfers between devices  54.2 us (24%)
  Pallas kernels  44.5 us (20%)
  matrix products  19.7 us (9%)
  between operations  14.6 us (7%)
  other arithmetic  14.5 us (6%)
  local copies, waits for them, and re-layouts  10 us (4%)
    ppermute x16, waiting for transfers between devices, shift(): return lax.ppermute(x, 'nbr', [(i, (i + by) % n) for i in range(n)])  48.8 us
    ppermute x16, starting transfers between devices, shift(): return lax.ppermute(x, 'nbr', [(i, (i + by) % n) for i in range(n)])  30 us
    ppermute x12, starting transfers between devices, along(): return lax.ppermute(share, ('seq', 'batch'), pairs)  27.6 us
    pallas_call x1, Pallas kernels, attend(): pl.pallas_call(attend_kernel, in_specs=[SMEM, SMEM] + [VMEM] * 6, out_spe...  17.5 us
    dot_general x4, matrix products, encode(): jnp.dot(enc_normed.reshape(-1, width), w_enc, preferred_element_type=F32)  15.2 us
    pallas_call x1, Pallas kernels, keys_values(): pl.pallas_call(keys_kernel, in_specs=[SMEM] + [VMEM] * 6, out_specs=[VMEM...  8.07 us
    pallas_call x1, Pallas kernels, finish(): pl.pallas_call(finish_kernel, grid_spec=pltpu.PrefetchScalarGridSpec(num_...  7.42 us
    pallas_call x1, Pallas kernels, outer(): pl.pallas_call(outer_kernel, in_specs=[SMEM, SMEM, VMEM, VMEM], out_specs...  5.66 us
  transfers between devices with their start and end apart: 32, of which 11 were waited for; matrix products, arithmetic and copies ran while one was open for 17% of the time, Pallas kernels for 10%

profile of v3, /device:TPU:0, one launch (start us, length us, event | category | flops | bytes accessed | tf_op | source)
XLA Modules:
  0.0 219.7 jit_solution(6556711137250696528)
XLA Ops:
  7.3 1.9 copy.36
  9.2 1.1 bitcast_select_fusion
  12.7 13.6 %collective-permute-start.4 = (bf16[6,128,896]{2,1,0:T(8,128)(2,1)}, bf16[6,128,896]{2,1,0:T(8,128)(2,1)}, u32[]{:S(2)}, u32[]{:S(2)}) collective-permute-start(bf16[6,128,896]{2,1,0:T(8,128)(2,1)} %param.14), channel_id=1, source_target_pairs={{0,6},{2,0},{4,2},{6,4},{1,7},{3,1},{5,3},{7,5},{8,14},{10,8},{12,... | collective-permute-start | bytes 4128776 | tf_op jit(solution)/shard_map/ppermute | solution.py:28
  26.3 1.0 bitcast_reduce_fusion
  27.3 3.8 %collective-permute-start = (bf16[1,1024]{1,0:T(2,128)(2,1)S(1)}, bf16[1,1024]{1,0:T(2,128)(2,1)S(1)}, u32[]{:S(2)}, u32[]{:S(2)}) collective-permute-start(bf16[1,1024]{1,0:T(2,128)(2,1)S(1)} %get-tuple-element.99), channel_id=1, source_target_pairs={{0,8},{8,16},{16,24},{24,32},{32,40},{40,48},{48,56},{56,64},{64,7... | collective-permute-start | bytes 6152 | tf_op jit(solution)/shard_map/ppermute | solution.py:366
  32.9 4.7 %collective-permute-start.2 = (f32[3,896]{1,0:T(4,128)S(1)}, f32[3,896]{1,0:T(4,128)S(1)}, u32[]{:S(2)}, u32[]{:S(2)}) collective-permute-start(f32[3,896]{1,0:T(4,128)S(1)} %pad_maximum_fusion.6), channel_id=1, source_target_pairs={{0,4},{2,6},{4,0},{6,2},{1,5},{3,7},{5,1},{7,3},{8,12},{10,14},{12... | collective-permute-start | bytes 32264 | tf_op jit(solution)/shard_map/ppermute | solution.py:28
  37.7 18.4 %collective-permute-done.1 = f32[3,896]{1,0:T(4,128)S(1)} collective-permute-done((f32[3,896]{1,0:T(4,128)S(1)}, f32[3,896]{1,0:T(4,128)S(1)}, u32[]{:S(2)}, u32[]{:S(2)}) %collective-permute-start.1) | collective-permute-done | bytes 10784 | tf_op jit(solution)/shard_map/ppermute | solution.py:28
  56.1 1.3 collective-permute-done.2
  58.1 2.1 add_convert_fusion.3.e0
  60.7 1.2 collective-permute-start.10
  62.3 1.2 slice.137
  63.5 2.8 %collective-permute-start.5 = (bf16[3,128,896]{2,1,0:T(8,128)(2,1)S(1)}, bf16[3,128,896]{2,1,0:T(8,128)(2,1)S(1)}, u32[]{:S(2)}, u32[]{:S(2)}) collective-permute-start(bf16[3,128,896]{2,1,0:T(8,128)(2,1)S(1)} %slice.137), channel_id=1, source_target_pairs={{0,6},{2,0},{4,2},{6,4},{1,7},{3,1},{5,3},{7,5},{8,14},{10,8},{12,... | collective-permute-start | bytes 2064392 | tf_op jit(solution)/shard_map/ppermute | solution.py:28
  66.4 1.2 slice.138
  67.8 1.8 multiply_reduce_fusion
  69.6 1.8 multiply_reduce_fusion.2
  71.5 5.1 %add_convert_fusion.e3 = bf16[6,128,896]{2,1,0:T(8,128)(2,1)} fusion(bf16[6,128,896]{2,1,0:T(8,128)(2,1)} %collective-permute-done.6, bf16[896,896]{1,0:T(8,128)(2,1)S(1)} %copy-done.14, f32[6,128]{1,0:T(8,128)S(1)} %add_rsqrt_fusion, f32[6,896]{1,0:T(8,128)S(1)} %get-tuple-element.95, f32[896]{0:T(1024)S(1)} %convert_element_type.170), kind=kOutput, calls=%fused_computation | convolution fusion | flops 1242071040 | bytes 4386304 | tf_op jit(solution)/shard_map/dot_general | solution.py:399
  76.6 4.9 %add_convert_fusion.2.e1 = bf16[6,128,896]{2,1,0:T(8,128)(2,1)} fusion(bf16[6,128,896]{2,1,0:T(8,128)(2,1)} %collective-permute-done.4, bf16[896,896]{1,0:T(8,128)(2,1)S(1)} %copy-done.14, f32[6,128]{1,0:T(8,128)S(1)} %add_rsqrt_fusion.2, f32[6,896]{1,0:T(8,128)S(1)} %get-tuple-element.96, f32[896]{0:T(1024)S(1)} %convert_element_type.170), kind=kOutput, calls=%fused_computation.8 | convolution fusion | flops 1242071040 | bytes 4386304 | tf_op jit(solution)/shard_map/dot_general | solution.py:399
  81.6 4.6 %collective-permute-done.5 = bf16[3,128,896]{2,1,0:T(8,128)(2,1)S(1)} collective-permute-done((bf16[3,128,896]{2,1,0:T(8,128)(2,1)S(1)}, bf16[3,128,896]{2,1,0:T(8,128)(2,1)S(1)}, u32[]{:S(2)}, u32[]{:S(2)}) %collective-permute-start.5) | collective-permute-done | bytes 688160 | tf_op jit(solution)/shard_map/ppermute | solution.py:28
  86.2 1.9 collective-permute-done.7
  88.6 3.2 %add_convert_fusion.1.e2 = bf16[6,128,896]{2,1,0:T(8,128)(2,1)} fusion(bf16[896,896]{1,0:T(8,128)(2,1)S(1)} %copy-done.14, f32[6,128]{1,0:T(8,128)S(1)} %add_rsqrt_fusion.1, f32[6,896]{1,0:T(8,128)S(1)} %get-tuple-element.97, f32[896]{0:T(1024)S(1)} %convert_element_type.170, bf16[3,128,896]{2,1,0:T(8,128)(2,1)S(1)} %collective-permute-done.7, ...), kind=kOutput, calls=%fused_computation.4 | convolution fusion | flops 1243447296 | bytes 4386304 | tf_op jit(solution)/shard_map/dot_general | solution.py:399
  91.7 1.6 fusion.55
  93.3 5.2 %project.1 = bf16[4,256,512]{2,1,0:T(8,128)(2,1)S(1)} custom-call(s32[1]{0:T(128)} %bitcast.n_ref, bf16[128,1024]{1,0:T(8,128)(2,1)S(1)} %multiply_convert_fusion.16.x, bf16[128,1024]{1,0:T(8,128)(2,1)S(1)} %copy-done.3, bf16[16,2,312,512]{3,2,1,0:T(8,128)(2,1)} %bitcast.110, bf16[16,2,312,512]{3,2,1,0:T(8,128)(2,1)} %bitcast.111), custom_call_target="tpu_custom_call" | custom-call | flops 1073741824 | bytes 12582912 | tf_op jit(solution)/shard_map/project/pallas_call | solution.py:74
  98.6 1.1 collective-permute-start.12
  100.2 2.8 %collective-permute-start.14 = (bf16[256,512]{1,0:T(8,128)(2,1)S(1)}, bf16[256,512]{1,0:T(8,128)(2,1)S(1)}, u32[]{:S(2)}, u32[]{:S(2)}) collective-permute-start(bf16[256,512]{1,0:T(8,128)(2,1)S(1)} %get-tuple-element.82), channel_id=1, source_target_pairs={{0,6},{2,0},{4,2},{6,4},{1,7},{3,1},{5,3},{7,5},{8,14},{10,8},{12,... | collective-permute-start | bytes 786440 | tf_op jit(solution)/shard_map/ppermute | solution.py:28
  103.0 8.1 %keys_values.1 = (bf16[16,128,896]{2,1,0:T(8,128)(2,1)}, bf16[2048,512]{1,0:T(8,128)(2,1)S(1)}, bf16[2048,512]{1,0:T(8,128)(2,1)S(1)}) custom-call(s32[18]{0:T(128)S(1)} %pad_add_fusion.1.tab, bf16[6,128,896]{2,1,0:T(8,128)(2,1)S(1)} %add_convert_fusion.3.e0, bf16[6,128,896]{2,1,0:T(8,128)(2,1)S(1)} %copy-done.7, bf16[6,128,896]{2,1,0:T(8,128)(2,1)S(1)} %copy-done.8, ...), custom_call_target="tpu_custom_call" | custom-call | flops 3758096384 | bytes 16777216 | tf_op jit(solution)/shard_map/keys_values/pallas_call | solution.py:127
  111.1 1.7 collective-permute-done.13
  113.0 17.5 %attend.1 = (bf16[128,512]{1,0:T(8,128)(2,1)S(1)}, bf16[128,512]{1,0:T(8,128)(2,1)S(1)}, bf16[2048,512]{1,0:T(8,128)(2,1)}, bf16[2048,512]{1,0:T(8,128)(2,1)}, bf16[24,128,896]{2,1,0:T(8,128)(2,1)}) custom-call(s32[18]{0:T(128)S(1)} %pad_add_fusion.1.tab, s32[24]{0:T(128)S(1)} %get-tuple-element.109.inv, bf16[2048,512]{1,0:T(8,128)(2,1)S(1)} %get-tuple-element.28.kb, ...), custom_call_target="tpu_custom_call" | custom-call | flops 3758096384 | bytes 41943040 | tf_op jit(solution)/shard_map/attend/pallas_call | solution.py:190
  130.7 5.7 %outer.1 = (bf16[4,256,512]{2,1,0:T(8,128)(2,1)S(1)}, bf16[4,256,512]{2,1,0:T(8,128)(2,1)}, bf16[4,256,512]{2,1,0:T(8,128)(2,1)S(1)}, bf16[4,256,512]{2,1,0:T(8,128)(2,1)S(1)}) custom-call(s32[16]{0:T(128)S(1)} %fusion.43.dest, s32[1]{0:T(128)} %bitcast.n_ref, bf16[4,128,1024]{2,1,0:T(8,128)(2,1)S(1)} %pad_maximum_fusion.2.d, ...), custom_call_target="tpu_custom_call" | custom-call | flops 536870912 | bytes 6291456 | tf_op jit(solution)/shard_map/outer/pallas_call | solution.py:273
  136.4 1.0 copy-done.5
  137.3 3.9 %collective-permute-start.19 = (bf16[4,256,512]{2,1,0:T(8,128)(2,1)}, bf16[4,256,512]{2,1,0:T(8,128)(2,1)}, u32[]{:S(2)}, u32[]{:S(2)}) collective-permute-start(bf16[4,256,512]{2,1,0:T(8,128)(2,1)} %get-tuple-element.40), channel_id=1, source_target_pairs={{0,32},{1,9},{8,40},{9,17},{16,48},{17,25},{24,56},{25,1},{32,64},... | collective-permute-start | bytes 3145736 | tf_op jit(solution)/shard_map/ppermute | solution.py:314
  143.6 1.5 collective-permute-start.18
  145.1 11.7 %collective-permute-done.15 = bf16[272,512]{1,0:T(8,128)(2,1)S(1)} collective-permute-done((bf16[272,512]{1,0:T(8,128)(2,1)S(1)}, bf16[272,512]{1,0:T(8,128)(2,1)S(1)}, u32[]{:S(2)}, u32[]{:S(2)}) %collective-permute-start.15) | collective-permute-done | bytes 278560 | tf_op jit(solution)/shard_map/ppermute | solution.py:28
  156.9 2.4 %collective-permute-done.16 = bf16[272,512]{1,0:T(8,128)(2,1)} collective-permute-done((bf16[272,512]{1,0:T(8,128)(2,1)S(1)}, bf16[272,512]{1,0:T(8,128)(2,1)}, u32[]{:S(2)}, u32[]{:S(2)}) %collective-permute-start.16) | collective-permute-done | bytes 278560 | tf_op jit(solution)/shard_map/ppermute | solution.py:28
  159.3 6.7 %collective-permute-done.17 = bf16[272,512]{1,0:T(8,128)(2,1)} collective-permute-done((bf16[272,512]{1,0:T(8,128)(2,1)S(1)}, bf16[272,512]{1,0:T(8,128)(2,1)}, u32[]{:S(2)}, u32[]{:S(2)}) %collective-permute-start.17) | collective-permute-done | bytes 278560 | tf_op jit(solution)/shard_map/ppermute | solution.py:28
  166.0 1.2 pad_maximum_fusion.1.x
  167.4 7.4 %finish.1 = (bf16[128,1024]{1,0:T(8,128)(2,1)}, bf16[128,1024]{1,0:T(8,128)(2,1)}) custom-call(s32[1]{0:T(128)} %bitcast.n_ref, bf16[4,272,512]{2,1,0:T(8,128)(2,1)S(1)} %pad_maximum_fusion.1.x, bf16[128,1024]{1,0:T(8,128)(2,1)S(1)} %copy-done.2, bf16[128,1024]{1,0:T(8,128)(2,1)S(1)} %copy-done.3, bf16[1,1024]{1,0:T(2,128)(2,1)S(1)} %broadcast_in_dim.175.gain, ...), custom_call_target="tpu_custom_call" | custom-call | flops 1073741824 | bytes 12582912 | tf_op jit(solution)/shard_map/finish/pallas_call | solution.py:233
  174.9 2.1 convolution_convert_fusion
  177.0 2.1 convolution_convert_fusion.1
  179.7 2.8 %collective-permute-start.24 = (bf16[4,2,56,512]{3,2,1,0:T(8,128)(2,1)S(1)}, bf16[4,2,56,512]{3,2,1,0:T(8,128)(2,1)S(1)}, u32[]{:S(2)}, u32[]{:S(2)}) collective-permute-start(bf16[4,2,56,512]{3,2,1,0:T(8,128)(2,1)S(1)} %get-tuple-element.47), channel_id=1, source_target_pairs={{0,64},{1,17},{8,72},{9,25},{16,80},{17,1},{24,88},{25,9},{32,96},... | collective-permute-start | bytes 1376264 | tf_op jit(solution)/shard_map/ppermute | solution.py:314
  182.5 3.2 %collective-permute-start.26 = (bf16[4,2,56,512]{3,2,1,0:T(8,128)(2,1)S(1)}, bf16[4,2,56,512]{3,2,1,0:T(8,128)(2,1)S(1)}, u32[]{:S(2)}, u32[]{:S(2)}) collective-permute-start(bf16[4,2,56,512]{3,2,1,0:T(8,128)(2,1)S(1)} %get-tuple-element.49), channel_id=1, source_target_pairs={{0,96},{1,25},{8,104},{9,1},{16,112},{17,9},{24,120},{25,17},{32,0... | collective-permute-start | bytes 1376264 | tf_op jit(solution)/shard_map/ppermute | solution.py:314
  185.8 2.4 %add_convert_fusion.4 = bf16[4,256,512]{2,1,0:T(8,128)(2,1)S(1)} fusion(bf16[4,256,512]{2,1,0:T(8,128)(2,1)} %collective-permute-done.20, bf16[4,256,512]{2,1,0:T(8,128)(2,1)} %collective-permute-done.19, bf16[4,256,512]{2,1,0:T(8,128)(2,1)} %collective-permute-done.18, bf16[4,256,512]{2,1,0:T(8,128)(2,1)S(1)} %get-tuple-element.38), kind=kLoop, calls=%fused_computation.16 | loop fusion | flops 4194304 | bytes 5242880 | tf_op jit(solution)/shard_map/convert_element_type | solution.py:322
  188.3 4.0 %collective-permute-start.21 = (bf16[256,512]{1,0:T(8,128)(2,1)S(1)}, bf16[256,512]{1,0:T(8,128)(2,1)S(1)}, u32[]{:S(2)}, u32[]{:S(2)}) collective-permute-start(bf16[256,512]{1,0:T(8,128)(2,1)S(1)} %get-tuple-element.78), channel_id=1, source_target_pairs={{0,16},{1,65},{8,24},{9,73},{16,0},{17,81},{24,8},{25,89},{32,48},... | collective-permute-start | bytes 786440 | tf_op jit(solution)/shard_map/ppermute | solution.py:314
  192.9 2.7 %collective-permute-start.23 = (bf16[256,512]{1,0:T(8,128)(2,1)S(1)}, bf16[256,512]{1,0:T(8,128)(2,1)S(1)}, u32[]{:S(2)}, u32[]{:S(2)}) collective-permute-start(bf16[256,512]{1,0:T(8,128)(2,1)S(1)} %get-tuple-element.79), channel_id=1, source_target_pairs={{0,24},{1,97},{8,0},{9,105},{16,8},{17,113},{24,16},{25,121},{32,5... | collective-permute-start | bytes 786440 | tf_op jit(solution)/shard_map/ppermute | solution.py:314
  195.5 3.1 %collective-permute-done.25 = bf16[4,2,56,512]{3,2,1,0:T(8,128)(2,1)S(1)} collective-permute-done((bf16[4,2,56,512]{3,2,1,0:T(8,128)(2,1)S(1)}, bf16[4,2,56,512]{3,2,1,0:T(8,128)(2,1)S(1)}, u32[]{:S(2)}, u32[]{:S(2)}) %collective-permute-start.25) | collective-permute-done | bytes 458784 | tf_op jit(solution)/shard_map/ppermute | solution.py:314
  199.6 5.6 %collective-permute-start.27 = (bf16[2,56,512]{2,1,0:T(8,128)(2,1)}, bf16[2,56,512]{2,1,0:T(8,128)(2,1)S(1)}, u32[]{:S(2)}, u32[]{:S(2)}) collective-permute-start(bf16[2,56,512]{2,1,0:T(8,128)(2,1)} %get-tuple-element.84), channel_id=1, source_target_pairs={{0,16},{1,65},{8,24},{9,73},{16,0},{17,81},{24,8},{25,89},{32,48},... | collective-permute-start | bytes 344072 | tf_op jit(solution)/shard_map/ppermute | solution.py:314
  205.2 3.2 %collective-permute-start.29 = (bf16[2,56,512]{2,1,0:T(8,128)(2,1)S(1)}, bf16[2,56,512]{2,1,0:T(8,128)(2,1)}, u32[]{:S(2)}, u32[]{:S(2)}) collective-permute-start(bf16[2,56,512]{2,1,0:T(8,128)(2,1)S(1)} %get-tuple-element.85), channel_id=1, source_target_pairs={{0,24},{1,97},{8,0},{9,105},{16,8},{17,113},{24,16},{25,121},{32,5... | collective-permute-start | bytes 344072 | tf_op jit(solution)/shard_map/ppermute | solution.py:314
  208.6 1.0 copy.41
  209.6 1.6 collective-permute-done.28
  (132 shorter events, 14.1 us)
Async XLA Ops:
  7.2 25.3 %copy-start = (bf16[1024,896]{1,0:T(8,128)(2,1)S(1)}, bf16[1024,896]{1,0:T(8,128)(2,1)}, u32[]{:S(2)}) copy-start(bf16[1024,896]{1,0:T(8,128)(2,1)} %param.18) | copy-start | bytes 5505028
  7.2 50.3 %copy-start.9 = (bf16[6,128,896]{2,1,0:T(8,128)(2,1)S(1)}, bf16[6,128,896]{2,1,0:T(8,128)(2,1)}, u32[]{:S(2)}) copy-start(bf16[6,128,896]{2,1,0:T(8,128)(2,1)} %param.14) | copy-start | bytes 4128772
  7.2 24.4 %copy-start.2 = (bf16[128,1024]{1,0:T(8,128)(2,1)S(1)}, bf16[128,1024]{1,0:T(8,128)(2,1)}, u32[]{:S(2)}) copy-start(bf16[128,1024]{1,0:T(8,128)(2,1)} %hid.1) | copy-start | bytes 786436
  7.2 24.0 %copy-start.13 = (s32[24]{0:T(128)S(1)}, s32[24]{0:T(128)}, u32[]{:S(2)}) copy-start(s32[24]{0:T(128)} %param.15) | copy-start | bytes 292
  7.2 30.4 %copy-start.11 = (bf16[1024]{0:T(1024)(128)(2,1)S(1)}, bf16[1024]{0:T(1024)(128)(2,1)}, u32[]{:S(2)}) copy-start(bf16[1024]{0:T(1024)(128)(2,1)} %param.16) | copy-start | bytes 6148
  7.2 30.4 %copy-start.12 = (bf16[896]{0:T(1024)(128)(2,1)S(1)}, bf16[896]{0:T(1024)(128)(2,1)}, u32[]{:S(2)}) copy-start(bf16[896]{0:T(1024)(128)(2,1)} %param.17) | copy-start | bytes 5380
  7.2 84.5 %all-gather.3.cloned.1.call-start = ((), (), s32[]{:S(2)}) async-start(), calls=%async_computation.2 | async-start | bytes 10543104 | tf_op jit(solution)/shard_map/all_gather | solution.py:358
  10.3 1.5 collective-permute-start.8
  12.6 200.3 %reduce-scatter.2.cloned.1.call-start = ((), (), s32[]{:S(2)}) async-start(), calls=%async_computation.1 | async-start | bytes 6881280 | tf_op jit(solution)/shard_map/reduce_scatter | solution.py:420
  12.7 47.5 %collective-permute-start.4 = (bf16[6,128,896]{2,1,0:T(8,128)(2,1)}, bf16[6,128,896]{2,1,0:T(8,128)(2,1)}, u32[]{:S(2)}, u32[]{:S(2)}) collective-permute-start(bf16[6,128,896]{2,1,0:T(8,128)(2,1)} %param.14), channel_id=1, source_target_pairs={{0,6},{2,0},{4,2},{6,4},{1,7},{3,1},{5,3},{7,5},{8,14},{10,8},{12,... | collective-permute-start | bytes 4128776 | tf_op jit(solution)/shard_map/ppermute | solution.py:28
  26.3 33.9 %collective-permute-start.6 = (bf16[6,128,896]{2,1,0:T(8,128)(2,1)}, bf16[6,128,896]{2,1,0:T(8,128)(2,1)}, u32[]{:S(2)}, u32[]{:S(2)}) collective-permute-start(bf16[6,128,896]{2,1,0:T(8,128)(2,1)} %param.14), channel_id=1, source_target_pairs={{0,2},{2,4},{4,6},{6,0},{1,3},{3,5},{5,7},{7,1},{8,10},{10,12},{12... | collective-permute-start | bytes 4128776 | tf_op jit(solution)/shard_map/ppermute | solution.py:28
  27.3 5.1 %collective-permute-start = (bf16[1,1024]{1,0:T(2,128)(2,1)S(1)}, bf16[1,1024]{1,0:T(2,128)(2,1)S(1)}, u32[]{:S(2)}, u32[]{:S(2)}) collective-permute-start(bf16[1,1024]{1,0:T(2,128)(2,1)S(1)} %get-tuple-element.99), channel_id=1, source_target_pairs={{0,8},{8,16},{16,24},{24,32},{32,40},{40,48},{48,56},{56,64},{64,7... | collective-permute-start | bytes 6152 | tf_op jit(solution)/shard_map/ppermute | solution.py:366
  31.3 26.8 %copy-start.10 = (bf16[6,128,896]{2,1,0:T(8,128)(2,1)S(1)}, bf16[6,128,896]{2,1,0:T(8,128)(2,1)}, u32[]{:S(2)}) copy-start(bf16[6,128,896]{2,1,0:T(8,128)(2,1)} %param.14) | copy-start | bytes 4128772
  31.3 26.8 %copy-start.14 = (bf16[896,896]{1,0:T(8,128)(2,1)S(1)}, bf16[896,896]{1,0:T(8,128)(2,1)}, u32[]{:S(2)}) copy-start(bf16[896,896]{1,0:T(8,128)(2,1)} %param.19) | copy-start | bytes 4816900
  32.8 23.2 %collective-permute-start.1 = (f32[3,896]{1,0:T(4,128)S(1)}, f32[3,896]{1,0:T(4,128)S(1)}, u32[]{:S(2)}, u32[]{:S(2)}) collective-permute-start(f32[3,896]{1,0:T(4,128)S(1)} %pad_maximum_fusion.6), channel_id=1, source_target_pairs={{0,2},{2,4},{4,6},{6,0},{1,3},{3,5},{5,7},{7,1},{8,10},{10,12},{12... | collective-permute-start | bytes 32264 | tf_op jit(solution)/shard_map/ppermute | solution.py:28
  32.9 24.4 %collective-permute-start.2 = (f32[3,896]{1,0:T(4,128)S(1)}, f32[3,896]{1,0:T(4,128)S(1)}, u32[]{:S(2)}, u32[]{:S(2)}) collective-permute-start(f32[3,896]{1,0:T(4,128)S(1)} %pad_maximum_fusion.6), channel_id=1, source_target_pairs={{0,4},{2,6},{4,0},{6,2},{1,5},{3,7},{5,1},{7,3},{8,12},{10,14},{12... | collective-permute-start | bytes 32264 | tf_op jit(solution)/shard_map/ppermute | solution.py:28
  37.6 19.7 %collective-permute-start.3 = (f32[3,896]{1,0:T(4,128)S(1)}, f32[3,896]{1,0:T(4,128)S(1)}, u32[]{:S(2)}, u32[]{:S(2)}) collective-permute-start(f32[3,896]{1,0:T(4,128)S(1)} %pad_maximum_fusion.6), channel_id=1, source_target_pairs={{0,6},{2,0},{4,2},{6,4},{1,7},{3,1},{5,3},{7,5},{8,14},{10,8},{12,... | collective-permute-start | bytes 32264 | tf_op jit(solution)/shard_map/ppermute | solution.py:28
  58.1 2.1 copy-start.3
  60.2 21.2 %collective-permute-start.9 = (bf16[128,1024]{1,0:T(8,128)(2,1)S(1)}, bf16[128,1024]{1,0:T(8,128)(2,1)S(1)}, u32[]{:S(2)}, u32[]{:S(2)}) collective-permute-start(bf16[128,1024]{1,0:T(8,128)(2,1)S(1)} %copy-done.3), channel_id=1, source_target_pairs={{0,6},{2,0},{4,2},{6,4},{1,7},{3,1},{5,3},{7,5},{8,14},{10,8},{12,... | collective-permute-start | bytes 786440 | tf_op jit(solution)/shard_map/ppermute | solution.py:28
  60.7 20.8 %collective-permute-start.10 = (bf16[128,1024]{1,0:T(8,128)(2,1)S(1)}, bf16[128,1024]{1,0:T(8,128)(2,1)S(1)}, u32[]{:S(2)}, u32[]{:S(2)}) collective-permute-start(bf16[128,1024]{1,0:T(8,128)(2,1)S(1)} %copy-done.3), channel_id=1, source_target_pairs={{0,4},{2,6},{4,0},{6,2},{1,5},{3,7},{5,1},{7,3},{8,12},{10,14},{12... | collective-permute-start | bytes 786440 | tf_op jit(solution)/shard_map/ppermute | solution.py:28
  61.9 19.6 %collective-permute-start.11 = (bf16[128,1024]{1,0:T(8,128)(2,1)S(1)}, bf16[128,1024]{1,0:T(8,128)(2,1)S(1)}, u32[]{:S(2)}, u32[]{:S(2)}) collective-permute-start(bf16[128,1024]{1,0:T(8,128)(2,1)S(1)} %copy-done.3), channel_id=1, source_target_pairs={{0,2},{2,4},{4,6},{6,0},{1,3},{3,5},{5,7},{7,1},{8,10},{10,12},{12... | collective-permute-start | bytes 786440 | tf_op jit(solution)/shard_map/ppermute | solution.py:28
  63.5 22.7 %collective-permute-start.5 = (bf16[3,128,896]{2,1,0:T(8,128)(2,1)S(1)}, bf16[3,128,896]{2,1,0:T(8,128)(2,1)S(1)}, u32[]{:S(2)}, u32[]{:S(2)}) collective-permute-start(bf16[3,128,896]{2,1,0:T(8,128)(2,1)S(1)} %slice.137), channel_id=1, source_target_pairs={{0,6},{2,0},{4,2},{6,4},{1,7},{3,1},{5,3},{7,5},{8,14},{10,8},{12,... | collective-permute-start | bytes 2064392 | tf_op jit(solution)/shard_map/ppermute | solution.py:28
  67.6 20.6 %collective-permute-start.7 = (bf16[3,128,896]{2,1,0:T(8,128)(2,1)S(1)}, bf16[3,128,896]{2,1,0:T(8,128)(2,1)S(1)}, u32[]{:S(2)}, u32[]{:S(2)}) collective-permute-start(bf16[3,128,896]{2,1,0:T(8,128)(2,1)S(1)} %slice.138), channel_id=1, source_target_pairs={{0,2},{2,4},{4,6},{6,0},{1,3},{3,5},{5,7},{7,1},{8,10},{10,12},{12... | collective-permute-start | bytes 2064392 | tf_op jit(solution)/shard_map/ppermute | solution.py:28
  93.3 9.7 %copy-start.6 = (bf16[6,128,896]{2,1,0:T(8,128)(2,1)S(1)}, bf16[6,128,896]{2,1,0:T(8,128)(2,1)}, u32[]{:S(2)}) copy-start(bf16[6,128,896]{2,1,0:T(8,128)(2,1)} %add_convert_fusion.e3) | copy-start | bytes 4128772
  93.3 9.7 %copy-start.7 = (bf16[6,128,896]{2,1,0:T(8,128)(2,1)S(1)}, bf16[6,128,896]{2,1,0:T(8,128)(2,1)}, u32[]{:S(2)}) copy-start(bf16[6,128,896]{2,1,0:T(8,128)(2,1)} %add_convert_fusion.2.e1) | copy-start | bytes 4128772
  93.3 9.7 %copy-start.8 = (bf16[6,128,896]{2,1,0:T(8,128)(2,1)S(1)}, bf16[6,128,896]{2,1,0:T(8,128)(2,1)}, u32[]{:S(2)}) copy-start(bf16[6,128,896]{2,1,0:T(8,128)(2,1)} %add_convert_fusion.1.e2) | copy-start | bytes 4128772
  98.6 12.5 %collective-permute-start.12 = (bf16[256,512]{1,0:T(8,128)(2,1)S(1)}, bf16[256,512]{1,0:T(8,128)(2,1)S(1)}, u32[]{:S(2)}, u32[]{:S(2)}) collective-permute-start(bf16[256,512]{1,0:T(8,128)(2,1)S(1)} %get-tuple-element.81), channel_id=1, source_target_pairs={{0,4},{2,6},{4,0},{6,2},{1,5},{3,7},{5,1},{7,3},{8,12},{10,14},{12... | collective-permute-start | bytes 786440 | tf_op jit(solution)/shard_map/ppermute | solution.py:28
  99.8 13.0 %collective-permute-start.13 = (bf16[256,512]{1,0:T(8,128)(2,1)S(1)}, bf16[256,512]{1,0:T(8,128)(2,1)S(1)}, u32[]{:S(2)}, u32[]{:S(2)}) collective-permute-start(bf16[256,512]{1,0:T(8,128)(2,1)S(1)} %get-tuple-element.83), channel_id=1, source_target_pairs={{0,2},{2,4},{4,6},{6,0},{1,3},{3,5},{5,7},{7,1},{8,10},{10,12},{12... | collective-permute-start | bytes 786440 | tf_op jit(solution)/shard_map/ppermute | solution.py:28
  100.2 12.6 %collective-permute-start.14 = (bf16[256,512]{1,0:T(8,128)(2,1)S(1)}, bf16[256,512]{1,0:T(8,128)(2,1)S(1)}, u32[]{:S(2)}, u32[]{:S(2)}) collective-permute-start(bf16[256,512]{1,0:T(8,128)(2,1)S(1)} %get-tuple-element.82), channel_id=1, source_target_pairs={{0,6},{2,0},{4,2},{6,4},{1,7},{3,1},{5,3},{7,5},{8,14},{10,8},{12,... | collective-permute-start | bytes 786440 | tf_op jit(solution)/shard_map/ppermute | solution.py:28
  137.3 6.2 %copy-start.4 = (bf16[4,256,512]{2,1,0:T(8,128)(2,1)}, bf16[4,256,512]{2,1,0:T(8,128)(2,1)S(1)}, u32[]{:S(2)}) copy-start(bf16[4,256,512]{2,1,0:T(8,128)(2,1)S(1)} %get-tuple-element.41) | copy-start | bytes 3145732
  137.3 37.5 %collective-permute-start.19 = (bf16[4,256,512]{2,1,0:T(8,128)(2,1)}, bf16[4,256,512]{2,1,0:T(8,128)(2,1)}, u32[]{:S(2)}, u32[]{:S(2)}) collective-permute-start(bf16[4,256,512]{2,1,0:T(8,128)(2,1)} %get-tuple-element.40), channel_id=1, source_target_pairs={{0,32},{1,9},{8,40},{9,17},{16,48},{17,25},{24,56},{25,1},{32,64},... | collective-permute-start | bytes 3145736 | tf_op jit(solution)/shard_map/ppermute | solution.py:314
  141.4 15.5 %collective-permute-start.15 = (bf16[272,512]{1,0:T(8,128)(2,1)S(1)}, bf16[272,512]{1,0:T(8,128)(2,1)S(1)}, u32[]{:S(2)}, u32[]{:S(2)}) collective-permute-start(bf16[272,512]{1,0:T(8,128)(2,1)S(1)} %get-tuple-element.88), channel_id=1, source_target_pairs={{0,6},{2,0},{4,2},{6,4},{1,7},{3,1},{5,3},{7,5},{8,14},{10,8},{12,... | collective-permute-start | bytes 835592 | tf_op jit(solution)/shard_map/ppermute | solution.py:28
  142.3 17.1 %collective-permute-start.16 = (bf16[272,512]{1,0:T(8,128)(2,1)S(1)}, bf16[272,512]{1,0:T(8,128)(2,1)}, u32[]{:S(2)}, u32[]{:S(2)}) collective-permute-start(bf16[272,512]{1,0:T(8,128)(2,1)S(1)} %get-tuple-element.88), channel_id=1, source_target_pairs={{0,4},{2,6},{4,0},{6,2},{1,5},{3,7},{5,1},{7,3},{8,12},{10,14},{12... | collective-permute-start | bytes 835592 | tf_op jit(solution)/shard_map/ppermute | solution.py:28
  142.6 23.5 %collective-permute-start.17 = (bf16[272,512]{1,0:T(8,128)(2,1)S(1)}, bf16[272,512]{1,0:T(8,128)(2,1)}, u32[]{:S(2)}, u32[]{:S(2)}) collective-permute-start(bf16[272,512]{1,0:T(8,128)(2,1)S(1)} %get-tuple-element.88), channel_id=1, source_target_pairs={{0,2},{2,4},{4,6},{6,0},{1,3},{3,5},{5,7},{7,1},{8,10},{10,12},{12... | collective-permute-start | bytes 835592 | tf_op jit(solution)/shard_map/ppermute | solution.py:28
  143.6 42.2 %collective-permute-start.18 = (bf16[4,256,512]{2,1,0:T(8,128)(2,1)}, bf16[4,256,512]{2,1,0:T(8,128)(2,1)}, u32[]{:S(2)}, u32[]{:S(2)}) collective-permute-start(bf16[4,256,512]{2,1,0:T(8,128)(2,1)} %copy-done.5), channel_id=1, source_target_pairs={{0,64},{1,17},{8,72},{9,25},{16,80},{17,1},{24,88},{25,9},{32,96},... | collective-permute-start | bytes 3145736 | tf_op jit(solution)/shard_map/ppermute | solution.py:314
  156.9 28.9 %collective-permute-start.20 = (bf16[4,256,512]{2,1,0:T(8,128)(2,1)}, bf16[4,256,512]{2,1,0:T(8,128)(2,1)}, u32[]{:S(2)}, u32[]{:S(2)}) collective-permute-start(bf16[4,256,512]{2,1,0:T(8,128)(2,1)} %copy-done.4), channel_id=1, source_target_pairs={{0,96},{1,25},{8,104},{9,1},{16,112},{17,9},{24,120},{25,17},{32,0... | collective-permute-start | bytes 3145736 | tf_op jit(solution)/shard_map/ppermute | solution.py:314
  167.4 7.4 %copy-start.15 = (bf16[16,128,896]{2,1,0:T(8,128)(2,1)S(1)}, bf16[16,128,896]{2,1,0:T(8,128)(2,1)}, u32[]{:S(2)}) copy-start(bf16[16,128,896]{2,1,0:T(8,128)(2,1)} %get-tuple-element.43) | copy-start | bytes 11010052
  167.4 7.4 %copy-start.17 = (bf16[2048,512]{1,0:T(8,128)(2,1)S(1)}, bf16[2048,512]{1,0:T(8,128)(2,1)}, u32[]{:S(2)}) copy-start(bf16[2048,512]{1,0:T(8,128)(2,1)} %get-tuple-element.45) | copy-start | bytes 6291460
  179.7 13.1 %collective-permute-start.24 = (bf16[4,2,56,512]{3,2,1,0:T(8,128)(2,1)S(1)}, bf16[4,2,56,512]{3,2,1,0:T(8,128)(2,1)S(1)}, u32[]{:S(2)}, u32[]{:S(2)}) collective-permute-start(bf16[4,2,56,512]{3,2,1,0:T(8,128)(2,1)S(1)} %get-tuple-element.47), channel_id=1, source_target_pairs={{0,64},{1,17},{8,72},{9,25},{16,80},{17,1},{24,88},{25,9},{32,96},... | collective-permute-start | bytes 1376264 | tf_op jit(solution)/shard_map/ppermute | solution.py:314
  182.5 16.2 %collective-permute-start.25 = (bf16[4,2,56,512]{3,2,1,0:T(8,128)(2,1)S(1)}, bf16[4,2,56,512]{3,2,1,0:T(8,128)(2,1)S(1)}, u32[]{:S(2)}, u32[]{:S(2)}) collective-permute-start(bf16[4,2,56,512]{3,2,1,0:T(8,128)(2,1)S(1)} %get-tuple-element.48), channel_id=1, source_target_pairs={{0,32},{1,9},{8,40},{9,17},{16,48},{17,25},{24,56},{25,1},{32,64},... | collective-permute-start | bytes 1376264 | tf_op jit(solution)/shard_map/ppermute | solution.py:314
  182.5 16.2 %collective-permute-start.26 = (bf16[4,2,56,512]{3,2,1,0:T(8,128)(2,1)S(1)}, bf16[4,2,56,512]{3,2,1,0:T(8,128)(2,1)S(1)}, u32[]{:S(2)}, u32[]{:S(2)}) collective-permute-start(bf16[4,2,56,512]{3,2,1,0:T(8,128)(2,1)S(1)} %get-tuple-element.49), channel_id=1, source_target_pairs={{0,96},{1,25},{8,104},{9,1},{16,112},{17,9},{24,120},{25,17},{32,0... | collective-permute-start | bytes 1376264 | tf_op jit(solution)/shard_map/ppermute | solution.py:314
  188.3 17.0 %collective-permute-start.21 = (bf16[256,512]{1,0:T(8,128)(2,1)S(1)}, bf16[256,512]{1,0:T(8,128)(2,1)S(1)}, u32[]{:S(2)}, u32[]{:S(2)}) collective-permute-start(bf16[256,512]{1,0:T(8,128)(2,1)S(1)} %get-tuple-element.78), channel_id=1, source_target_pairs={{0,16},{1,65},{8,24},{9,73},{16,0},{17,81},{24,8},{25,89},{32,48},... | collective-permute-start | bytes 786440 | tf_op jit(solution)/shard_map/ppermute | solution.py:314
  192.3 16.2 %collective-permute-start.22 = (bf16[256,512]{1,0:T(8,128)(2,1)S(1)}, bf16[256,512]{1,0:T(8,128)(2,1)S(1)}, u32[]{:S(2)}, u32[]{:S(2)}) collective-permute-start(bf16[256,512]{1,0:T(8,128)(2,1)S(1)} %get-tuple-element.80), channel_id=1, source_target_pairs={{0,8},{1,33},{8,16},{9,41},{16,24},{17,49},{24,0},{25,57},{32,40},... | collective-permute-start | bytes 786440 | tf_op jit(solution)/shard_map/ppermute | solution.py:314
  192.9 15.6 %collective-permute-start.23 = (bf16[256,512]{1,0:T(8,128)(2,1)S(1)}, bf16[256,512]{1,0:T(8,128)(2,1)S(1)}, u32[]{:S(2)}, u32[]{:S(2)}) collective-permute-start(bf16[256,512]{1,0:T(8,128)(2,1)S(1)} %get-tuple-element.79), channel_id=1, source_target_pairs={{0,24},{1,97},{8,0},{9,105},{16,8},{17,113},{24,16},{25,121},{32,5... | collective-permute-start | bytes 786440 | tf_op jit(solution)/shard_map/ppermute | solution.py:314
  198.7 14.2 %copy-start.1 = (bf16[1024,896]{1,0:T(8,128)(2,1)S(1)}, bf16[1024,896]{1,0:T(8,128)(2,1)}, u32[]{:S(2)}) copy-start(bf16[1024,896]{1,0:T(8,128)(2,1)} %param.18) | copy-start | bytes 5505028
  199.6 10.0 %collective-permute-start.27 = (bf16[2,56,512]{2,1,0:T(8,128)(2,1)}, bf16[2,56,512]{2,1,0:T(8,128)(2,1)S(1)}, u32[]{:S(2)}, u32[]{:S(2)}) collective-permute-start(bf16[2,56,512]{2,1,0:T(8,128)(2,1)} %get-tuple-element.84), channel_id=1, source_target_pairs={{0,16},{1,65},{8,24},{9,73},{16,0},{17,81},{24,8},{25,89},{32,48},... | collective-permute-start | bytes 344072 | tf_op jit(solution)/shard_map/ppermute | solution.py:314
  205.2 6.0 %collective-permute-start.28 = (bf16[2,56,512]{2,1,0:T(8,128)(2,1)S(1)}, bf16[2,56,512]{2,1,0:T(8,128)(2,1)S(1)}, u32[]{:S(2)}, u32[]{:S(2)}) collective-permute-start(bf16[2,56,512]{2,1,0:T(8,128)(2,1)S(1)} %get-tuple-element.86), channel_id=1, source_target_pairs={{0,8},{1,33},{8,16},{9,41},{16,24},{17,49},{24,0},{25,57},{32,40},... | collective-permute-start | bytes 344072 | tf_op jit(solution)/shard_map/ppermute | solution.py:314
  205.2 6.0 %collective-permute-start.29 = (bf16[2,56,512]{2,1,0:T(8,128)(2,1)S(1)}, bf16[2,56,512]{2,1,0:T(8,128)(2,1)}, u32[]{:S(2)}, u32[]{:S(2)}) collective-permute-start(bf16[2,56,512]{2,1,0:T(8,128)(2,1)S(1)} %get-tuple-element.85), channel_id=1, source_target_pairs={{0,24},{1,97},{8,0},{9,105},{16,8},{17,113},{24,16},{25,121},{32,5... | collective-permute-start | bytes 344072 | tf_op jit(solution)/shard_map/ppermute | solution.py:314
  (2 other events, 3.1 us)
Sparse Core Ops, SparseCore 0:
  12.7 69.6 all-gather.2
  130.6 70.4 reduce-scatter.1

commit v4 on v3

--- a/solution.py
+++ b/solution.py
@@ -91,8 +91,8 @@
     )(n, normed, dout, weights, weights)
 
 
-def keys_kernel(tab, e0, e1, e2, e3, wk, wv, enc, kb, vb):
-    tables = ((e0, 0), (e1, 6), (e2, 12), (e3, 18))
+def keys_kernel(tab, e0, near, far, wk, wv, enc, kb, vb):
+    tables = ((e0, 0, 6, 0), (near, 6, 12, 0), (far, 12, 18, 0), (near, 18, 24, 6))
 
     def pick(j, carry):
         src = tab[j]
@@ -101,11 +101,11 @@
         def _():
             enc[j] = jnp.zeros(enc.shape[1:], BF16)
 
-        for ref, first in tables:
-
-            @pl.when((src >= first) & (src < first + ref.shape[0]))
-            def _(ref=ref, first=first):
-                enc[j] = ref[src - first]
+        for ref, first, end, base in tables:
+
+            @pl.when((src >= first) & (src < end))
+            def _(ref=ref, first=first, base=base):
+                enc[j] = ref[src - first + base]
 
         return carry
 
@@ -126,7 +126,7 @@
     flat = jax.ShapeDtypeStruct((rows, wk.shape[1]), BF16)
     return pl.pallas_call(
         keys_kernel,
-        in_specs=[SMEM] + [VMEM] * 6,
+        in_specs=[SMEM] + [VMEM] * 5,
         out_specs=[VMEM] * 3,
         out_shape=[pltpu.HBM((2 * KMAX, NLEN, wk.shape[0]), BF16), flat, flat],
         cost_estimate=cost(2048 * 896 * 1024, 16 << 20),
@@ -255,50 +255,34 @@
     )(n, x, hidden, dout, gain[None], rstd, stat, weights, weights)
 
 
-def outer_kernel(dest, n_ref, d, ctx, o0, o1, o2, o3):
+def pack_kernel(dest, n_ref, d, ctx, wk, wv, o0, o1, o2, o3):
+    rows = wk.shape[1]
     for i, out in enumerate((o0, o1, o2, o3)):
 
         def share(j, carry, i=i, out=out):
             to = dest[4 * i + j]
             block = lax.rem(to // 4 + 4 - n_ref[0], 4)
             first = pl.multiple_of(lax.rem(to, 4) * 256, 256)
-            out[j] = dot(d[block, :, pl.ds(first, 256)], ctx[...], TN).astype(BF16)
+            part = dot(d[block, :, pl.ds(first, 256)], ctx[...], TN)
+            out[j, 0:256] = part.astype(BF16)
+            out[j, 256 : 256 + rows] = wk[to]
+            out[j, 320 : 320 + rows] = wv[to]
             return carry
 
         lax.fori_loop(0, 4, share, 0)
 
 
-def outer(dest, n, dout, ctx):
-    share = jax.ShapeDtypeStruct((4, 256, ctx.shape[1]), BF16)
+def pack(dest, n, dout, ctx, wk, wv):
+    share = jax.ShapeDtypeStruct((4, 384, ctx.shape[1]), BF16)
     return pl.pallas_call(
-        outer_kernel,
-        in_specs=[SMEM, SMEM, VMEM, VMEM],
+        pack_kernel,
+        in_specs=[SMEM, SMEM, VMEM, VMEM, VMEM, VMEM],
         out_specs=[VMEM] * 4,
         out_shape=[share] * 4,
-        cost_estimate=cost(ctx.shape[0] * 4096 * 512, 6 << 20),
-        compiler_params=pltpu.CompilerParams(vmem_limit_bytes=16 << 20),
-        name="outer",
-    )(dest, n, dout, ctx)
-
-
-def order_kernel(dest, wk, wv, o0, o1, o2, o3):
-    for i, out in enumerate((o0, o1, o2, o3)):
-        for j in range(4):
-            out[j, 0] = wk[dest[4 * i + j]]
-            out[j, 1] = wv[dest[4 * i + j]]
-
-
-def order(dest, wk, wv):
-    share = jax.ShapeDtypeStruct((4, 2) + wk.shape[1:], BF16)
-    return pl.pallas_call(
-        order_kernel,
-        in_specs=[SMEM, VMEM, VMEM],
-        out_specs=[VMEM] * 4,
-        out_shape=[share] * 4,
-        cost_estimate=cost(0, 4 << 20),
-        compiler_params=pltpu.CompilerParams(vmem_limit_bytes=16 << 20),
-        name="order",
-    )(dest, wk, wv)
+        cost_estimate=cost(ctx.shape[0] * 4096 * 512, 16 << 20),
+        compiler_params=pltpu.CompilerParams(vmem_limit_bytes=24 << 20),
+        name="pack",
+    )(dest, n, dout, ctx, wk, wv)
 
 
 def along(share, by, first):
@@ -318,8 +302,7 @@
     return [shares[0]] + [along(shares[i], i, True) for i in (2, 1, 3)]
 
 
-def second_phase(arrived):
-    near = total(arrived).astype(BF16)
+def second_phase(near):
     return total([near[0]] + [along(near[j], j, False) for j in (2, 1, 3)])
 
 
@@ -382,15 +365,11 @@
 
     nbr_emb = lax.optimization_barrier((nbr_emb, condition))[0]
     e1, e2a, e2b, e3 = ring_gather(nbr_emb)
-    later = lax.optimization_barrier((d_out, e1, e3))[0]
-    d2, d1, d3 = (shift(later, r) for r in (2, -1, 1))
-    dout_rel = jnp.stack([d_out, d1, d2, d3])
 
     tab, inv = slot_tables(slot_span, n)
     rel_span = jnp.roll(slot_span.reshape(4, 6), -n, axis=0).reshape(-1)
 
-    def encode(block, first):
-        own = lax.slice_in_dim(rel_span, first, first + block.shape[0])
+    def encode(block, own):
         own = own[:, None, None]
         cond = jnp.where(own == 0, condition[0], jnp.where(own == 1, condition[1], 0.0))
         x = block.astype(F32) + cond
@@ -407,25 +386,25 @@
     wk = pairs[:, 0, 256:].reshape(-1, 512)
     wv = pairs[:, 1, 256:].reshape(-1, 512)
 
-    normed, dout_rel = lax.optimization_barrier((normed, dout_rel))
-    shares = scattered(project(n1, normed, d_out, weights))
-    both = total(shares).astype(BF16)
+    shares = project(n1, normed, d_out, weights)
+    both = total(scattered(shares)).astype(BF16)
+    later = lax.optimization_barrier((d_out, both))[0]
+    d2, d1, d3 = (shift(later, r) for r in (2, -1, 1))
     query, d_ctx = both[:tokens], both[tokens:]
-    e2 = jnp.concatenate([e2a, e2b], axis=0)
-    encoded = [encode(nbr_emb, 0), encode(e1, 6), encode(e2, 12), encode(e3, 18)]
+    near = jnp.concatenate([e1, e3], axis=0)
+    far = jnp.concatenate([e2a, e2b], axis=0)
+    encoded = [
+        encode(nbr_emb, rel_span[:6]),
+        encode(near, jnp.concatenate([rel_span[6:12], rel_span[18:]])),
+        encode(far, rel_span[12:18]),
+    ]
     enc, keys, values = keys_values(tab, encoded, wk, wv)
     ctx, d_query, d_key, d_value, parts = attend(
         tab, inv, keys, values, query, d_ctx, wk, wv
     )
+    parts, d1, d2, d3 = lax.optimization_barrier((parts, d1, d2, d3))
+    dout_rel = jnp.stack([d_out, d1, d2, d3])
     d_enc = lax.psum_scatter(parts, "nbr", scatter_dimension=0, tiled=True)
-
-    inner = jnp.sum(d_query.astype(F32) * query.astype(F32), axis=-1).astype(BF16)
-    more = jnp.broadcast_to(jnp.pad(inner, (0, ctx.shape[1] - tokens))[None], (16, ctx.shape[1]))
-    local = jnp.concatenate([ctx, d_query, more], axis=0)
-    heads = jnp.stack([local, shift(local, -1), shift(local, 2), shift(local, 1)])
-    stat = jnp.sum(heads[:, 2 * tokens, :tokens].astype(F32), axis=0)[:, None]
-    stat = stat / (rstd * (4 * feats))
-    out, d_hidden = finish(n1, heads, hidden, d_out, dec_gain, rstd, stat, weights)
 
     place = lax.axis_index("seq")
     step = jnp.arange(4, dtype=jnp.int32)
@@ -433,15 +412,23 @@
     by_x, by_z = jnp.where(b == 0, one, two), jnp.where(b == 0, two, one)
     dest = (place // 4 + by_x) % 4 * 4 + (place % 4 + by_z) % 4
     dest = dest.astype(jnp.int32).reshape(-1)
-    arrived = first_phase(outer(dest, n1, dout_rel, ctx))
-    d_wo = second_phase(arrived).T
-
-    enc = lax.optimization_barrier((enc, arrived[2]))[0]
     rows = enc.reshape(-1, enc.shape[2])
     wk_parts = dot(rows, d_key, TN).astype(BF16).reshape(16, -1, 512)
     wv_parts = dot(rows, d_value, TN).astype(BF16).reshape(16, -1, 512)
-    both = second_phase(first_phase(order(dest, wk_parts, wv_parts)))
-    d_wk, d_wv = both[0], both[1]
+    arrived = first_phase(pack(dest, n1, dout_rel, ctx, wk_parts, wv_parts))
+    near = total(arrived).astype(BF16)
+    whole = second_phase(near)
+    d_wo = whole[:256].T
+    d_wk, d_wv = whole[256:312], whole[320:376]
+
+    inner = jnp.sum(d_query.astype(F32) * query.astype(F32), axis=-1).astype(BF16)
+    more = jnp.broadcast_to(jnp.pad(inner, (0, ctx.shape[1] - tokens))[None], (16, ctx.shape[1]))
+    local = jnp.concatenate([ctx, d_query, more], axis=0)
+    heads = jnp.stack([local, shift(local, -1), shift(local, 2), shift(local, 1)])
+    heads = lax.optimization_barrier((heads, near))[0]
+    stat = jnp.sum(heads[:, 2 * tokens, :tokens].astype(F32), axis=0)[:, None]
+    stat = stat / (rstd * (4 * feats))
+    out, d_hidden = finish(n1, heads, hidden, d_out, dec_gain, rstd, stat, weights)
 
     return (out, d_hidden, d_enc, d_wo, d_wk, d_wv)
 

time: 224 us -> 213 us (0.951); the launches traced: 220 us -> 213 us
  starting transfers between devices: 62.2 us -> 48.9 us
    ppermute x12 -> x6, starting transfers between devices: 27.6 us -> 10.6 us  [along(): return lax.ppermute(share, ('seq', 'batch'), pairs)]
    ppermute x16, waiting for transfers between devices: 48.8 us -> 52.6 us  [shift(): return lax.ppermute(x, 'nbr', [(i, (i + by) % n) for i in range(n)])]
    ppermute x16, starting transfers between devices: 30 us -> 33.8 us  [shift(): return lax.ppermute(x, 'nbr', [(i, (i + by) % n) for i in range(n)])]
    dot_general x2, matrix products: 4.16 us -> 7.01 us  [dot(): return lax.dot_general(a, b, (dims, ((), ())), preferred_element_type=F32)]
    ppermute x12 -> x6, waiting for transfers between devices: 4.8 us -> 2.2 us  [along(): return lax.ppermute(share, ('seq', 'batch'), pairs)]
    dot_general x4 -> x3, matrix products: 15.2 us -> 13.3 us  [encode(): jnp.dot(enc_normed.reshape(-1, width), w_enc, preferred_element_type=F32)]
    unnamed x38 -> x48, local copies, waits for them, and re-layouts: 4 us -> 5.57 us
    reduce_sum x4 -> x3, other arithmetic: 4.5 us -> 3.45 us  [rms_scale(): return lax.rsqrt(jnp.mean(values * values, axis=-1, keepdims=True) + 1e-06)]
  transfers between devices with their start and end apart: 32 -> 26, of which waited for: 11 -> 12; matrix products, arithmetic and copies ran while one was open for 17% -> 19% of each run, Pallas kernels for 10% -> 19%
where the time goes in v4:
time: 213 us
  waiting for transfers between devices  56.4 us (26%)
  starting transfers between devices  48.9 us (23%)
  Pallas kernels  45 us (21%)
  matrix products  20.7 us (10%)
  other arithmetic  15.4 us (7%)
  between operations  14.6 us (7%)
  local copies, waits for them, and re-layouts  11.9 us (6%)
    ppermute x16, waiting for transfers between devices, shift(): return lax.ppermute(x, 'nbr', [(i, (i + by) % n) for i in range(n)])  52.6 us
    ppermute x16, starting transfers between devices, shift(): return lax.ppermute(x, 'nbr', [(i, (i + by) % n) for i in range(n)])  33.8 us
    pallas_call x1, Pallas kernels, attend(): pl.pallas_call(attend_kernel, in_specs=[SMEM, SMEM] + [VMEM] * 6, out_spe...  17.5 us
    dot_general x3, matrix products, encode(): jnp.dot(enc_normed.reshape(-1, width), w_enc, preferred_element_type=F32)  13.3 us
    ppermute x6, starting transfers between devices, along(): return lax.ppermute(share, ('seq', 'batch'), pairs)  10.6 us
    pallas_call x1, Pallas kernels, keys_values(): pl.pallas_call(keys_kernel, in_specs=[SMEM] + [VMEM] * 5, out_specs=[VMEM...  8.07 us
    pallas_call x1, Pallas kernels, finish(): pl.pallas_call(finish_kernel, grid_spec=pltpu.PrefetchScalarGridSpec(num_...  7.1 us
    dot_general x2, matrix products, dot(): return lax.dot_general(a, b, (dims, ((), ())), preferred_element_type=F32)  7.01 us
  transfers between devices with their start and end apart: 26, of which 12 were waited for; matrix products, arithmetic and copies ran while one was open for 19% of the time, Pallas kernels for 19%

profile of v4, /device:TPU:0, one launch (start us, length us, event | category | flops | bytes accessed | tf_op | source)
XLA Modules:
  0.0 212.9 jit_solution(7830147623629443421)
XLA Ops:
  7.3 1.2 copy.36
  8.5 1.0 bitcast_select_fusion
  10.2 0.8 broadcast_select_fusion
  11.9 13.6 %collective-permute-start.4 = (bf16[6,128,896]{2,1,0:T(8,128)(2,1)}, bf16[6,128,896]{2,1,0:T(8,128)(2,1)}, u32[]{:S(2)}, u32[]{:S(2)}) collective-permute-start(bf16[6,128,896]{2,1,0:T(8,128)(2,1)} %param.14), channel_id=1, source_target_pairs={{0,6},{2,0},{4,2},{6,4},{1,7},{3,1},{5,3},{7,5},{8,14},{10,8},{12,... | collective-permute-start | bytes 4128776 | tf_op jit(solution)/shard_map/ppermute | solution.py:28
  25.5 1.0 bitcast_reduce_fusion
  26.5 3.8 %collective-permute-start = (bf16[1,1024]{1,0:T(2,128)(2,1)S(1)}, bf16[1,1024]{1,0:T(2,128)(2,1)S(1)}, u32[]{:S(2)}, u32[]{:S(2)}) collective-permute-start(bf16[1,1024]{1,0:T(2,128)(2,1)S(1)} %get-tuple-element.90), channel_id=1, source_target_pairs={{0,8},{8,16},{16,24},{24,32},{32,40},{40,48},{48,56},{56,64},{64,7... | collective-permute-start | bytes 6152 | tf_op jit(solution)/shard_map/ppermute | solution.py:349
  32.1 4.7 %collective-permute-start.2 = (f32[3,896]{1,0:T(4,128)S(1)}, f32[3,896]{1,0:T(4,128)S(1)}, u32[]{:S(2)}, u32[]{:S(2)}) collective-permute-start(f32[3,896]{1,0:T(4,128)S(1)} %pad_maximum_fusion.8), channel_id=1, source_target_pairs={{0,4},{2,6},{4,0},{6,2},{1,5},{3,7},{5,1},{7,3},{8,12},{10,14},{12... | collective-permute-start | bytes 32264 | tf_op jit(solution)/shard_map/ppermute | solution.py:28
  36.9 17.5 %collective-permute-done.1 = f32[3,896]{1,0:T(4,128)S(1)} collective-permute-done((f32[3,896]{1,0:T(4,128)S(1)}, f32[3,896]{1,0:T(4,128)S(1)}, u32[]{:S(2)}, u32[]{:S(2)}) %collective-permute-start.1) | collective-permute-done | bytes 10784 | tf_op jit(solution)/shard_map/ppermute | solution.py:28
  55.6 3.1 %add_convert_fusion.3.e0 = bf16[6,128,896]{2,1,0:T(8,128)(2,1)} fusion(bf16[6,128,896]{2,1,0:T(8,128)(2,1)S(1)} %copy-done.10, bf16[896,896]{1,0:T(8,128)(2,1)S(1)} %copy-done.20, f32[896]{0:T(1024)S(1)} %convert_element_type.134, f32[6,128]{1,0:T(8,128)S(1)} %add_rsqrt_fusion.2, f32[6,896]{1,0:T(8,128)S(1)} %get-tuple-element.89), kind=kOutput, calls=%fused_computation.14 | convolution fusion | flops 1242071040 | bytes 4386304 | tf_op jit(solution)/shard_map/dot_general | solution.py:378
  58.7 1.2 slice.123
  60.4 1.2 slice.124
  61.5 1.7 collective-permute-start.7
  63.3 2.6 %multiply_reduce_fusion = f32[12,128]{1,0:T(8,128)S(1)} fusion(f32[12,896]{1,0:T(8,128)S(1)} %select_select_fusion, bf16[6,128,896]{2,1,0:T(8,128)(2,1)} %collective-permute-done.5, bf16[6,128,896]{2,1,0:T(8,128)(2,1)} %collective-permute-done.4), kind=kLoop, calls=%fused_computation.2 | loop fusion | flops 6879744 | bytes 2801664 | tf_op jit(solution)/shard_map/reduce_sum | solution.py:53
  65.9 7.1 %add_convert_fusion.near = bf16[12,128,896]{2,1,0:T(8,128)(2,1)} fusion(f32[896]{0:T(1024)S(1)} %convert_element_type.134, f32[12,128]{1,0:T(8,128)S(1)} %add_rsqrt_fusion, f32[12,896]{1,0:T(8,128)S(1)} %select_select_fusion, bf16[6,128,896]{2,1,0:T(8,128)(2,1)} %collective-permute-done.5, bf16[6,128,896]{2,1,0:T(8,128)(2,1)} %collective-permute-done.4, ...), kind=kOutput, calls=%fused_computation | convolution fusion | flops 2486894592 | bytes 7163392 | tf_op jit(solution)/shard_map/dot_general | solution.py:378
  73.1 2.9 %collective-permute-done.7 = bf16[3,128,896]{2,1,0:T(8,128)(2,1)S(1)} collective-permute-done((bf16[3,128,896]{2,1,0:T(8,128)(2,1)S(1)}, bf16[3,128,896]{2,1,0:T(8,128)(2,1)S(1)}, u32[]{:S(2)}, u32[]{:S(2)}) %collective-permute-start.7) | collective-permute-done | bytes 688160 | tf_op jit(solution)/shard_map/ppermute | solution.py:28
  76.5 3.1 %add_convert_fusion.2.far = bf16[6,128,896]{2,1,0:T(8,128)(2,1)} fusion(bf16[896,896]{1,0:T(8,128)(2,1)S(1)} %copy-done.20, f32[6,128]{1,0:T(8,128)S(1)} %add_rsqrt_fusion.1, f32[6,896]{1,0:T(8,128)S(1)} %get-tuple-element.88, f32[896]{0:T(1024)S(1)} %convert_element_type.134, bf16[3,128,896]{2,1,0:T(8,128)(2,1)S(1)} %collective-permute-done.7, ...), kind=kOutput, calls=%fused_computation.7 | convolution fusion | flops 1243447296 | bytes 4386304 | tf_op jit(solution)/shard_map/dot_general | solution.py:378
  79.6 1.1 all-gather.3.cloned.1.call-done
  80.7 1.6 fusion.43
  82.4 5.5 %project.1 = bf16[4,256,512]{2,1,0:T(8,128)(2,1)S(1)} custom-call(s32[1]{0:T(128)} %bitcast.n_ref, bf16[128,1024]{1,0:T(8,128)(2,1)S(1)} %multiply_convert_fusion.12.x, bf16[128,1024]{1,0:T(8,128)(2,1)S(1)} %copy-done.3, bf16[16,2,312,512]{3,2,1,0:T(8,128)(2,1)} %bitcast.85, bf16[16,2,312,512]{3,2,1,0:T(8,128)(2,1)} %bitcast.86), custom_call_target="tpu_custom_call" | custom-call | flops 1073741824 | bytes 12582912 | tf_op jit(solution)/shard_map/project/pallas_call | solution.py:74
  88.0 1.6 collective-permute-start.10
  89.5 1.8 collective-permute-start.11
  91.3 1.8 collective-permute-start.9
  93.1 8.1 %keys_values.1 = (bf16[16,128,896]{2,1,0:T(8,128)(2,1)}, bf16[2048,512]{1,0:T(8,128)(2,1)S(1)}, bf16[2048,512]{1,0:T(8,128)(2,1)S(1)}) custom-call(s32[18]{0:T(128)S(1)} %pad_add_fusion.1.tab, bf16[6,128,896]{2,1,0:T(8,128)(2,1)S(1)} %copy-done.5, bf16[12,128,896]{2,1,0:T(8,128)(2,1)S(1)} %copy-done.4, bf16[6,128,896]{2,1,0:T(8,128)(2,1)S(1)} %copy-done.6, ...), custom_call_target="tpu_custom_call" | custom-call | flops 3758096384 | bytes 16777216 | tf_op jit(solution)/shard_map/keys_values/pallas_call | solution.py:127
  101.1 1.5 collective-permute-done.11
  102.7 1.6 collective-permute-done.9
  104.5 2.1 collective-permute-start.15
  106.6 1.2 collective-permute-start.16
  107.8 17.5 %attend.1 = (bf16[128,512]{1,0:T(8,128)(2,1)S(1)}, bf16[128,512]{1,0:T(8,128)(2,1)S(1)}, bf16[2048,512]{1,0:T(8,128)(2,1)}, bf16[2048,512]{1,0:T(8,128)(2,1)}, bf16[24,128,896]{2,1,0:T(8,128)(2,1)}) custom-call(s32[18]{0:T(128)S(1)} %pad_add_fusion.1.tab, s32[24]{0:T(128)S(1)} %get-tuple-element.100.inv, bf16[2048,512]{1,0:T(8,128)(2,1)S(1)} %get-tuple-element.26.kb, ...), custom_call_target="tpu_custom_call" | custom-call | flops 3758096384 | bytes 41943040 | tf_op jit(solution)/shard_map/attend/pallas_call | solution.py:190
  127.0 4.9 %convolution_convert_fusion = bf16[896,512]{1,0:T(8,128)(2,1)S(1)} fusion(bf16[2048,896]{1,0:T(8,128)(2,1)} %bitcast.95, bf16[2048,512]{1,0:T(8,128)(2,1)} %get-tuple-element.37), kind=kOutput, calls=%fused_computation.23 | convolution fusion | flops 1879506944 | bytes 6684672 | tf_op jit(solution)/shard_map/dot_general | solution.py:19
  132.0 2.1 convolution_convert_fusion.1
  134.2 6.7 %pack.1 = (bf16[4,384,512]{2,1,0:T(8,128)(2,1)S(1)}, bf16[4,384,512]{2,1,0:T(8,128)(2,1)}, bf16[4,384,512]{2,1,0:T(8,128)(2,1)}, bf16[4,384,512]{2,1,0:T(8,128)(2,1)}) custom-call(s32[16]{0:T(128)S(1)} %fusion.30.dest, s32[1]{0:T(128)} %bitcast.n_ref, bf16[4,128,1024]{2,1,0:T(8,128)(2,1)S(1)} %pad_maximum_fusion.4.d, ...), custom_call_target="tpu_custom_call" | custom-call | flops 536870912 | bytes 16777216 | tf_op jit(solution)/shard_map/pack/pallas_call | solution.py:277
  141.0 3.0 %collective-permute-start.18 = (bf16[4,384,512]{2,1,0:T(8,128)(2,1)}, bf16[4,384,512]{2,1,0:T(8,128)(2,1)}, u32[]{:S(2)}, u32[]{:S(2)}) collective-permute-start(bf16[4,384,512]{2,1,0:T(8,128)(2,1)} %get-tuple-element.39), channel_id=1, source_target_pairs={{0,64},{1,17},{8,72},{9,25},{16,80},{17,1},{24,88},{25,9},{32,96},... | collective-permute-start | bytes 4718600 | tf_op jit(solution)/shard_map/ppermute | solution.py:298
  144.5 2.7 %collective-permute-start.20 = (bf16[4,384,512]{2,1,0:T(8,128)(2,1)}, bf16[4,384,512]{2,1,0:T(8,128)(2,1)}, u32[]{:S(2)}, u32[]{:S(2)}) collective-permute-start(bf16[4,384,512]{2,1,0:T(8,128)(2,1)} %get-tuple-element.41), channel_id=1, source_target_pairs={{0,96},{1,25},{8,104},{9,1},{16,112},{17,9},{24,120},{25,17},{32,0... | collective-permute-start | bytes 4718600 | tf_op jit(solution)/shard_map/ppermute | solution.py:298
  148.1 3.2 %collective-permute-start.12 = (bf16[272,512]{1,0:T(8,128)(2,1)S(1)}, bf16[272,512]{1,0:T(8,128)(2,1)}, u32[]{:S(2)}, u32[]{:S(2)}) collective-permute-start(bf16[272,512]{1,0:T(8,128)(2,1)S(1)} %get-tuple-element.83), channel_id=1, source_target_pairs={{0,6},{2,0},{4,2},{6,4},{1,7},{3,1},{5,3},{7,5},{8,14},{10,8},{12,... | collective-permute-start | bytes 835592 | tf_op jit(solution)/shard_map/ppermute | solution.py:28
  151.3 1.2 collective-permute-start.13
  152.4 12.8 %collective-permute-done.12 = bf16[272,512]{1,0:T(8,128)(2,1)} collective-permute-done((bf16[272,512]{1,0:T(8,128)(2,1)S(1)}, bf16[272,512]{1,0:T(8,128)(2,1)}, u32[]{:S(2)}, u32[]{:S(2)}) %collective-permute-start.12) | collective-permute-done | bytes 278560 | tf_op jit(solution)/shard_map/ppermute | solution.py:28
  165.8 1.7 collective-permute-done.13
  167.5 14.0 %collective-permute-done.14 = bf16[272,512]{1,0:T(8,128)(2,1)S(1)} collective-permute-done((bf16[272,512]{1,0:T(8,128)(2,1)S(1)}, bf16[272,512]{1,0:T(8,128)(2,1)S(1)}, u32[]{:S(2)}, u32[]{:S(2)}) %collective-permute-start.14) | collective-permute-done | bytes 278560 | tf_op jit(solution)/shard_map/ppermute | solution.py:28
  182.2 1.3 pad_maximum_fusion.3.x
  183.6 3.2 %add_convert_fusion.1 = bf16[4,384,512]{2,1,0:T(8,128)(2,1)S(1)} fusion(bf16[4,384,512]{2,1,0:T(8,128)(2,1)} %collective-permute-done.20, bf16[4,384,512]{2,1,0:T(8,128)(2,1)} %collective-permute-done.19, bf16[4,384,512]{2,1,0:T(8,128)(2,1)} %collective-permute-done.18, bf16[4,384,512]{2,1,0:T(8,128)(2,1)S(1)} %get-tuple-element.38), kind=kLoop, calls=%fused_computation.4 | loop fusion | flops 6291456 | bytes 7864320 | tf_op jit(solution)/shard_map/convert_element_type | solution.py:419
  186.8 1.1 copy-done.7
  187.9 1.0 slice_bitcast_fusion.3
  189.0 1.1 collective-permute-start.21
  190.8 2.5 %collective-permute-start.23 = (bf16[384,512]{1,0:T(8,128)(2,1)}, bf16[384,512]{1,0:T(8,128)(2,1)}, u32[]{:S(2)}, u32[]{:S(2)}) collective-permute-start(bf16[384,512]{1,0:T(8,128)(2,1)} %get-tuple-element.75), channel_id=1, source_target_pairs={{0,24},{1,97},{8,0},{9,105},{16,8},{17,113},{24,16},{25,121},{32,5... | collective-permute-start | bytes 1179656 | tf_op jit(solution)/shard_map/ppermute | solution.py:298
  193.5 7.1 %finish.1 = (bf16[128,1024]{1,0:T(8,128)(2,1)}, bf16[128,1024]{1,0:T(8,128)(2,1)}) custom-call(s32[1]{0:T(128)} %bitcast.n_ref, bf16[4,272,512]{2,1,0:T(8,128)(2,1)S(1)} %pad_maximum_fusion.3.x, bf16[128,1024]{1,0:T(8,128)(2,1)S(1)} %copy-done.2, bf16[128,1024]{1,0:T(8,128)(2,1)S(1)} %copy-done.3, bf16[1,1024]{1,0:T(2,128)(2,1)S(1)} %broadcast_in_dim.179.gain, ...), custom_call_target="tpu_custom_call" | custom-call | flops 1073741824 | bytes 12582912 | tf_op jit(solution)/shard_map/finish/pallas_call | solution.py:233
  200.6 2.2 %collective-permute-done.22 = bf16[384,512]{1,0:T(8,128)(2,1)} collective-permute-done((bf16[384,512]{1,0:T(8,128)(2,1)}, bf16[384,512]{1,0:T(8,128)(2,1)}, u32[]{:S(2)}, u32[]{:S(2)}) %collective-permute-start.22) | collective-permute-done | bytes 393248 | tf_op jit(solution)/shard_map/ppermute | solution.py:298
  202.8 1.5 fusion.20
  204.4 1.0 copy.41
  (127 shorter events, 12.0 us)
Async XLA Ops:
  7.2 24.5 %copy-start = (bf16[1024,896]{1,0:T(8,128)(2,1)S(1)}, bf16[1024,896]{1,0:T(8,128)(2,1)}, u32[]{:S(2)}) copy-start(bf16[1024,896]{1,0:T(8,128)(2,1)} %param.18) | copy-start | bytes 5505028
  7.2 23.7 %copy-start.2 = (bf16[128,1024]{1,0:T(8,128)(2,1)S(1)}, bf16[128,1024]{1,0:T(8,128)(2,1)}, u32[]{:S(2)}) copy-start(bf16[128,1024]{1,0:T(8,128)(2,1)} %hid.1) | copy-start | bytes 786436
  7.2 23.2 %copy-start.19 = (s32[24]{0:T(128)S(1)}, s32[24]{0:T(128)}, u32[]{:S(2)}) copy-start(s32[24]{0:T(128)} %param.15) | copy-start | bytes 292
  7.2 29.7 %copy-start.18 = (bf16[896]{0:T(1024)(128)(2,1)S(1)}, bf16[896]{0:T(1024)(128)(2,1)}, u32[]{:S(2)}) copy-start(bf16[896]{0:T(1024)(128)(2,1)} %param.17) | copy-start | bytes 5380
  7.2 29.7 %copy-start.17 = (bf16[1024]{0:T(1024)(128)(2,1)S(1)}, bf16[1024]{0:T(1024)(128)(2,1)}, u32[]{:S(2)}) copy-start(bf16[1024]{0:T(1024)(128)(2,1)} %param.16) | copy-start | bytes 6148
  7.2 73.5 %all-gather.3.cloned.1.call-start = ((), (), s32[]{:S(2)}) async-start(), calls=%async_computation.2 | async-start | bytes 10543104 | tf_op jit(solution)/shard_map/all_gather | solution.py:341
  9.5 1.5 collective-permute-start.8
  11.8 194.3 %reduce-scatter.2.cloned.1.call-start = ((), (), s32[]{:S(2)}) async-start(), calls=%async_computation.1 | async-start | bytes 6881280 | tf_op jit(solution)/shard_map/reduce_scatter | solution.py:407
  11.9 46.9 %collective-permute-start.4 = (bf16[6,128,896]{2,1,0:T(8,128)(2,1)}, bf16[6,128,896]{2,1,0:T(8,128)(2,1)}, u32[]{:S(2)}, u32[]{:S(2)}) collective-permute-start(bf16[6,128,896]{2,1,0:T(8,128)(2,1)} %param.14), channel_id=1, source_target_pairs={{0,6},{2,0},{4,2},{6,4},{1,7},{3,1},{5,3},{7,5},{8,14},{10,8},{12,... | collective-permute-start | bytes 4128776 | tf_op jit(solution)/shard_map/ppermute | solution.py:28
  25.5 34.9 %collective-permute-start.5 = (bf16[6,128,896]{2,1,0:T(8,128)(2,1)}, bf16[6,128,896]{2,1,0:T(8,128)(2,1)}, u32[]{:S(2)}, u32[]{:S(2)}) collective-permute-start(bf16[6,128,896]{2,1,0:T(8,128)(2,1)} %param.14), channel_id=1, source_target_pairs={{0,2},{2,4},{4,6},{6,0},{1,3},{3,5},{5,7},{7,1},{8,10},{10,12},{12... | collective-permute-start | bytes 4128776 | tf_op jit(solution)/shard_map/ppermute | solution.py:28
  26.5 5.1 %collective-permute-start = (bf16[1,1024]{1,0:T(2,128)(2,1)S(1)}, bf16[1,1024]{1,0:T(2,128)(2,1)S(1)}, u32[]{:S(2)}, u32[]{:S(2)}) collective-permute-start(bf16[1,1024]{1,0:T(2,128)(2,1)S(1)} %get-tuple-element.90), channel_id=1, source_target_pairs={{0,8},{8,16},{16,24},{24,32},{32,40},{40,48},{48,56},{56,64},{64,7... | collective-permute-start | bytes 6152 | tf_op jit(solution)/shard_map/ppermute | solution.py:349
  30.5 24.4 %copy-start.10 = (bf16[6,128,896]{2,1,0:T(8,128)(2,1)S(1)}, bf16[6,128,896]{2,1,0:T(8,128)(2,1)}, u32[]{:S(2)}) copy-start(bf16[6,128,896]{2,1,0:T(8,128)(2,1)} %param.14) | copy-start | bytes 4128772
  30.5 25.1 %copy-start.20 = (bf16[896,896]{1,0:T(8,128)(2,1)S(1)}, bf16[896,896]{1,0:T(8,128)(2,1)}, u32[]{:S(2)}) copy-start(bf16[896,896]{1,0:T(8,128)(2,1)} %param.19) | copy-start | bytes 4816900
  32.0 22.4 %collective-permute-start.1 = (f32[3,896]{1,0:T(4,128)S(1)}, f32[3,896]{1,0:T(4,128)S(1)}, u32[]{:S(2)}, u32[]{:S(2)}) collective-permute-start(f32[3,896]{1,0:T(4,128)S(1)} %pad_maximum_fusion.8), channel_id=1, source_target_pairs={{0,2},{2,4},{4,6},{6,0},{1,3},{3,5},{5,7},{7,1},{8,10},{10,12},{12... | collective-permute-start | bytes 32264 | tf_op jit(solution)/shard_map/ppermute | solution.py:28
  32.1 22.7 %collective-permute-start.2 = (f32[3,896]{1,0:T(4,128)S(1)}, f32[3,896]{1,0:T(4,128)S(1)}, u32[]{:S(2)}, u32[]{:S(2)}) collective-permute-start(f32[3,896]{1,0:T(4,128)S(1)} %pad_maximum_fusion.8), channel_id=1, source_target_pairs={{0,4},{2,6},{4,0},{6,2},{1,5},{3,7},{5,1},{7,3},{8,12},{10,14},{12... | collective-permute-start | bytes 32264 | tf_op jit(solution)/shard_map/ppermute | solution.py:28
  36.8 18.0 %collective-permute-start.3 = (f32[3,896]{1,0:T(4,128)S(1)}, f32[3,896]{1,0:T(4,128)S(1)}, u32[]{:S(2)}, u32[]{:S(2)}) collective-permute-start(f32[3,896]{1,0:T(4,128)S(1)} %pad_maximum_fusion.8), channel_id=1, source_target_pairs={{0,6},{2,0},{4,2},{6,4},{1,7},{3,1},{5,3},{7,5},{8,14},{10,8},{12,... | collective-permute-start | bytes 32264 | tf_op jit(solution)/shard_map/ppermute | solution.py:28
  59.9 13.3 %collective-permute-start.6 = (bf16[3,128,896]{2,1,0:T(8,128)(2,1)S(1)}, bf16[3,128,896]{2,1,0:T(8,128)(2,1)S(1)}, u32[]{:S(2)}, u32[]{:S(2)}) collective-permute-start(bf16[3,128,896]{2,1,0:T(8,128)(2,1)S(1)} %slice.123), channel_id=1, source_target_pairs={{0,6},{2,0},{4,2},{6,4},{1,7},{3,1},{5,3},{7,5},{8,14},{10,8},{12,... | collective-permute-start | bytes 2064392 | tf_op jit(solution)/shard_map/ppermute | solution.py:28
  61.5 14.5 %collective-permute-start.7 = (bf16[3,128,896]{2,1,0:T(8,128)(2,1)S(1)}, bf16[3,128,896]{2,1,0:T(8,128)(2,1)S(1)}, u32[]{:S(2)}, u32[]{:S(2)}) collective-permute-start(bf16[3,128,896]{2,1,0:T(8,128)(2,1)S(1)} %slice.124), channel_id=1, source_target_pairs={{0,2},{2,4},{4,6},{6,0},{1,3},{3,5},{5,7},{7,1},{8,10},{10,12},{12... | collective-permute-start | bytes 2064392 | tf_op jit(solution)/shard_map/ppermute | solution.py:28
  79.6 2.7 %copy-start.3 = (bf16[128,1024]{1,0:T(8,128)(2,1)S(1)}, bf16[128,1024]{1,0:T(8,128)(2,1)}, u32[]{:S(2)}) copy-start(bf16[128,1024]{1,0:T(8,128)(2,1)} %dout.1) | copy-start | bytes 786436
  82.3 10.7 %copy-start.4 = (bf16[12,128,896]{2,1,0:T(8,128)(2,1)S(1)}, bf16[12,128,896]{2,1,0:T(8,128)(2,1)}, u32[]{:S(2)}) copy-start(bf16[12,128,896]{2,1,0:T(8,128)(2,1)} %add_convert_fusion.near) | copy-start | bytes 8257540
  82.3 10.7 %copy-start.5 = (bf16[6,128,896]{2,1,0:T(8,128)(2,1)S(1)}, bf16[6,128,896]{2,1,0:T(8,128)(2,1)}, u32[]{:S(2)}) copy-start(bf16[6,128,896]{2,1,0:T(8,128)(2,1)} %add_convert_fusion.3.e0) | copy-start | bytes 4128772
  82.3 10.7 %copy-start.6 = (bf16[6,128,896]{2,1,0:T(8,128)(2,1)S(1)}, bf16[6,128,896]{2,1,0:T(8,128)(2,1)}, u32[]{:S(2)}) copy-start(bf16[6,128,896]{2,1,0:T(8,128)(2,1)} %add_convert_fusion.2.far) | copy-start | bytes 4128772
  88.0 13.2 %collective-permute-start.10 = (bf16[256,512]{1,0:T(8,128)(2,1)S(1)}, bf16[256,512]{1,0:T(8,128)(2,1)S(1)}, u32[]{:S(2)}, u32[]{:S(2)}) collective-permute-start(bf16[256,512]{1,0:T(8,128)(2,1)S(1)} %get-tuple-element.79), channel_id=1, source_target_pairs={{0,2},{2,4},{4,6},{6,0},{1,3},{3,5},{5,7},{7,1},{8,10},{10,12},{12... | collective-permute-start | bytes 786440 | tf_op jit(solution)/shard_map/ppermute | solution.py:28
  89.5 13.2 %collective-permute-start.11 = (bf16[256,512]{1,0:T(8,128)(2,1)S(1)}, bf16[256,512]{1,0:T(8,128)(2,1)S(1)}, u32[]{:S(2)}, u32[]{:S(2)}) collective-permute-start(bf16[256,512]{1,0:T(8,128)(2,1)S(1)} %get-tuple-element.78), channel_id=1, source_target_pairs={{0,6},{2,0},{4,2},{6,4},{1,7},{3,1},{5,3},{7,5},{8,14},{10,8},{12,... | collective-permute-start | bytes 786440 | tf_op jit(solution)/shard_map/ppermute | solution.py:28
  91.3 13.0 %collective-permute-start.9 = (bf16[256,512]{1,0:T(8,128)(2,1)S(1)}, bf16[256,512]{1,0:T(8,128)(2,1)S(1)}, u32[]{:S(2)}, u32[]{:S(2)}) collective-permute-start(bf16[256,512]{1,0:T(8,128)(2,1)S(1)} %get-tuple-element.77), channel_id=1, source_target_pairs={{0,4},{2,6},{4,0},{6,2},{1,5},{3,7},{5,1},{7,3},{8,12},{10,14},{12... | collective-permute-start | bytes 786440 | tf_op jit(solution)/shard_map/ppermute | solution.py:28
  104.4 20.9 %copy-start.8 = (bf16[256,512]{1,0:T(8,128)(2,1)}, bf16[256,512]{1,0:T(8,128)(2,1)S(1)}, u32[]{:S(2)}) copy-start(bf16[256,512]{1,0:T(8,128)(2,1)S(1)} %fusion.23) | copy-start | bytes 786436
  104.5 20.8 %collective-permute-start.15 = (bf16[128,1024]{1,0:T(8,128)(2,1)S(1)}, bf16[128,1024]{1,0:T(8,128)(2,1)S(1)}, u32[]{:S(2)}, u32[]{:S(2)}) collective-permute-start(bf16[128,1024]{1,0:T(8,128)(2,1)S(1)} %copy-done.3), channel_id=1, source_target_pairs={{0,6},{2,0},{4,2},{6,4},{1,7},{3,1},{5,3},{7,5},{8,14},{10,8},{12,... | collective-permute-start | bytes 786440 | tf_op jit(solution)/shard_map/ppermute | solution.py:28
  106.6 18.7 %collective-permute-start.16 = (bf16[128,1024]{1,0:T(8,128)(2,1)S(1)}, bf16[128,1024]{1,0:T(8,128)(2,1)S(1)}, u32[]{:S(2)}, u32[]{:S(2)}) collective-permute-start(bf16[128,1024]{1,0:T(8,128)(2,1)S(1)} %copy-done.3), channel_id=1, source_target_pairs={{0,4},{2,6},{4,0},{6,2},{1,5},{3,7},{5,1},{7,3},{8,12},{10,14},{12... | collective-permute-start | bytes 786440 | tf_op jit(solution)/shard_map/ppermute | solution.py:28
  107.8 17.6 %collective-permute-start.17 = (bf16[128,1024]{1,0:T(8,128)(2,1)S(1)}, bf16[128,1024]{1,0:T(8,128)(2,1)S(1)}, u32[]{:S(2)}, u32[]{:S(2)}) collective-permute-start(bf16[128,1024]{1,0:T(8,128)(2,1)S(1)} %copy-done.3), channel_id=1, source_target_pairs={{0,2},{2,4},{4,6},{6,0},{1,3},{3,5},{5,7},{7,1},{8,10},{10,12},{12... | collective-permute-start | bytes 786440 | tf_op jit(solution)/shard_map/ppermute | solution.py:28
  125.3 0.7 copy-start.13
  127.0 5.0 %copy-start.21 = (bf16[16,128,896]{2,1,0:T(8,128)(2,1)S(1)}, bf16[16,128,896]{2,1,0:T(8,128)(2,1)}, u32[]{:S(2)}) copy-start(bf16[16,128,896]{2,1,0:T(8,128)(2,1)} %get-tuple-element.35) | copy-start | bytes 11010052
  127.0 5.0 %copy-start.22 = (bf16[2048,512]{1,0:T(8,128)(2,1)S(1)}, bf16[2048,512]{1,0:T(8,128)(2,1)}, u32[]{:S(2)}) copy-start(bf16[2048,512]{1,0:T(8,128)(2,1)} %get-tuple-element.36) | copy-start | bytes 6291460
  131.9 2.1 copy-start.14
  131.9 2.1 copy-start.16
  134.0 13.1 %copy-start.9 = (bf16[256,512]{1,0:T(8,128)(2,1)S(1)}, bf16[256,512]{1,0:T(8,128)(2,1)}, u32[]{:S(2)}) copy-start(bf16[256,512]{1,0:T(8,128)(2,1)} %copy-done.8) | copy-start | bytes 786436
  141.0 42.6 %collective-permute-start.18 = (bf16[4,384,512]{2,1,0:T(8,128)(2,1)}, bf16[4,384,512]{2,1,0:T(8,128)(2,1)}, u32[]{:S(2)}, u32[]{:S(2)}) collective-permute-start(bf16[4,384,512]{2,1,0:T(8,128)(2,1)} %get-tuple-element.39), channel_id=1, source_target_pairs={{0,64},{1,17},{8,72},{9,25},{16,80},{17,1},{24,88},{25,9},{32,96},... | collective-permute-start | bytes 4718600 | tf_op jit(solution)/shard_map/ppermute | solution.py:298
  143.9 39.6 %collective-permute-start.19 = (bf16[4,384,512]{2,1,0:T(8,128)(2,1)}, bf16[4,384,512]{2,1,0:T(8,128)(2,1)}, u32[]{:S(2)}, u32[]{:S(2)}) collective-permute-start(bf16[4,384,512]{2,1,0:T(8,128)(2,1)} %get-tuple-element.40), channel_id=1, source_target_pairs={{0,32},{1,9},{8,40},{9,17},{16,48},{17,25},{24,56},{25,1},{32,64},... | collective-permute-start | bytes 4718600 | tf_op jit(solution)/shard_map/ppermute | solution.py:298
  144.5 39.1 %collective-permute-start.20 = (bf16[4,384,512]{2,1,0:T(8,128)(2,1)}, bf16[4,384,512]{2,1,0:T(8,128)(2,1)}, u32[]{:S(2)}, u32[]{:S(2)}) collective-permute-start(bf16[4,384,512]{2,1,0:T(8,128)(2,1)} %get-tuple-element.41), channel_id=1, source_target_pairs={{0,96},{1,25},{8,104},{9,1},{16,112},{17,9},{24,120},{25,17},{32,0... | collective-permute-start | bytes 4718600 | tf_op jit(solution)/shard_map/ppermute | solution.py:298
  148.1 17.2 %collective-permute-start.12 = (bf16[272,512]{1,0:T(8,128)(2,1)S(1)}, bf16[272,512]{1,0:T(8,128)(2,1)}, u32[]{:S(2)}, u32[]{:S(2)}) collective-permute-start(bf16[272,512]{1,0:T(8,128)(2,1)S(1)} %get-tuple-element.83), channel_id=1, source_target_pairs={{0,6},{2,0},{4,2},{6,4},{1,7},{3,1},{5,3},{7,5},{8,14},{10,8},{12,... | collective-permute-start | bytes 835592 | tf_op jit(solution)/shard_map/ppermute | solution.py:28
  151.3 16.2 %collective-permute-start.13 = (bf16[272,512]{1,0:T(8,128)(2,1)S(1)}, bf16[272,512]{1,0:T(8,128)(2,1)S(1)}, u32[]{:S(2)}, u32[]{:S(2)}) collective-permute-start(bf16[272,512]{1,0:T(8,128)(2,1)S(1)} %get-tuple-element.83), channel_id=1, source_target_pairs={{0,4},{2,6},{4,0},{6,2},{1,5},{3,7},{5,1},{7,3},{8,12},{10,14},{12... | collective-permute-start | bytes 835592 | tf_op jit(solution)/shard_map/ppermute | solution.py:28
  165.2 16.3 %collective-permute-start.14 = (bf16[272,512]{1,0:T(8,128)(2,1)S(1)}, bf16[272,512]{1,0:T(8,128)(2,1)S(1)}, u32[]{:S(2)}, u32[]{:S(2)}) collective-permute-start(bf16[272,512]{1,0:T(8,128)(2,1)S(1)} %get-tuple-element.83), channel_id=1, source_target_pairs={{0,2},{2,4},{4,6},{6,0},{1,3},{3,5},{5,7},{7,1},{8,10},{10,12},{12... | collective-permute-start | bytes 835592 | tf_op jit(solution)/shard_map/ppermute | solution.py:28
  167.5 14.0 %copy-start.11 = (bf16[272,512]{1,0:T(8,128)(2,1)}, bf16[272,512]{1,0:T(8,128)(2,1)S(1)}, u32[]{:S(2)}) copy-start(bf16[272,512]{1,0:T(8,128)(2,1)S(1)} %collective-permute-done.13) | copy-start | bytes 835588
  181.5 0.7 copy-start.12
  186.8 1.1 copy-start.7
  189.0 11.6 %collective-permute-start.21 = (bf16[384,512]{1,0:T(8,128)(2,1)}, bf16[384,512]{1,0:T(8,128)(2,1)}, u32[]{:S(2)}, u32[]{:S(2)}) collective-permute-start(bf16[384,512]{1,0:T(8,128)(2,1)} %get-tuple-element.74), channel_id=1, source_target_pairs={{0,16},{1,65},{8,24},{9,73},{16,0},{17,81},{24,8},{25,89},{32,48},... | collective-permute-start | bytes 1179656 | tf_op jit(solution)/shard_map/ppermute | solution.py:298
  190.1 12.7 %collective-permute-start.22 = (bf16[384,512]{1,0:T(8,128)(2,1)}, bf16[384,512]{1,0:T(8,128)(2,1)}, u32[]{:S(2)}, u32[]{:S(2)}) collective-permute-start(bf16[384,512]{1,0:T(8,128)(2,1)} %get-tuple-element.76), channel_id=1, source_target_pairs={{0,8},{1,33},{8,16},{9,41},{16,24},{17,49},{24,0},{25,57},{32,40},... | collective-permute-start | bytes 1179656 | tf_op jit(solution)/shard_map/ppermute | solution.py:298
  190.8 12.0 %collective-permute-start.23 = (bf16[384,512]{1,0:T(8,128)(2,1)}, bf16[384,512]{1,0:T(8,128)(2,1)}, u32[]{:S(2)}, u32[]{:S(2)}) collective-permute-start(bf16[384,512]{1,0:T(8,128)(2,1)} %get-tuple-element.75), channel_id=1, source_target_pairs={{0,24},{1,97},{8,0},{9,105},{16,8},{17,113},{24,16},{25,121},{32,5... | collective-permute-start | bytes 1179656 | tf_op jit(solution)/shard_map/ppermute | solution.py:298
  193.5 12.6 %copy-start.1 = (bf16[1024,896]{1,0:T(8,128)(2,1)S(1)}, bf16[1024,896]{1,0:T(8,128)(2,1)}, u32[]{:S(2)}) copy-start(bf16[1024,896]{1,0:T(8,128)(2,1)} %param.18) | copy-start | bytes 5505028
  (1 other events, 0.7 us)
Sparse Core Ops, SparseCore 0:
  11.9 68.7 all-gather.2
  126.9 69.8 reduce-scatter.1

commit v5 on v4

--- a/solution.py
+++ b/solution.py
@@ -79,14 +79,14 @@
             in_specs=[
                 pl.BlockSpec((tokens, feats), lambda r, n: (0, 0)),
                 pl.BlockSpec((tokens, feats), lambda r, n: (0, 0)),
-                pl.BlockSpec((4, 1, 256, 512), lambda r, n: ((2 * n[0] + r) % 4, 0, 0, 0)),
-                pl.BlockSpec((4, 1, 256, 512), lambda r, n: ((4 - r) % 4, 1, 0, 0)),
+                pl.BlockSpec((4, 1, 256, 512), lambda r, n: ((n[0] + 6 - r) % 4, 0, 0, 0)),
+                pl.BlockSpec((4, 1, 256, 512), lambda r, n: ((n[0] + 6 - r) % 4, 1, 0, 0)),
             ],
             out_specs=pl.BlockSpec((1, 2 * tokens, 512), lambda r, n: (r, 0, 0)),
         ),
         out_shape=jax.ShapeDtypeStruct((4, 2 * tokens, 512), BF16),
         cost_estimate=cost(2 * tokens * 4096 * 512, 12 << 20),
-        compiler_params=pltpu.CompilerParams(vmem_limit_bytes=24 << 20),
+        compiler_params=pltpu.CompilerParams(vmem_limit_bytes=12 << 20),
         name="project",
     )(n, normed, dout, weights, weights)
 
@@ -130,12 +130,26 @@
         out_specs=[VMEM] * 3,
         out_shape=[pltpu.HBM((2 * KMAX, NLEN, wk.shape[0]), BF16), flat, flat],
         cost_estimate=cost(2048 * 896 * 1024, 16 << 20),
-        compiler_params=pltpu.CompilerParams(vmem_limit_bytes=26 << 20),
+        compiler_params=pltpu.CompilerParams(vmem_limit_bytes=22 << 20),
         name="keys_values",
     )(tab, *blocks, wk, wv)
 
 
-def attend_kernel(tab, inv, kb, vb, q, dc, wk, wv, ctx, dq, dk, dv, out, de):
+def attend_kernel(tab, inv, kb, vb, q, dc, wk, wv, ctx, dq, dk_out, dv_out, out, dk, dv, de, blank, sems):
+    slots = out.shape[0]
+    blank[...] = jnp.zeros(blank.shape, BF16)
+
+    def to_slot(i, source):
+        return pltpu.make_async_copy(source, out.at[i], sems.at[i])
+
+    def empty(i, carry):
+        @pl.when(inv[i] < 0)
+        def _():
+            to_slot(i, blank).start()
+
+        return carry
+
+    lax.fori_loop(0, slots, empty, 0)
     factor = HD ** (-0.5)
     heads = q.shape[1] // HD
     keys = KMAX * NLEN
@@ -159,28 +173,38 @@
             dk[rows, cols] = dot(ds, qh, TN).astype(BF16)
             dv[rows, cols] = dot(pb, dh, TN).astype(BF16)
 
+    copies = [
+        pltpu.make_async_copy(dk, dk_out, sems.at[slots]),
+        pltpu.make_async_copy(dv, dv_out, sems.at[slots + 1]),
+    ]
+    for copy in copies:
+        copy.start()
+
     def grad(c, carry):
         rows = pl.ds(pl.multiple_of(c * 512, 512), 512)
         part = dot(dk[rows, :], wk[...], NT) + dot(dv[rows, :], wv[...], NT)
         de[pl.ds(4 * c, 4)] = part.astype(BF16).reshape(4, NLEN, wk.shape[0])
+
+        def send(i, carry):
+            src = inv[i]
+
+            @pl.when((src >= 4 * c) & (src < 4 * c + 4))
+            def _():
+                to_slot(i, de.at[src]).start()
+
+            return carry
+
+        return lax.fori_loop(0, slots, send, carry)
+
+    lax.fori_loop(0, 4, grad, 0)
+
+    def arrive(i, carry):
+        to_slot(i, blank).wait()
         return carry
 
-    lax.fori_loop(0, 4, grad, 0)
-
-    def place(i, carry):
-        src = inv[i]
-
-        @pl.when(src < 0)
-        def _():
-            out[i] = jnp.zeros(out.shape[1:], BF16)
-
-        @pl.when(src >= 0)
-        def _():
-            out[i] = de[src]
-
-        return carry
-
-    lax.fori_loop(0, out.shape[0], place, 0)
+    lax.fori_loop(0, slots, arrive, 0)
+    for copy in copies:
+        copy.wait()
 
 
 def attend(tab, inv, kb, vb, q, dc, wk, wv):
@@ -190,11 +214,17 @@
     return pl.pallas_call(
         attend_kernel,
         in_specs=[SMEM, SMEM] + [VMEM] * 6,
-        out_specs=[VMEM] * 5,
+        out_specs=[VMEM] * 2 + [pl.BlockSpec(memory_space=pl.ANY)] * 3,
         out_shape=[same, same, flat, flat, pltpu.HBM((inv.shape[0], NLEN, width), BF16)],
-        scratch_shapes=[pltpu.VMEM((2 * KMAX, NLEN, width), BF16)],
+        scratch_shapes=[
+            pltpu.VMEM(kb.shape, BF16),
+            pltpu.VMEM(kb.shape, BF16),
+            pltpu.VMEM((2 * KMAX, NLEN, width), BF16),
+            pltpu.VMEM((NLEN, width), BF16),
+            pltpu.SemaphoreType.DMA((inv.shape[0] + 2,)),
+        ],
         cost_estimate=cost(2048 * 896 * 1024, 40 << 20),
-        compiler_params=pltpu.CompilerParams(vmem_limit_bytes=34 << 20),
+        compiler_params=pltpu.CompilerParams(vmem_limit_bytes=24 << 20),
         name="attend",
     )(tab, inv, kb, vb, q, dc, wk, wv)
 
@@ -242,15 +272,15 @@
                 pl.BlockSpec((1, feats), lambda r, n: (0, 0)),
                 column,
                 column,
-                pl.BlockSpec((4, 1, 256, 512), lambda r, n: ((2 * n[0] + r) % 4, 0, 0, 0)),
-                pl.BlockSpec((4, 1, 256, 512), lambda r, n: ((4 - r) % 4, 1, 0, 0)),
+                pl.BlockSpec((4, 1, 256, 512), lambda r, n: ((n[0] + 6 - r) % 4, 0, 0, 0)),
+                pl.BlockSpec((4, 1, 256, 512), lambda r, n: ((n[0] + 6 - r) % 4, 1, 0, 0)),
             ],
             out_specs=[whole, whole],
             scratch_shapes=[pltpu.VMEM((tokens, feats), F32)] * 2,
         ),
         out_shape=[jax.ShapeDtypeStruct((tokens, feats), BF16)] * 2,
         cost_estimate=cost(2 * tokens * 4096 * 512, 12 << 20),
-        compiler_params=pltpu.CompilerParams(vmem_limit_bytes=24 << 20),
+        compiler_params=pltpu.CompilerParams(vmem_limit_bytes=12 << 20),
         name="finish",
     )(n, x, hidden, dout, gain[None], rstd, stat, weights, weights)
 
@@ -280,7 +310,7 @@
         out_specs=[VMEM] * 4,
         out_shape=[share] * 4,
         cost_estimate=cost(ctx.shape[0] * 4096 * 512, 16 << 20),
-        compiler_params=pltpu.CompilerParams(vmem_limit_bytes=24 << 20),
+        compiler_params=pltpu.CompilerParams(vmem_limit_bytes=16 << 20),
         name="pack",
     )(dest, n, dout, ctx, wk, wv)
 
@@ -303,7 +333,7 @@
 
 
 def second_phase(near):
-    return total([near[0]] + [along(near[j], j, False) for j in (2, 1, 3)])
+    return [near[0]] + [along(near[j], j, False) for j in (2, 1, 3)]
 
 
 def slot_tables(slot_span, n):
@@ -329,15 +359,13 @@
     spans = tokens // CLEN
 
     kv_half = jnp.where(b == 0, w_k, w_v)
-    swap = []
-    for i in range(4):
-        for j in range(4):
-            for k in range(4):
-                for core, x in ((0, (i + k) % 4), (1, (i - k) % 4)):
-                    swap.append((((4 * i + j) * 4 + k) * 2 + core, ((4 * x + j) * 4 + i) * 2 + core))
-    qo_half = lax.ppermute(
-        jnp.where(b == 0, w_q, w_o.T), ("seq", "nbr", "batch"), swap
-    )
+    swap = [
+        ((4 * i + j) * 4 + k, ((2 * i + 2 - k) % 4 * 4 + j) * 4 + i)
+        for i in range(4)
+        for j in range(4)
+        for k in range(4)
+    ]
+    qo_half = lax.ppermute(jnp.where(b == 0, w_q, w_o.T), ("seq", "nbr"), swap)
     weights = lax.all_gather(
         jnp.concatenate([qo_half, kv_half], axis=0), ("seq", "batch"), axis=0
     )
@@ -416,20 +444,22 @@
     wk_parts = dot(rows, d_key, TN).astype(BF16).reshape(16, -1, 512)
     wv_parts = dot(rows, d_value, TN).astype(BF16).reshape(16, -1, 512)
     arrived = first_phase(pack(dest, n1, dout_rel, ctx, wk_parts, wv_parts))
-    near = total(arrived).astype(BF16)
-    whole = second_phase(near)
-    d_wo = whole[:256].T
-    d_wk, d_wv = whole[256:312], whole[320:376]
+    near = [total([share[j] for share in arrived]).astype(BF16) for j in range(4)]
+    last = second_phase(near)
 
     inner = jnp.sum(d_query.astype(F32) * query.astype(F32), axis=-1).astype(BF16)
     more = jnp.broadcast_to(jnp.pad(inner, (0, ctx.shape[1] - tokens))[None], (16, ctx.shape[1]))
     local = jnp.concatenate([ctx, d_query, more], axis=0)
-    heads = jnp.stack([local, shift(local, -1), shift(local, 2), shift(local, 1)])
+    h1, h2a, h2b, h3 = ring_gather(local)
+    heads = jnp.stack([local, h1, jnp.concatenate([h2a, h2b], axis=0), h3])
     heads = lax.optimization_barrier((heads, near))[0]
     stat = jnp.sum(heads[:, 2 * tokens, :tokens].astype(F32), axis=0)[:, None]
     stat = stat / (rstd * (4 * feats))
     out, d_hidden = finish(n1, heads, hidden, d_out, dec_gain, rstd, stat, weights)
 
+    whole = total(lax.optimization_barrier((last, out))[0])
+    d_wo = whole[:256].T
+    d_wk, d_wv = whole[256:312], whole[320:376]
     return (out, d_hidden, d_enc, d_wo, d_wk, d_wv)
 
 

time: 213 us -> 205 us (0.962)
  Pallas kernels: 45 us -> 41.8 us
  local copies, waits for them, and re-layouts: 11.9 us -> 9.06 us
  starting transfers between devices: 48.9 us -> 46.1 us
    ppermute x16 -> x17, starting transfers between devices: 33.8 us -> 25.7 us  [shift(): return lax.ppermute(x, 'nbr', [(i, (i + by) % n) for i in range(n)])]
    ppermute x16 -> x17, waiting for transfers between devices: 52.6 us -> 47.9 us  [shift(): return lax.ppermute(x, 'nbr', [(i, (i + by) % n) for i in range(n)])]
    ppermute x1, waiting for transfers between devices: 0.01 us -> 4.7 us  [body(): qo_half = lax.ppermute(jnp.where(b == 0, w_q, w_o.T), ('seq', 'nbr'), swap)]
    add x1 -> x2, other arithmetic: 1.54 us -> 5.67 us  [total(): return sum((x.astype(F32) for x in shares))]
    convert_element_type x1 -> x0, other arithmetic: 3.23 us -> none  [body(): near = total(arrived).astype(BF16)]
    pallas_call x1, Pallas kernels: 17.5 us -> 14.3 us  [attend(): pl.pallas_call(attend_kernel, in_specs=[SMEM, SMEM] + [VMEM] * 6, out_spe...]
    ppermute x6, starting transfers between devices: 10.6 us -> 13.3 us  [along(): return lax.ppermute(share, ('seq', 'batch'), pairs)]
    ppermute x1, starting transfers between devices: 0.68 us -> 3.17 us  [body(): qo_half = lax.ppermute(jnp.where(b == 0, w_q, w_o.T), ('seq', 'nbr'), swap)]
  transfers between devices with their start and end apart: 26 -> 27, of which waited for: 12 -> 12; matrix products, arithmetic and copies ran while one was open for 19% -> 19% of each run, Pallas kernels for 19% -> 18%
where the time goes in v5:
time: 205 us; the launch traced here: 204 us
  waiting for transfers between devices  55.5 us (27%)
  starting transfers between devices  46.1 us (22%)
  Pallas kernels  41.8 us (20%)
  matrix products  20.7 us (10%)
  other arithmetic  16.3 us (8%)
  between operations  14.7 us (7%)
  local copies, waits for them, and re-layouts  9.06 us (4%)
    ppermute x17, waiting for transfers between devices, shift(): return lax.ppermute(x, 'nbr', [(i, (i + by) % n) for i in range(n)])  47.9 us
    ppermute x17, starting transfers between devices, shift(): return lax.ppermute(x, 'nbr', [(i, (i + by) % n) for i in range(n)])  25.7 us
    pallas_call x1, Pallas kernels, attend(): pl.pallas_call(attend_kernel, in_specs=[SMEM, SMEM] + [VMEM] * 6, out_spe...  14.3 us
    dot_general x3, matrix products, encode(): jnp.dot(enc_normed.reshape(-1, width), w_enc, preferred_element_type=F32)  13.3 us
    ppermute x6, starting transfers between devices, along(): return lax.ppermute(share, ('seq', 'batch'), pairs)  13.3 us
    pallas_call x1, Pallas kernels, keys_values(): pl.pallas_call(keys_kernel, in_specs=[SMEM] + [VMEM] * 5, out_specs=[VMEM...  8.05 us
    pallas_call x1, Pallas kernels, finish(): pl.pallas_call(finish_kernel, grid_spec=pltpu.PrefetchScalarGridSpec(num_...  7.12 us
    dot_general x2, matrix products, dot(): return lax.dot_general(a, b, (dims, ((), ())), preferred_element_type=F32)  7.01 us
  transfers between devices with their start and end apart: 27, of which 12 were waited for; matrix products, arithmetic and copies ran while one was open for 19% of the time, Pallas kernels for 18%

profile of v5, /device:TPU:0, one launch (start us, length us, event | category | flops | bytes accessed | tf_op | source)
XLA Modules:
  0.0 204.0 jit_solution(4641285031525099296)
XLA Ops:
  7.3 1.2 copy.36
  8.5 1.0 bitcast_select_fusion
  9.5 3.2 %collective-permute-start.8 = (bf16[256,512]{1,0:T(8,128)(2,1)S(1)}, bf16[256,512]{1,0:T(8,128)(2,1)S(1)}, u32[]{:S(2)}, u32[]{:S(2)}) collective-permute-start(bf16[256,512]{1,0:T(8,128)(2,1)S(1)} %bitcast_select_fusion), channel_id=1, source_target_pairs={{0,64},{2,32},{4,0},{6,96},{8,72},{10,40},{12,8},{14,104},{16,80},... | collective-permute-start | bytes 786440 | tf_op jit(solution)/shard_map/ppermute | solution.py:368
  12.7 0.8 broadcast_select_fusion
  13.5 4.7 %collective-permute-done.8 = bf16[256,512]{1,0:T(8,128)(2,1)S(1)} collective-permute-done((bf16[256,512]{1,0:T(8,128)(2,1)S(1)}, bf16[256,512]{1,0:T(8,128)(2,1)S(1)}, u32[]{:S(2)}, u32[]{:S(2)}) %collective-permute-start.8) | collective-permute-done | bytes 262176 | tf_op jit(solution)/shard_map/ppermute | solution.py:368
  18.2 0.7 pad_maximum_fusion.6
  19.0 4.9 %collective-permute-start.4 = (bf16[6,128,896]{2,1,0:T(8,128)(2,1)}, bf16[6,128,896]{2,1,0:T(8,128)(2,1)}, u32[]{:S(2)}, u32[]{:S(2)}) collective-permute-start(bf16[6,128,896]{2,1,0:T(8,128)(2,1)} %param.14), channel_id=1, source_target_pairs={{0,6},{2,0},{4,2},{6,4},{1,7},{3,1},{5,3},{7,5},{8,14},{10,8},{12,... | collective-permute-start | bytes 4128776 | tf_op jit(solution)/shard_map/ppermute | solution.py:28
  24.0 1.0 bitcast_reduce_fusion
  25.0 3.8 %collective-permute-start = (bf16[1,1024]{1,0:T(2,128)(2,1)S(1)}, bf16[1,1024]{1,0:T(2,128)(2,1)S(1)}, u32[]{:S(2)}, u32[]{:S(2)}) collective-permute-start(bf16[1,1024]{1,0:T(2,128)(2,1)S(1)} %get-tuple-element.99), channel_id=1, source_target_pairs={{0,8},{8,16},{16,24},{24,32},{32,40},{40,48},{48,56},{56,64},{64,7... | collective-permute-start | bytes 6152 | tf_op jit(solution)/shard_map/ppermute | solution.py:377
  30.6 4.7 %collective-permute-start.2 = (f32[3,896]{1,0:T(4,128)S(1)}, f32[3,896]{1,0:T(4,128)S(1)}, u32[]{:S(2)}, u32[]{:S(2)}) collective-permute-start(f32[3,896]{1,0:T(4,128)S(1)} %pad_maximum_fusion.8), channel_id=1, source_target_pairs={{0,4},{2,6},{4,0},{6,2},{1,5},{3,7},{5,1},{7,3},{8,12},{10,14},{12... | collective-permute-start | bytes 32264 | tf_op jit(solution)/shard_map/ppermute | solution.py:28
  35.4 20.4 %collective-permute-done.1 = f32[3,896]{1,0:T(4,128)S(1)} collective-permute-done((f32[3,896]{1,0:T(4,128)S(1)}, f32[3,896]{1,0:T(4,128)S(1)}, u32[]{:S(2)}, u32[]{:S(2)}) %collective-permute-start.1) | collective-permute-done | bytes 10784 | tf_op jit(solution)/shard_map/ppermute | solution.py:28
  56.6 3.1 %add_convert_fusion.2.e0 = bf16[6,128,896]{2,1,0:T(8,128)(2,1)} fusion(bf16[6,128,896]{2,1,0:T(8,128)(2,1)S(1)} %copy-done.10, bf16[896,896]{1,0:T(8,128)(2,1)S(1)} %copy-done.20, f32[896]{0:T(1024)S(1)} %convert_element_type.184, f32[6,128]{1,0:T(8,128)S(1)} %add_rsqrt_fusion.2, f32[6,896]{1,0:T(8,128)S(1)} %get-tuple-element.98), kind=kOutput, calls=%fused_computation.13 | convolution fusion | flops 1242071040 | bytes 4386304 | tf_op jit(solution)/shard_map/dot_general | solution.py:406
  59.8 1.2 slice.179
  61.3 1.2 slice.180
  62.4 1.8 collective-permute-start.7
  64.2 2.6 %multiply_reduce_fusion = f32[12,128]{1,0:T(8,128)S(1)} fusion(f32[12,896]{1,0:T(8,128)S(1)} %select_select_fusion, bf16[6,128,896]{2,1,0:T(8,128)(2,1)} %collective-permute-done.5, bf16[6,128,896]{2,1,0:T(8,128)(2,1)} %collective-permute-done.4), kind=kLoop, calls=%fused_computation.2 | loop fusion | flops 6879744 | bytes 2801664 | tf_op jit(solution)/shard_map/reduce_sum | solution.py:53
  66.9 7.1 %add_convert_fusion.near = bf16[12,128,896]{2,1,0:T(8,128)(2,1)} fusion(f32[896]{0:T(1024)S(1)} %convert_element_type.184, f32[12,128]{1,0:T(8,128)S(1)} %add_rsqrt_fusion, f32[12,896]{1,0:T(8,128)S(1)} %select_select_fusion, bf16[6,128,896]{2,1,0:T(8,128)(2,1)} %collective-permute-done.5, bf16[6,128,896]{2,1,0:T(8,128)(2,1)} %collective-permute-done.4, ...), kind=kOutput, calls=%fused_computation | convolution fusion | flops 2486894592 | bytes 7163392 | tf_op jit(solution)/shard_map/dot_general | solution.py:406
  73.9 1.1 collective-permute-done.6
  75.0 2.9 %collective-permute-done.7 = bf16[3,128,896]{2,1,0:T(8,128)(2,1)S(1)} collective-permute-done((bf16[3,128,896]{2,1,0:T(8,128)(2,1)S(1)}, bf16[3,128,896]{2,1,0:T(8,128)(2,1)S(1)}, u32[]{:S(2)}, u32[]{:S(2)}) %collective-permute-start.7) | collective-permute-done | bytes 688160 | tf_op jit(solution)/shard_map/ppermute | solution.py:28
  78.3 3.1 %add_convert_fusion.1.far = bf16[6,128,896]{2,1,0:T(8,128)(2,1)} fusion(bf16[896,896]{1,0:T(8,128)(2,1)S(1)} %copy-done.20, f32[6,128]{1,0:T(8,128)S(1)} %add_rsqrt_fusion.1, f32[6,896]{1,0:T(8,128)S(1)} %get-tuple-element.97, f32[896]{0:T(1024)S(1)} %convert_element_type.184, bf16[3,128,896]{2,1,0:T(8,128)(2,1)S(1)} %collective-permute-done.7, ...), kind=kOutput, calls=%fused_computation.6 | convolution fusion | flops 1243447296 | bytes 4386304 | tf_op jit(solution)/shard_map/dot_general | solution.py:406
  81.4 1.6 fusion.45
  83.1 5.5 %project.1 = bf16[4,256,512]{2,1,0:T(8,128)(2,1)S(1)} custom-call(s32[1]{0:T(128)} %bitcast.n_ref, bf16[128,1024]{1,0:T(8,128)(2,1)S(1)} %multiply_convert_fusion.12.x, bf16[128,1024]{1,0:T(8,128)(2,1)S(1)} %copy-done.3, bf16[16,2,312,512]{3,2,1,0:T(8,128)(2,1)} %bitcast.83, bf16[16,2,312,512]{3,2,1,0:T(8,128)(2,1)} %bitcast.84), custom_call_target="tpu_custom_call" | custom-call | flops 1073741824 | bytes 12582912 | tf_op jit(solution)/shard_map/project/pallas_call | solution.py:74
  88.9 3.1 %collective-permute-start.11 = (bf16[256,512]{1,0:T(8,128)(2,1)S(1)}, bf16[256,512]{1,0:T(8,128)(2,1)S(1)}, u32[]{:S(2)}, u32[]{:S(2)}) collective-permute-start(bf16[256,512]{1,0:T(8,128)(2,1)S(1)} %get-tuple-element.87), channel_id=1, source_target_pairs={{0,6},{2,0},{4,2},{6,4},{1,7},{3,1},{5,3},{7,5},{8,14},{10,8},{12,... | collective-permute-start | bytes 786440 | tf_op jit(solution)/shard_map/ppermute | solution.py:28
  92.0 8.1 %keys_values.1 = (bf16[16,128,896]{2,1,0:T(8,128)(2,1)}, bf16[2048,512]{1,0:T(8,128)(2,1)S(1)}, bf16[2048,512]{1,0:T(8,128)(2,1)S(1)}) custom-call(s32[18]{0:T(128)S(1)} %pad_add_fusion.1.tab, bf16[6,128,896]{2,1,0:T(8,128)(2,1)S(1)} %copy-done.5, bf16[12,128,896]{2,1,0:T(8,128)(2,1)S(1)} %copy-done.4, bf16[6,128,896]{2,1,0:T(8,128)(2,1)S(1)} %copy-done.6, ...), custom_call_target="tpu_custom_call" | custom-call | flops 3758096384 | bytes 16777216 | tf_op jit(solution)/shard_map/keys_values/pallas_call | solution.py:127
  100.1 1.2 collective-permute-done.11
  101.3 1.2 collective-permute-done.9
  102.7 2.5 %collective-permute-start.16 = (bf16[128,1024]{1,0:T(8,128)(2,1)S(1)}, bf16[128,1024]{1,0:T(8,128)(2,1)S(1)}, u32[]{:S(2)}, u32[]{:S(2)}) collective-permute-start(bf16[128,1024]{1,0:T(8,128)(2,1)S(1)} %copy-done.3), channel_id=1, source_target_pairs={{0,6},{2,0},{4,2},{6,4},{1,7},{3,1},{5,3},{7,5},{8,14},{10,8},{12,... | collective-permute-start | bytes 786440 | tf_op jit(solution)/shard_map/ppermute | solution.py:28
  105.2 0.8 collective-permute-start.17
  106.2 14.3 %attend.1 = (bf16[128,512]{1,0:T(8,128)(2,1)S(1)}, bf16[128,512]{1,0:T(8,128)(2,1)S(1)}, bf16[2048,512]{1,0:T(8,128)(2,1)}, bf16[2048,512]{1,0:T(8,128)(2,1)}, bf16[24,128,896]{2,1,0:T(8,128)(2,1)}) custom-call(s32[18]{0:T(128)S(1)} %pad_add_fusion.1.tab, s32[24]{0:T(128)S(1)} %get-tuple-element.109.inv, bf16[2048,512]{1,0:T(8,128)(2,1)S(1)} %get-tuple-element.30.kb, ...), custom_call_target="tpu_custom_call" | custom-call | flops 3758096384 | bytes 41943040 | tf_op jit(solution)/shard_map/attend/pallas_call | solution.py:214
  122.2 4.9 %convolution_convert_fusion = bf16[896,512]{1,0:T(8,128)(2,1)S(1)} fusion(bf16[2048,896]{1,0:T(8,128)(2,1)} %bitcast.93, bf16[2048,512]{1,0:T(8,128)(2,1)} %get-tuple-element.41), kind=kOutput, calls=%fused_computation.22 | convolution fusion | flops 1879506944 | bytes 6684672 | tf_op jit(solution)/shard_map/dot_general | solution.py:19
  127.2 2.1 %convolution_convert_fusion.1 = bf16[896,512]{1,0:T(8,128)(2,1)S(1)} fusion(bf16[2048,896]{1,0:T(8,128)(2,1)S(1)} %bitcast.94, bf16[2048,512]{1,0:T(8,128)(2,1)S(1)} %copy-done.22), kind=kOutput, calls=%fused_computation.23 | convolution fusion | flops 1879506944 | bytes 6684672 | tf_op jit(solution)/shard_map/dot_general | solution.py:19
  129.4 6.8 %pack.1 = (bf16[4,384,512]{2,1,0:T(8,128)(2,1)S(1)}, bf16[4,384,512]{2,1,0:T(8,128)(2,1)}, bf16[4,384,512]{2,1,0:T(8,128)(2,1)}, bf16[4,384,512]{2,1,0:T(8,128)(2,1)}) custom-call(s32[16]{0:T(128)S(1)} %fusion.32.dest, s32[1]{0:T(128)} %bitcast.n_ref, bf16[4,128,1024]{2,1,0:T(8,128)(2,1)S(1)} %pad_maximum_fusion.4.d, ...), custom_call_target="tpu_custom_call" | custom-call | flops 536870912 | bytes 16777216 | tf_op jit(solution)/shard_map/pack/pallas_call | solution.py:307
  136.3 3.6 %collective-permute-start.19 = (bf16[4,384,512]{2,1,0:T(8,128)(2,1)}, bf16[4,384,512]{2,1,0:T(8,128)(2,1)}, u32[]{:S(2)}, u32[]{:S(2)}) collective-permute-start(bf16[4,384,512]{2,1,0:T(8,128)(2,1)} %get-tuple-element.43), channel_id=1, source_target_pairs={{0,64},{1,17},{8,72},{9,25},{16,80},{17,1},{24,88},{25,9},{32,96},... | collective-permute-start | bytes 4718600 | tf_op jit(solution)/shard_map/ppermute | solution.py:328
  140.4 2.7 %collective-permute-start.21 = (bf16[4,384,512]{2,1,0:T(8,128)(2,1)}, bf16[4,384,512]{2,1,0:T(8,128)(2,1)}, u32[]{:S(2)}, u32[]{:S(2)}) collective-permute-start(bf16[4,384,512]{2,1,0:T(8,128)(2,1)} %get-tuple-element.45), channel_id=1, source_target_pairs={{0,96},{1,25},{8,104},{9,1},{16,112},{17,9},{24,120},{25,17},{32,0... | collective-permute-start | bytes 4718600 | tf_op jit(solution)/shard_map/ppermute | solution.py:328
  143.2 0.7 fusion.44
  144.0 3.3 %collective-permute-start.12 = (bf16[272,512]{1,0:T(8,128)(2,1)S(1)}, bf16[272,512]{1,0:T(8,128)(2,1)S(1)}, u32[]{:S(2)}, u32[]{:S(2)}) collective-permute-start(bf16[272,512]{1,0:T(8,128)(2,1)S(1)} %get-tuple-element.92), channel_id=1, source_target_pairs={{0,6},{2,0},{4,2},{6,4},{1,7},{3,1},{5,3},{7,5},{8,14},{10,8},{12,... | collective-permute-start | bytes 835592 | tf_op jit(solution)/shard_map/ppermute | solution.py:28
  147.3 11.8 %collective-permute-done.12 = bf16[272,512]{1,0:T(8,128)(2,1)S(1)} collective-permute-done((bf16[272,512]{1,0:T(8,128)(2,1)S(1)}, bf16[272,512]{1,0:T(8,128)(2,1)S(1)}, u32[]{:S(2)}, u32[]{:S(2)}) %collective-permute-start.12) | collective-permute-done | bytes 278560 | tf_op jit(solution)/shard_map/ppermute | solution.py:28
  159.0 3.8 %collective-permute-start.13 = (bf16[136,512]{1,0:T(8,128)(2,1)S(1)}, bf16[136,512]{1,0:T(8,128)(2,1)S(1)}, u32[]{:S(2)}, u32[]{:S(2)}) collective-permute-start(bf16[136,512]{1,0:T(8,128)(2,1)S(1)} %slice.190), channel_id=1, source_target_pairs={{0,6},{2,0},{4,2},{6,4},{1,7},{3,1},{5,3},{7,5},{8,14},{10,8},{12,... | collective-permute-start | bytes 417800 | tf_op jit(solution)/shard_map/ppermute | solution.py:28
  163.0 5.5 %collective-permute-done.13 = bf16[136,512]{1,0:T(8,128)(2,1)S(1)} collective-permute-done((bf16[136,512]{1,0:T(8,128)(2,1)S(1)}, bf16[136,512]{1,0:T(8,128)(2,1)S(1)}, u32[]{:S(2)}, u32[]{:S(2)}) %collective-permute-start.13) | collective-permute-done | bytes 139296 | tf_op jit(solution)/shard_map/ppermute | solution.py:28
  168.5 3.8 %collective-permute-done.15 = bf16[136,512]{1,0:T(8,128)(2,1)S(1)} collective-permute-done((bf16[136,512]{1,0:T(8,128)(2,1)S(1)}, bf16[136,512]{1,0:T(8,128)(2,1)S(1)}, u32[]{:S(2)}, u32[]{:S(2)}) %collective-permute-start.15) | collective-permute-done | bytes 139296 | tf_op jit(solution)/shard_map/ppermute | solution.py:28
  172.4 1.3 pad_maximum_fusion.3.x
  173.6 1.8 collective-permute-done.20
  176.0 4.2 %fusion.25 = (bf16[384,512]{1,0:T(8,128)(2,1)}, bf16[384,512]{1,0:T(8,128)(2,1)}, bf16[384,512]{1,0:T(8,128)(2,1)}, bf16[384,512]{1,0:T(8,128)(2,1)}) fusion(bf16[4,384,512]{2,1,0:T(8,128)(2,1)} %collective-permute-done.21, bf16[4,384,512]{2,1,0:T(8,128)(2,1)} %collective-permute-done.20, bf16[4,384,512]{2,1,0:T(8,128)(2,1)} %collective-permute-done.19, ...), kind=kLoop, calls=%fused_computation.49 | loop fusion | flops 6291456 | bytes 7864320 | tf_op jit(solution)/shard_map/add | solution.py:45
  180.2 3.2 %collective-permute-start.22 = (bf16[384,512]{1,0:T(8,128)(2,1)}, bf16[384,512]{1,0:T(8,128)(2,1)}, u32[]{:S(2)}, u32[]{:S(2)}) collective-permute-start(bf16[384,512]{1,0:T(8,128)(2,1)} %get-tuple-element.83), channel_id=1, source_target_pairs={{0,16},{1,65},{8,24},{9,73},{16,0},{17,81},{24,8},{25,89},{32,48},... | collective-permute-start | bytes 1179656 | tf_op jit(solution)/shard_map/ppermute | solution.py:328
  183.6 3.1 %collective-permute-start.24 = (bf16[384,512]{1,0:T(8,128)(2,1)}, bf16[384,512]{1,0:T(8,128)(2,1)}, u32[]{:S(2)}, u32[]{:S(2)}) collective-permute-start(bf16[384,512]{1,0:T(8,128)(2,1)} %get-tuple-element.82), channel_id=1, source_target_pairs={{0,24},{1,97},{8,0},{9,105},{16,8},{17,113},{24,16},{25,121},{32,5... | collective-permute-start | bytes 1179656 | tf_op jit(solution)/shard_map/ppermute | solution.py:328
  186.9 7.1 %finish.1 = (bf16[128,1024]{1,0:T(8,128)(2,1)}, bf16[128,1024]{1,0:T(8,128)(2,1)}) custom-call(s32[1]{0:T(128)} %bitcast.n_ref, bf16[4,272,512]{2,1,0:T(8,128)(2,1)S(1)} %pad_maximum_fusion.3.x, bf16[128,1024]{1,0:T(8,128)(2,1)S(1)} %copy-done.2, bf16[128,1024]{1,0:T(8,128)(2,1)S(1)} %copy-done.3, bf16[1,1024]{1,0:T(2,128)(2,1)S(1)} %broadcast_in_dim.179.gain, ...), custom_call_target="tpu_custom_call" | custom-call | flops 1073741824 | bytes 12582912 | tf_op jit(solution)/shard_map/finish/pallas_call | solution.py:263
  194.0 1.4 convert_add_fusion.3
  195.5 1.0 copy.41
  (131 shorter events, 8.3 us)
Async XLA Ops:
  7.2 23.0 %copy-start = (bf16[1024,896]{1,0:T(8,128)(2,1)S(1)}, bf16[1024,896]{1,0:T(8,128)(2,1)}, u32[]{:S(2)}) copy-start(bf16[1024,896]{1,0:T(8,128)(2,1)} %param.18) | copy-start | bytes 5505028
  7.2 22.3 %copy-start.2 = (bf16[128,1024]{1,0:T(8,128)(2,1)S(1)}, bf16[128,1024]{1,0:T(8,128)(2,1)}, u32[]{:S(2)}) copy-start(bf16[128,1024]{1,0:T(8,128)(2,1)} %hid.1) | copy-start | bytes 786436
  7.2 21.7 %copy-start.19 = (s32[24]{0:T(128)S(1)}, s32[24]{0:T(128)}, u32[]{:S(2)}) copy-start(s32[24]{0:T(128)} %param.15) | copy-start | bytes 292
  7.2 28.2 %copy-start.18 = (bf16[896]{0:T(1024)(128)(2,1)S(1)}, bf16[896]{0:T(1024)(128)(2,1)}, u32[]{:S(2)}) copy-start(bf16[896]{0:T(1024)(128)(2,1)} %param.17) | copy-start | bytes 5380
  7.2 28.2 %copy-start.17 = (bf16[1024]{0:T(1024)(128)(2,1)S(1)}, bf16[1024]{0:T(1024)(128)(2,1)}, u32[]{:S(2)}) copy-start(bf16[1024]{0:T(1024)(128)(2,1)} %param.16) | copy-start | bytes 6148
  7.2 74.2 %all-gather.3.cloned.1.call-start = ((), (), s32[]{:S(2)}) async-start(), calls=%async_computation.2 | async-start | bytes 10543104 | tf_op jit(solution)/shard_map/all_gather | solution.py:369
  9.5 8.7 %collective-permute-start.8 = (bf16[256,512]{1,0:T(8,128)(2,1)S(1)}, bf16[256,512]{1,0:T(8,128)(2,1)S(1)}, u32[]{:S(2)}, u32[]{:S(2)}) collective-permute-start(bf16[256,512]{1,0:T(8,128)(2,1)S(1)} %bitcast_select_fusion), channel_id=1, source_target_pairs={{0,64},{2,32},{4,0},{6,96},{8,72},{10,40},{12,8},{14,104},{16,80},... | collective-permute-start | bytes 786440 | tf_op jit(solution)/shard_map/ppermute | solution.py:368
  19.0 178.2 %reduce-scatter.2.cloned.1.call-start = ((), (), s32[]{:S(2)}) async-start(), calls=%async_computation.1 | async-start | bytes 6881280 | tf_op jit(solution)/shard_map/reduce_scatter | solution.py:435
  19.0 40.7 %collective-permute-start.4 = (bf16[6,128,896]{2,1,0:T(8,128)(2,1)}, bf16[6,128,896]{2,1,0:T(8,128)(2,1)}, u32[]{:S(2)}, u32[]{:S(2)}) collective-permute-start(bf16[6,128,896]{2,1,0:T(8,128)(2,1)} %param.14), channel_id=1, source_target_pairs={{0,6},{2,0},{4,2},{6,4},{1,7},{3,1},{5,3},{7,5},{8,14},{10,8},{12,... | collective-permute-start | bytes 4128776 | tf_op jit(solution)/shard_map/ppermute | solution.py:28
  24.0 37.3 %collective-permute-start.5 = (bf16[6,128,896]{2,1,0:T(8,128)(2,1)}, bf16[6,128,896]{2,1,0:T(8,128)(2,1)}, u32[]{:S(2)}, u32[]{:S(2)}) collective-permute-start(bf16[6,128,896]{2,1,0:T(8,128)(2,1)} %param.14), channel_id=1, source_target_pairs={{0,2},{2,4},{4,6},{6,0},{1,3},{3,5},{5,7},{7,1},{8,10},{10,12},{12... | collective-permute-start | bytes 4128776 | tf_op jit(solution)/shard_map/ppermute | solution.py:28
  25.0 5.1 %collective-permute-start = (bf16[1,1024]{1,0:T(2,128)(2,1)S(1)}, bf16[1,1024]{1,0:T(2,128)(2,1)S(1)}, u32[]{:S(2)}, u32[]{:S(2)}) collective-permute-start(bf16[1,1024]{1,0:T(2,128)(2,1)S(1)} %get-tuple-element.99), channel_id=1, source_target_pairs={{0,8},{8,16},{16,24},{24,32},{32,40},{40,48},{48,56},{56,64},{64,7... | collective-permute-start | bytes 6152 | tf_op jit(solution)/shard_map/ppermute | solution.py:377
  29.0 27.0 %copy-start.10 = (bf16[6,128,896]{2,1,0:T(8,128)(2,1)S(1)}, bf16[6,128,896]{2,1,0:T(8,128)(2,1)}, u32[]{:S(2)}) copy-start(bf16[6,128,896]{2,1,0:T(8,128)(2,1)} %param.14) | copy-start | bytes 4128772
  29.0 27.6 %copy-start.20 = (bf16[896,896]{1,0:T(8,128)(2,1)S(1)}, bf16[896,896]{1,0:T(8,128)(2,1)}, u32[]{:S(2)}) copy-start(bf16[896,896]{1,0:T(8,128)(2,1)} %param.19) | copy-start | bytes 4816900
  30.5 25.3 %collective-permute-start.1 = (f32[3,896]{1,0:T(4,128)S(1)}, f32[3,896]{1,0:T(4,128)S(1)}, u32[]{:S(2)}, u32[]{:S(2)}) collective-permute-start(f32[3,896]{1,0:T(4,128)S(1)} %pad_maximum_fusion.8), channel_id=1, source_target_pairs={{0,2},{2,4},{4,6},{6,0},{1,3},{3,5},{5,7},{7,1},{8,10},{10,12},{12... | collective-permute-start | bytes 32264 | tf_op jit(solution)/shard_map/ppermute | solution.py:28
  30.6 25.2 %collective-permute-start.2 = (f32[3,896]{1,0:T(4,128)S(1)}, f32[3,896]{1,0:T(4,128)S(1)}, u32[]{:S(2)}, u32[]{:S(2)}) collective-permute-start(f32[3,896]{1,0:T(4,128)S(1)} %pad_maximum_fusion.8), channel_id=1, source_target_pairs={{0,4},{2,6},{4,0},{6,2},{1,5},{3,7},{5,1},{7,3},{8,12},{10,14},{12... | collective-permute-start | bytes 32264 | tf_op jit(solution)/shard_map/ppermute | solution.py:28
  35.3 20.5 %collective-permute-start.3 = (f32[3,896]{1,0:T(4,128)S(1)}, f32[3,896]{1,0:T(4,128)S(1)}, u32[]{:S(2)}, u32[]{:S(2)}) collective-permute-start(f32[3,896]{1,0:T(4,128)S(1)} %pad_maximum_fusion.8), channel_id=1, source_target_pairs={{0,6},{2,0},{4,2},{6,4},{1,7},{3,1},{5,3},{7,5},{8,14},{10,8},{12,... | collective-permute-start | bytes 32264 | tf_op jit(solution)/shard_map/ppermute | solution.py:28
  60.9 14.1 %collective-permute-start.6 = (bf16[3,128,896]{2,1,0:T(8,128)(2,1)S(1)}, bf16[3,128,896]{2,1,0:T(8,128)(2,1)S(1)}, u32[]{:S(2)}, u32[]{:S(2)}) collective-permute-start(bf16[3,128,896]{2,1,0:T(8,128)(2,1)S(1)} %slice.179), channel_id=1, source_target_pairs={{0,6},{2,0},{4,2},{6,4},{1,7},{3,1},{5,3},{7,5},{8,14},{10,8},{12,... | collective-permute-start | bytes 2064392 | tf_op jit(solution)/shard_map/ppermute | solution.py:28
  62.4 15.5 %collective-permute-start.7 = (bf16[3,128,896]{2,1,0:T(8,128)(2,1)S(1)}, bf16[3,128,896]{2,1,0:T(8,128)(2,1)S(1)}, u32[]{:S(2)}, u32[]{:S(2)}) collective-permute-start(bf16[3,128,896]{2,1,0:T(8,128)(2,1)S(1)} %slice.180), channel_id=1, source_target_pairs={{0,2},{2,4},{4,6},{6,0},{1,3},{3,5},{5,7},{7,1},{8,10},{10,12},{12... | collective-permute-start | bytes 2064392 | tf_op jit(solution)/shard_map/ppermute | solution.py:28
  81.4 1.6 copy-start.3
  83.1 8.9 %copy-start.4 = (bf16[12,128,896]{2,1,0:T(8,128)(2,1)S(1)}, bf16[12,128,896]{2,1,0:T(8,128)(2,1)}, u32[]{:S(2)}) copy-start(bf16[12,128,896]{2,1,0:T(8,128)(2,1)} %add_convert_fusion.near) | copy-start | bytes 8257540
  83.1 8.9 %copy-start.5 = (bf16[6,128,896]{2,1,0:T(8,128)(2,1)S(1)}, bf16[6,128,896]{2,1,0:T(8,128)(2,1)}, u32[]{:S(2)}) copy-start(bf16[6,128,896]{2,1,0:T(8,128)(2,1)} %add_convert_fusion.2.e0) | copy-start | bytes 4128772
  83.1 8.9 %copy-start.6 = (bf16[6,128,896]{2,1,0:T(8,128)(2,1)S(1)}, bf16[6,128,896]{2,1,0:T(8,128)(2,1)}, u32[]{:S(2)}) copy-start(bf16[6,128,896]{2,1,0:T(8,128)(2,1)} %add_convert_fusion.1.far) | copy-start | bytes 4128772
  88.7 11.4 %collective-permute-start.10 = (bf16[256,512]{1,0:T(8,128)(2,1)S(1)}, bf16[256,512]{1,0:T(8,128)(2,1)S(1)}, u32[]{:S(2)}, u32[]{:S(2)}) collective-permute-start(bf16[256,512]{1,0:T(8,128)(2,1)S(1)} %get-tuple-element.88), channel_id=1, source_target_pairs={{0,2},{2,4},{4,6},{6,0},{1,3},{3,5},{5,7},{7,1},{8,10},{10,12},{12... | collective-permute-start | bytes 786440 | tf_op jit(solution)/shard_map/ppermute | solution.py:28
  88.9 12.4 %collective-permute-start.11 = (bf16[256,512]{1,0:T(8,128)(2,1)S(1)}, bf16[256,512]{1,0:T(8,128)(2,1)S(1)}, u32[]{:S(2)}, u32[]{:S(2)}) collective-permute-start(bf16[256,512]{1,0:T(8,128)(2,1)S(1)} %get-tuple-element.87), channel_id=1, source_target_pairs={{0,6},{2,0},{4,2},{6,4},{1,7},{3,1},{5,3},{7,5},{8,14},{10,8},{12,... | collective-permute-start | bytes 786440 | tf_op jit(solution)/shard_map/ppermute | solution.py:28
  92.0 10.5 %collective-permute-start.9 = (bf16[256,512]{1,0:T(8,128)(2,1)S(1)}, bf16[256,512]{1,0:T(8,128)(2,1)S(1)}, u32[]{:S(2)}, u32[]{:S(2)}) collective-permute-start(bf16[256,512]{1,0:T(8,128)(2,1)S(1)} %get-tuple-element.86), channel_id=1, source_target_pairs={{0,4},{2,6},{4,0},{6,2},{1,5},{3,7},{5,1},{7,3},{8,12},{10,14},{12... | collective-permute-start | bytes 786440 | tf_op jit(solution)/shard_map/ppermute | solution.py:28
  102.7 17.8 %copy-start.7 = (bf16[256,512]{1,0:T(8,128)(2,1)}, bf16[256,512]{1,0:T(8,128)(2,1)S(1)}, u32[]{:S(2)}) copy-start(bf16[256,512]{1,0:T(8,128)(2,1)S(1)} %fusion.21) | copy-start | bytes 786436
  102.7 17.8 %collective-permute-start.16 = (bf16[128,1024]{1,0:T(8,128)(2,1)S(1)}, bf16[128,1024]{1,0:T(8,128)(2,1)S(1)}, u32[]{:S(2)}, u32[]{:S(2)}) collective-permute-start(bf16[128,1024]{1,0:T(8,128)(2,1)S(1)} %copy-done.3), channel_id=1, source_target_pairs={{0,6},{2,0},{4,2},{6,4},{1,7},{3,1},{5,3},{7,5},{8,14},{10,8},{12,... | collective-permute-start | bytes 786440 | tf_op jit(solution)/shard_map/ppermute | solution.py:28
  105.2 15.3 %collective-permute-start.17 = (bf16[128,1024]{1,0:T(8,128)(2,1)S(1)}, bf16[128,1024]{1,0:T(8,128)(2,1)S(1)}, u32[]{:S(2)}, u32[]{:S(2)}) collective-permute-start(bf16[128,1024]{1,0:T(8,128)(2,1)S(1)} %copy-done.3), channel_id=1, source_target_pairs={{0,4},{2,6},{4,0},{6,2},{1,5},{3,7},{5,1},{7,3},{8,12},{10,14},{12... | collective-permute-start | bytes 786440 | tf_op jit(solution)/shard_map/ppermute | solution.py:28
  106.0 14.5 %collective-permute-start.18 = (bf16[128,1024]{1,0:T(8,128)(2,1)S(1)}, bf16[128,1024]{1,0:T(8,128)(2,1)S(1)}, u32[]{:S(2)}, u32[]{:S(2)}) collective-permute-start(bf16[128,1024]{1,0:T(8,128)(2,1)S(1)} %copy-done.3), channel_id=1, source_target_pairs={{0,2},{2,4},{4,6},{6,0},{1,3},{3,5},{5,7},{7,1},{8,10},{10,12},{12... | collective-permute-start | bytes 786440 | tf_op jit(solution)/shard_map/ppermute | solution.py:28
  122.2 5.0 %copy-start.21 = (bf16[16,128,896]{2,1,0:T(8,128)(2,1)S(1)}, bf16[16,128,896]{2,1,0:T(8,128)(2,1)}, u32[]{:S(2)}) copy-start(bf16[16,128,896]{2,1,0:T(8,128)(2,1)} %get-tuple-element.39) | copy-start | bytes 11010052
  122.2 5.0 %copy-start.22 = (bf16[2048,512]{1,0:T(8,128)(2,1)S(1)}, bf16[2048,512]{1,0:T(8,128)(2,1)}, u32[]{:S(2)}) copy-start(bf16[2048,512]{1,0:T(8,128)(2,1)} %get-tuple-element.40) | copy-start | bytes 6291460
  127.1 2.1 %copy-start.14 = (bf16[128,1024]{1,0:T(8,128)(2,1)S(1)}, bf16[128,1024]{1,0:T(8,128)(2,1)}, u32[]{:S(2)}) copy-start(bf16[128,1024]{1,0:T(8,128)(2,1)} %copy-done.13) | copy-start | bytes 786436
  127.2 2.1 %copy-start.16 = (bf16[128,1024]{1,0:T(8,128)(2,1)S(1)}, bf16[128,1024]{1,0:T(8,128)(2,1)}, u32[]{:S(2)}) copy-start(bf16[128,1024]{1,0:T(8,128)(2,1)} %copy-done.15) | copy-start | bytes 786436
  129.3 13.9 %copy-start.8 = (bf16[256,512]{1,0:T(8,128)(2,1)S(1)}, bf16[256,512]{1,0:T(8,128)(2,1)}, u32[]{:S(2)}) copy-start(bf16[256,512]{1,0:T(8,128)(2,1)} %copy-done.7) | copy-start | bytes 786436
  136.3 37.4 %collective-permute-start.19 = (bf16[4,384,512]{2,1,0:T(8,128)(2,1)}, bf16[4,384,512]{2,1,0:T(8,128)(2,1)}, u32[]{:S(2)}, u32[]{:S(2)}) collective-permute-start(bf16[4,384,512]{2,1,0:T(8,128)(2,1)} %get-tuple-element.43), channel_id=1, source_target_pairs={{0,64},{1,17},{8,72},{9,25},{16,80},{17,1},{24,88},{25,9},{32,96},... | collective-permute-start | bytes 4718600 | tf_op jit(solution)/shard_map/ppermute | solution.py:328
  139.9 35.6 %collective-permute-start.20 = (bf16[4,384,512]{2,1,0:T(8,128)(2,1)}, bf16[4,384,512]{2,1,0:T(8,128)(2,1)}, u32[]{:S(2)}, u32[]{:S(2)}) collective-permute-start(bf16[4,384,512]{2,1,0:T(8,128)(2,1)} %get-tuple-element.44), channel_id=1, source_target_pairs={{0,32},{1,9},{8,40},{9,17},{16,48},{17,25},{24,56},{25,1},{32,64},... | collective-permute-start | bytes 4718600 | tf_op jit(solution)/shard_map/ppermute | solution.py:328
  140.4 35.6 %collective-permute-start.21 = (bf16[4,384,512]{2,1,0:T(8,128)(2,1)}, bf16[4,384,512]{2,1,0:T(8,128)(2,1)}, u32[]{:S(2)}, u32[]{:S(2)}) collective-permute-start(bf16[4,384,512]{2,1,0:T(8,128)(2,1)} %get-tuple-element.45), channel_id=1, source_target_pairs={{0,96},{1,25},{8,104},{9,1},{16,112},{17,9},{24,120},{25,17},{32,0... | collective-permute-start | bytes 4718600 | tf_op jit(solution)/shard_map/ppermute | solution.py:328
  144.0 15.0 %collective-permute-start.12 = (bf16[272,512]{1,0:T(8,128)(2,1)S(1)}, bf16[272,512]{1,0:T(8,128)(2,1)S(1)}, u32[]{:S(2)}, u32[]{:S(2)}) collective-permute-start(bf16[272,512]{1,0:T(8,128)(2,1)S(1)} %get-tuple-element.92), channel_id=1, source_target_pairs={{0,6},{2,0},{4,2},{6,4},{1,7},{3,1},{5,3},{7,5},{8,14},{10,8},{12,... | collective-permute-start | bytes 835592 | tf_op jit(solution)/shard_map/ppermute | solution.py:28
  147.3 15.6 %collective-permute-start.14 = (bf16[272,512]{1,0:T(8,128)(2,1)S(1)}, bf16[272,512]{1,0:T(8,128)(2,1)S(1)}, u32[]{:S(2)}, u32[]{:S(2)}) collective-permute-start(bf16[272,512]{1,0:T(8,128)(2,1)S(1)} %get-tuple-element.92), channel_id=1, source_target_pairs={{0,2},{2,4},{4,6},{6,0},{1,3},{3,5},{5,7},{7,1},{8,10},{10,12},{12... | collective-permute-start | bytes 835592 | tf_op jit(solution)/shard_map/ppermute | solution.py:28
  159.0 13.3 %copy-start.11 = (bf16[272,512]{1,0:T(8,128)(2,1)}, bf16[272,512]{1,0:T(8,128)(2,1)S(1)}, u32[]{:S(2)}) copy-start(bf16[272,512]{1,0:T(8,128)(2,1)S(1)} %collective-permute-done.12) | copy-start | bytes 835588
  159.0 9.5 %collective-permute-start.13 = (bf16[136,512]{1,0:T(8,128)(2,1)S(1)}, bf16[136,512]{1,0:T(8,128)(2,1)S(1)}, u32[]{:S(2)}, u32[]{:S(2)}) collective-permute-start(bf16[136,512]{1,0:T(8,128)(2,1)S(1)} %slice.190), channel_id=1, source_target_pairs={{0,6},{2,0},{4,2},{6,4},{1,7},{3,1},{5,3},{7,5},{8,14},{10,8},{12,... | collective-permute-start | bytes 417800 | tf_op jit(solution)/shard_map/ppermute | solution.py:28
  162.8 9.5 %copy-start.12 = (bf16[272,512]{1,0:T(8,128)(2,1)}, bf16[272,512]{1,0:T(8,128)(2,1)S(1)}, u32[]{:S(2)}) copy-start(bf16[272,512]{1,0:T(8,128)(2,1)S(1)} %collective-permute-done.14) | copy-start | bytes 835588
  162.8 9.5 %collective-permute-start.15 = (bf16[136,512]{1,0:T(8,128)(2,1)S(1)}, bf16[136,512]{1,0:T(8,128)(2,1)S(1)}, u32[]{:S(2)}, u32[]{:S(2)}) collective-permute-start(bf16[136,512]{1,0:T(8,128)(2,1)S(1)} %slice.191), channel_id=1, source_target_pairs={{0,2},{2,4},{4,6},{6,0},{1,3},{3,5},{5,7},{7,1},{8,10},{10,12},{12... | collective-permute-start | bytes 417800 | tf_op jit(solution)/shard_map/ppermute | solution.py:28
  180.2 13.8 %collective-permute-start.22 = (bf16[384,512]{1,0:T(8,128)(2,1)}, bf16[384,512]{1,0:T(8,128)(2,1)}, u32[]{:S(2)}, u32[]{:S(2)}) collective-permute-start(bf16[384,512]{1,0:T(8,128)(2,1)} %get-tuple-element.83), channel_id=1, source_target_pairs={{0,16},{1,65},{8,24},{9,73},{16,0},{17,81},{24,8},{25,89},{32,48},... | collective-permute-start | bytes 1179656 | tf_op jit(solution)/shard_map/ppermute | solution.py:328
  183.4 10.6 %collective-permute-start.23 = (bf16[384,512]{1,0:T(8,128)(2,1)}, bf16[384,512]{1,0:T(8,128)(2,1)}, u32[]{:S(2)}, u32[]{:S(2)}) collective-permute-start(bf16[384,512]{1,0:T(8,128)(2,1)} %get-tuple-element.84), channel_id=1, source_target_pairs={{0,8},{1,33},{8,16},{9,41},{16,24},{17,49},{24,0},{25,57},{32,40},... | collective-permute-start | bytes 1179656 | tf_op jit(solution)/shard_map/ppermute | solution.py:328
  183.6 10.5 %collective-permute-start.24 = (bf16[384,512]{1,0:T(8,128)(2,1)}, bf16[384,512]{1,0:T(8,128)(2,1)}, u32[]{:S(2)}, u32[]{:S(2)}) collective-permute-start(bf16[384,512]{1,0:T(8,128)(2,1)} %get-tuple-element.82), channel_id=1, source_target_pairs={{0,24},{1,97},{8,0},{9,105},{16,8},{17,113},{24,16},{25,121},{32,5... | collective-permute-start | bytes 1179656 | tf_op jit(solution)/shard_map/ppermute | solution.py:328
  186.8 7.2 %copy-start.9 = (bf16[384,512]{1,0:T(8,128)(2,1)S(1)}, bf16[384,512]{1,0:T(8,128)(2,1)}, u32[]{:S(2)}) copy-start(bf16[384,512]{1,0:T(8,128)(2,1)} %get-tuple-element.50) | copy-start | bytes 1179652
  186.8 10.4 %copy-start.1 = (bf16[1024,896]{1,0:T(8,128)(2,1)S(1)}, bf16[1024,896]{1,0:T(8,128)(2,1)}, u32[]{:S(2)}) copy-start(bf16[1024,896]{1,0:T(8,128)(2,1)} %param.18) | copy-start | bytes 5505028
  (2 other events, 1.4 us)
Sparse Core Ops, SparseCore 0:
  19.1 59.8 all-gather.2
  122.1 66.5 reduce-scatter.1
